TPU v7x, 32 devices: a whole 2x2x4 slice. The times are simulated.
32 devices in a mesh: fsdp: 4 (over y, x), seq: 8 (over z, core).
Axes of the slice: x: 2, y: 2, z: 4, core: 2. Of those that a mesh axis runs over, the one named last changes fastest.
Arguments:
- block_input: float32 [4, 1024, 1024], P('fsdp', 'seq'), may hold values from -6 to 6
- norm_gain: float32 [1024], replicated, may hold values from 0.5 to 1.5
- w_in: bfloat16 [1024, 4384], P('fsdp', 'seq'), may hold values from -0.1875 to 0.1875
- conv_w: float32 [4, 2304], replicated, may hold values from -0.5 to 0.5
- conv_b: float32 [2304], replicated, may hold values from -0.5 to 0.5
- dt_bias: float32 [32], replicated, may hold values from -6.5 to -2.5
- a_log: float32 [32], replicated, may hold values from 0 to 2.77
- skip_gain: float32 [32], replicated, may hold values from 0.5 to 1.5
- gate_gain: float32 [2048], replicated, may hold values from 0.5 to 1.5
- w_out: bfloat16 [2048, 1024], P('fsdp', 'seq'), may hold values from -0.125 to 0.125
- out_cotangent: float32 [4, 1024, 1024], P('fsdp', 'seq'), may hold values from -6 to 6
Outputs:
- block_output: float32 [4, 1024, 1024], P('fsdp', 'seq')
- grad_input: float32 [4, 1024, 1024], P('fsdp', 'seq')
- grad_norm_gain: float32 [1024], replicated
- grad_w_in: float32 [1024, 4384], P('fsdp', 'seq')
- grad_conv_w: float32 [4, 2304], replicated
- grad_conv_b: float32 [2304], replicated
- grad_dt_bias: float32 [32], replicated
- grad_a_log: float32 [32], replicated
- grad_skip_gain: float32 [32], replicated
- grad_gate_gain: float32 [2048], replicated
- grad_w_out: float32 [2048, 1024], P('fsdp', 'seq')
All inputs are finite; a program needn't handle non-finite values.
Results may differ from a plain program's by a relative error of at most 0.011.
Values may be sent and summed in bfloat16 or wider, within the bound.
No kernel may reach another device: no remote copies, remote signals or barrier semaphores. Data moves between devices by JAX's collectives and lax.ppermute only.
A program may use at most 128 MiB of HBM per device.

v0:
```python
import functools

import jax
import jax.numpy as jnp
import numpy as np
from jax import lax
from jax.experimental import pallas as pl
from jax.experimental.pallas import tpu as pltpu
from jax.sharding import PartitionSpec as P


HEAD_DIM = 64
STATE = 128
CONV_W = 4
GROUP = 128
LANES = 128
EPS = 1e-05
HALO = 8
BF = jnp.bfloat16
F32 = jnp.float32
HIGH = lax.Precision.HIGHEST


def ceil_to(n, k):
    return (n + k - 1) // k * k


def dot(a, b, ca, cb, precision=None):
    return lax.dot_general(
        a, b, (((ca,), (cb,)), ((), ())), precision=precision, preferred_element_type=F32
    )


class Routes:
    def __init__(self, seq, columns, inner, state, heads):
        self.pair = 2 if seq % 2 == 0 else 1
        self.own = columns // seq
        self.width = inner // seq
        self.shared = 2 * state + heads
        width, own, pair = self.width, self.own, self.pair
        pieces = []
        for dst in range(seq):
            wants = [(dst * width, width, 0), (inner + dst * width, width, width)]
            if dst % pair == pair - 1:
                wants.append((2 * inner, self.shared, 2 * width))
            for start, length, at in wants:
                col = start
                while col < start + length:
                    src = col // own
                    stop = min(start + length, (src + 1) * own)
                    pieces.append((src, dst, col - src * own, stop - col, at + col - start))
                    col = stop
        self.local = [p for p in pieces if p[0] == p[1]]
        remote = [p for p in pieces if p[0] != p[1]]
        common = [p for p in remote if p[4] >= 2 * width]
        self.rounds = self.color(common) + self.color([p for p in remote if p[4] < 2 * width])
        self.sizes = [ceil_to(max(p[3] for p in group), 16) for group in self.rounds]
        self.starts = [sum(self.sizes[:r]) for r in range(len(self.sizes))]
        total = sum(self.sizes)
        self.rows = 2 * width + self.shared
        self.send = np.full((seq, total), -1, np.int32)
        self.take = np.full((seq, self.rows), -1, np.int32)
        self.back = np.full((seq, total), -1, np.int32)
        self.home = np.full((seq, self.rows + total), -1, np.int32)
        for src, dst, at, length, to in self.local:
            for i in range(length):
                self.take[dst, to + i] = at + i
                self.home[dst, to + i] = at + i
        for r, group in enumerate(self.rounds):
            for src, dst, at, length, to in group:
                first = self.starts[r]
                for i in range(length):
                    self.send[src, first + i] = at + i
                    self.take[dst, to + i] = own + first + i
                    self.back[dst, first + i] = to + i
                    self.home[src, self.rows + first + i] = at + i

    @staticmethod
    def color(pieces):
        rounds = []
        left = sorted(pieces, key=lambda p: -p[3])
        degree = {}
        for p in left:
            degree[("s", p[0])] = degree.get(("s", p[0]), 0) + 1
            degree[("d", p[1])] = degree.get(("d", p[1]), 0) + 1
        limit = max(degree.values()) if degree else 0
        used = {}
        colors = {}

        def free(node):
            taken = used.setdefault(node, {})
            return next(c for c in range(limit) if c not in taken)

        for index, p in enumerate(left):
            u, v = ("s", p[0]), ("d", p[1])
            a, b = free(u), free(v)
            if a != b and a in used[v]:
                path, node, want = [], v, a
                while want in used[node]:
                    edge = used[node][want]
                    path.append(edge)
                    q = left[edge]
                    ends = (("s", q[0]), ("d", q[1]))
                    node = ends[1] if node == ends[0] else ends[0]
                    want = b if want == a else a
                for edge in path:
                    q = left[edge]
                    for end in (("s", q[0]), ("d", q[1])):
                        used[end].pop(colors[edge], None)
                for edge in path:
                    q = left[edge]
                    colors[edge] = b if colors[edge] == a else a
                    for end in (("s", q[0]), ("d", q[1])):
                        used[end][colors[edge]] = edge
            colors[index] = a
            used[u][a] = index
            used[v][a] = index
        for c in range(limit):
            rounds.append([left[i] for i in range(len(left)) if colors[i] == c])
        return rounds


def one_hot(index, size):
    return (index[:, None] == lax.broadcasted_iota(jnp.int32, (index.shape[0], size), 1)).astype(BF)


class Links:
    def __init__(self, fsdp, seq):
        self.F, self.S = fsdp, seq
        self.pair = 2 if seq % 2 == 0 else 1
        self.chips = seq // self.pair
        self.f = lax.axis_index("fsdp")
        self.s = lax.axis_index("seq")
        self.chip = self.s // self.pair
        self.core = self.s % self.pair

    def swap(self, x):
        return lax.ppermute(x, "seq", [(i, i ^ 1) for i in range(self.S)])

    def hop(self, x, k):
        step = self.pair * k
        return lax.ppermute(x, "seq", [(i, (i + step) % self.S) for i in range(self.S)])

    def chip_at(self, k):
        return lax.rem(self.chip + k + self.chips, self.chips)

    def across(self, x, k):
        if self.F & (self.F - 1) == 0:
            pairs = [(i, i ^ k) for i in range(self.F)]
        else:
            pairs = [(i, (i + k) % self.F) for i in range(self.F)]
        return lax.ppermute(x, "fsdp", pairs)

    def gather_seq(self, x):
        mine, other = [x], []
        for k in range(1, self.chips):
            mine.append(self.hop(x, k))
        if self.pair == 2:
            for k in range(self.chips):
                other.append(self.swap(mine[k]))
        return mine + other

    def scatter_seq(self, keep, give, tokens):
        chips, rows, depth = keep.shape
        rows += rows - tokens
        if self.pair == 2:
            got = self.swap(give)
            own, *held = call(
                functools.partial(hold_kernel, tokens),
                [((rows, depth), F32)] + [((rows, depth), BF)] * (chips - 1),
                [],
                keep,
                got,
            )
        else:
            own, held = keep[0].astype(F32), [keep[k] for k in range(1, chips)]
        arrived = [own]
        for k in range(1, chips):
            arrived.append(self.hop(held[k - 1], k))
        return sum((a[:tokens].astype(F32) for a in arrived[1:]), own[:tokens]), arrived

    def exchange_seq(self, keep, give):
        if self.pair == 2:
            got = self.swap(give)
            first = self.core == 0
            parts = jnp.stack([jnp.where(first, keep, got), jnp.where(first, got, keep)], 1)
        else:
            parts = keep[:, None]
        out = [parts[0]]
        for k in range(1, self.chips):
            out.append(self.hop(parts[k], k))
        return out

    def gather_fsdp(self, x):
        out = [x]
        for k in range(1, self.F):
            out.append(self.across(x, k))
        return out

    def scatter_fsdp(self, parts):
        total = parts[0].astype(F32)
        for k in range(1, self.F):
            total = total + self.across(parts[k], k).astype(F32)
        return total

    def sum_axis(self, x, axis):
        size = self.S if axis == "seq" else self.F
        if size & (size - 1):
            return lax.psum(x, axis)
        k = 1
        while k < size:
            x = x + lax.ppermute(x, axis, [(i, i ^ k) for i in range(size)])
            k *= 2
        return x


def spread(values, heads):
    rows = values.shape[0]
    return jnp.concatenate(
        [jnp.broadcast_to(values[:, h : h + 1], (rows, HEAD_DIM)) for h in range(heads)], axis=1
    )


def widen(x):
    return jnp.concatenate([x, jnp.zeros((x.shape[0], LANES - x.shape[1]), x.dtype)], axis=1)


def softplus(x):
    return jnp.maximum(x, 0.0) + jnp.log1p(jnp.exp(-jnp.abs(x)))


def tri(lower):
    row = lax.broadcasted_iota(jnp.int32, (GROUP, GROUP), 0)
    col = lax.broadcasted_iota(jnp.int32, (GROUP, GROUP), 1)
    return (row >= col) if lower else (row <= col)


def conv_taps(v, halo):
    ext = jnp.concatenate([halo, v], axis=0)
    return [
        (pltpu.roll(ext, CONV_W - 1 - k, 0) if k < CONV_W - 1 else ext)[HALO:]
        for k in range(CONV_W)
    ]


def conv_pre(taps, cw, cb):
    pre = cb + cw[0:1] * taps[0]
    for k in range(1, CONV_W):
        pre = pre + cw[k : k + 1] * taps[k]
    return pre


def halo_of(proj_ref, i, lo, hi):
    start = pl.multiple_of(jnp.maximum(i * GROUP - 16, 0), 16)
    rows = proj_ref[pl.ds(start, 16), lo:hi].astype(F32)[16 - HALO :]
    return jnp.where(i > 0, rows, 0.0)


def peer_to(f, k, count):
    return lax.bitwise_xor(f, k) if count & (count - 1) == 0 else lax.rem(f + k, count)


def peer_from(f, k, count):
    if count & (count - 1) == 0:
        return lax.bitwise_xor(f, k)
    return lax.rem(f - k + count, count)


def spot(pair):
    me = lax.axis_index("seq")
    return me // pair, lax.rem(me, pair)


def assemble(pieces, whole_ref, chips, pair):
    tokens = whole_ref.shape[0] // (chips * pair)
    chip, core = spot(pair)
    for n, piece in enumerate(pieces):
        k, other = n % chips, n // chips
        at = lax.rem(chip - k + chips, chips) * pair + (1 - core if other else core)
        whole_ref[pl.ds(pl.multiple_of(at * tokens, tokens), tokens), :] = piece[...]


def columns_of(index, size):
    return pl.ds(pl.multiple_of(index * size, size), size)


def forward_kernel(heads, chips, pair, shards, *refs):
    pieces, refs = refs[: chips * pair], refs[chips * pair :]
    w_refs, refs = refs[:shards], refs[shards:]
    cw_ref, cb_ref, hp_ref, normed_ref, proj_ref, y_ref, core_ref, open_ref, state = refs
    width = heads * HEAD_DIM
    chans = width + 2 * STATE
    state[...] = jnp.zeros_like(state)
    depth = w_refs[0].shape[1]
    assemble(pieces, normed_ref, chips, pair)
    at = [peer_from(lax.axis_index("fsdp"), k, shards) for k in range(shards)]

    def step(i, _):
        rows = pl.ds(pl.multiple_of(i * GROUP, GROUP), GROUP)
        acc = dot(normed_ref[rows, columns_of(at[0], depth)], w_refs[0][...], 1, 1)
        for k in range(1, shards):
            acc = acc + dot(normed_ref[rows, columns_of(at[k], depth)], w_refs[k][...], 1, 1)
        proj = acc.astype(BF)
        proj_ref[rows, :] = proj
        v = proj[:, width : width + chans].astype(F32)
        taps = conv_taps(v, halo_of(proj_ref, i, width, width + chans))
        pre = conv_pre(taps, cw_ref[...], cb_ref[...])
        act = pre * jax.nn.sigmoid(pre)
        xs = act[:, :width]
        bs = act[:, width : width + STATE].astype(BF)
        cs = act[:, width + STATE :].astype(BF)
        dt = softplus(widen(proj[:, width + chans :].astype(F32)) + hp_ref[0:1])
        rate = -jnp.exp(hp_ref[1:2]) * dt
        run = dot(tri(True).astype(F32), rate, 1, 0, HIGH)
        run_t = run.T
        last = run[GROUP - 1 : GROUP]
        xdt = (xs * spread(dt, heads)).astype(BF)
        scores = dot(cs, bs, 1, 1)
        causal = tri(True)
        within = []
        for h in range(heads):
            gap = run[:, h : h + 1] - run_t[h : h + 1, :]
            decay = jnp.exp(jnp.where(causal, gap, -1e30))
            mixed = (scores * decay).astype(BF)
            within.append(dot(mixed, xdt[:, h * HEAD_DIM : (h + 1) * HEAD_DIM], 1, 0))
        memory = state[...]
        open_ref[i] = memory
        core = jnp.concatenate(within, axis=1) + spread(jnp.exp(run), heads) * dot(
            cs, memory.astype(BF), 1, 0
        )
        core_ref[rows, :] = core
        y_ref[rows, :] = (core + spread(hp_ref[2:3], heads) * xs).astype(BF)
        toward = (xdt.astype(F32) * spread(jnp.exp(last - run), heads)).astype(BF)
        state[...] = spread(jnp.exp(last), heads) * memory + dot(bs, toward, 0, 0)
        return 0

    lax.fori_loop(0, normed_ref.shape[0] // GROUP, step, 0, unroll=2)


def stats_kernel(chips, pair, *refs):
    pieces, refs = refs[: chips * pair], refs[chips * pair :]
    wo_refs, refs = refs[:chips], refs[chips:]
    y_ref, proj_ref, gain_ref, cot_ref, wo_ref, dg_ref, stats_ref = refs
    width = y_ref.shape[1]
    ones = jnp.ones((8, width), F32)
    assemble(pieces, cot_ref, chips, pair)
    part = wo_refs[0].shape[1]
    for k in range(chips):
        for core in range(pair):
            src = lax.rem(spot(pair)[0] - k + chips, chips) * pair + core
            wo_ref[pl.ds(pl.multiple_of(src * part, part), part), :] = wo_refs[k][core]

    def step(i, _):
        rows = pl.ds(pl.multiple_of(i * GROUP, GROUP), GROUP)
        dg = dot(cot_ref[rows, :], wo_ref[...], 1, 0)
        dg_ref[rows, :] = dg
        z = proj_ref[rows, :width].astype(F32)
        u = y_ref[rows, :].astype(F32) * (z * jax.nn.sigmoid(z))
        stats_ref[0:1, rows] = dot(ones, u * u, 1, 1, HIGH)[0:1]
        stats_ref[1:2, rows] = dot(ones, u * gain_ref[...] * dg, 1, 1, HIGH)[0:1]
        return 0

    lax.fori_loop(0, cot_ref.shape[0] // GROUP, step, 0, unroll=4)


def gate_kernel(
    inner,
    chips,
    pair,
    cot_ref,
    wo_ref,
    y_ref,
    proj_ref,
    gain_ref,
    dg_ref,
    stats_ref,
    *refs,
):
    out_refs, refs = refs[:pair], refs[pair:]
    gwo_refs, (dy_ref, dz_ref, ggain_ref, acc) = refs[:-4], refs[-4:]
    width = y_ref.shape[1]
    tokens = cot_ref.shape[0] // (chips * pair)
    part = wo_ref.shape[0] // (chips * pair)
    acc[...] = jnp.zeros_like(acc)
    ggain_ref[...] = jnp.zeros_like(ggain_ref)
    gain = gain_ref[...]
    chip, core = spot(pair)

    def device(k, other):
        return lax.rem(chip + k, chips) * pair + (1 - core if other else core)

    def step(k, _):
        for other in range(pair):
            rows = columns_of(device(k, other), tokens)
            st = jnp.concatenate([stats_ref[:, rows], jnp.zeros((6, tokens), F32)], axis=0).T
            r = lax.rsqrt(st[:, 0:1] / inner + EPS)
            y = y_ref[rows, :].astype(F32)
            z = proj_ref[rows, :width].astype(F32)
            sig = jax.nn.sigmoid(z)
            sz = z * sig
            u = y * sz
            dg = dg_ref[rows, :]
            ur = u * r
            gated = (ur * gain).astype(BF)
            du = r * (gain * dg) - u * (r * r * r * (st[:, 1:2] / inner))
            ggain_ref[...] += jnp.sum(dg * ur, axis=0, keepdims=True)
            dy_ref[rows, :] = (du * sz).astype(BF)
            dz_ref[rows, :] = (du * y * (sig * (1.0 + z * (1.0 - sig)))).astype(BF)
            out_refs[other][k, :tokens] = dot(gated, wo_ref[...], 1, 1).astype(BF)
            acc[...] += dot(cot_ref[rows, :], gated, 0, 0)
        return 0

    lax.fori_loop(0, chips, step, 0, unroll=2)
    for k in range(chips):
        for other in range(pair):
            piece = acc[columns_of(device(k, other), part), :].astype(BF)
            if gwo_refs:
                gwo_refs[other][k] = piece
                continue
            rows = out_refs[other].shape[1] - tokens
            for j in range(part // rows):
                lanes = slice(j * width, (j + 1) * width)
                out_refs[other][k, tokens:, lanes] = piece[j * rows : (j + 1) * rows]


def backward_kernel(
    heads,
    chips,
    pair,
    shards,
    proj_ref,
    core_ref,
    open_ref,
    dy_ref,
    dz_ref,
    cw_ref,
    cb_ref,
    hp_ref,
    *refs,
):
    w_refs, refs = refs[:shards], refs[shards:]
    dn_refs, refs = refs[:pair], refs[pair:]
    dproj_ref, gcw_ref, gcb_ref, ghp_ref, dstate, ahead = refs
    shard = w_refs[0].shape[1]
    tokens = proj_ref.shape[0] // (chips * pair)
    per = tokens // GROUP
    at = [peer_from(lax.axis_index("fsdp"), k, shards) for k in range(shards)]
    chip, core = spot(pair)
    width = heads * HEAD_DIM
    chans = width + 2 * STATE
    blocks = proj_ref.shape[0] // GROUP
    dstate[...] = jnp.zeros_like(dstate)
    ahead[...] = jnp.zeros_like(ahead)
    gcw_ref[...] = jnp.zeros_like(gcw_ref)
    gcb_ref[...] = jnp.zeros_like(gcb_ref)
    ghp_ref[...] = jnp.zeros_like(ghp_ref)
    fold = (
        lax.broadcasted_iota(jnp.int32, (width, LANES), 0) // HEAD_DIM
        == lax.broadcasted_iota(jnp.int32, (width, LANES), 1)
    ).astype(F32)

    def step(n, _):
        i = blocks - 1 - n
        rows = pl.ds(pl.multiple_of(i * GROUP, GROUP), GROUP)
        v = proj_ref[rows, width : width + chans].astype(F32)
        taps = conv_taps(v, halo_of(proj_ref, i, width, width + chans))
        cw = cw_ref[...]
        pre = conv_pre(taps, cw, cb_ref[...])
        sig = jax.nn.sigmoid(pre)
        act = pre * sig
        xs = act[:, :width]
        bs = act[:, width : width + STATE].astype(BF)
        cs = act[:, width + STATE :].astype(BF)
        shifted = widen(proj_ref[rows, width + chans :].astype(F32)) + hp_ref[0:1]
        dt = softplus(shifted)
        neg = -jnp.exp(hp_ref[1:2])
        rate = neg * dt
        run = dot(tri(True).astype(F32), rate, 1, 0, HIGH)
        run_t = run.T
        last = run[GROUP - 1 : GROUP]
        dt_x = spread(dt, heads)
        xdt = (xs * dt_x).astype(BF)
        scores = dot(cs, bs, 1, 1)
        causal = tri(True)
        dyb = dy_ref[rows, :]
        dy = dyb.astype(F32)
        dscores = jnp.zeros((GROUP, GROUP), F32)
        parts = []
        for h in range(heads):
            cols = slice(h * HEAD_DIM, (h + 1) * HEAD_DIM)
            gap = run[:, h : h + 1] - run_t[h : h + 1, :]
            decay = jnp.exp(jnp.where(causal, gap, -1e30))
            mixed = (scores * decay).astype(BF)
            parts.append(dot(mixed, dyb[:, cols], 0, 0))
            dscores = dscores + dot(dyb[:, cols], xdt[:, cols], 1, 1) * decay
        dscores = dscores.astype(BF)
        memory = open_ref[i]
        mem_b = memory.astype(BF)
        ds = dstate[...]
        ds_b = ds.astype(BF)
        edy = (spread(jnp.exp(run), heads) * dy).astype(BF)
        dec = spread(jnp.exp(last - run), heads)
        xdt_f = xdt.astype(F32)
        inflow = dec * dot(bs, ds_b, 1, 0)
        dxdt = jnp.concatenate(parts, axis=1) + inflow
        dc = dot(dscores, bs, 1, 0) + dot(edy, mem_b, 1, 1)
        db = dot(dscores, cs, 0, 0) + dot((xdt_f * dec).astype(BF), ds_b, 1, 1)
        carried = spread(jnp.exp(last), heads)
        dstate[...] = dot(cs, edy, 0, 0) + carried * ds
        dx = dt_x * dxdt + spread(hp_ref[2:3], heads) * dy
        tops = jnp.concatenate(
            [
                jnp.sum(xdt_f * inflow, axis=0, keepdims=True)
                + carried * jnp.sum(ds * memory, axis=0, keepdims=True),
                jnp.sum(dy * xs, axis=0, keepdims=True),
                jnp.zeros((6, width), F32),
            ],
            axis=0,
        )
        folded = dot(
            jnp.concatenate([xs * dxdt, dy * core_ref[rows, :] - xdt_f * dxdt, tops], axis=0),
            fold,
            1,
            0,
            HIGH,
        )
        dend = folded[2 * GROUP : 2 * GROUP + 1]
        drate = dot(tri(False).astype(F32), folded[GROUP : 2 * GROUP], 1, 0, HIGH) + dend
        ddt = folded[:GROUP] + neg * drate
        ddtr = ddt * jax.nn.sigmoid(shifted)
        ghp_ref[0:1] += jnp.sum(ddtr, axis=0, keepdims=True)
        ghp_ref[1:2] += jnp.sum(drate * rate, axis=0, keepdims=True)
        ghp_ref[2:3] += folded[2 * GROUP + 1 : 2 * GROUP + 2]
        dact = jnp.concatenate([dx, db, dc], axis=1)
        dpre = dact * (sig * (1.0 + pre * (1.0 - sig)))
        gcb_ref[...] += jnp.sum(dpre, axis=0, keepdims=True)
        for k in range(CONV_W):
            gcw_ref[k : k + 1] += jnp.sum(dpre * taps[k], axis=0, keepdims=True)
        ext = jnp.concatenate([dpre, ahead[...]], axis=0)
        ahead[...] = dpre[:HALO]
        dv = cw[CONV_W - 1 :] * dpre
        for k in range(CONV_W - 1):
            moved = pltpu.roll(ext, ext.shape[0] - (CONV_W - 1 - k), 0)[:GROUP]
            dv = dv + cw[k : k + 1] * moved
        few = dproj_ref.shape[1] - width - chans
        dproj = jnp.concatenate(
            [dz_ref[rows, :], dv.astype(BF), ddtr[:, :few].astype(BF)], axis=1
        )
        dproj_ref[rows, :] = dproj
        owner = i // per
        k = lax.rem(owner // pair - chip + chips, chips)
        inside = pl.ds(pl.multiple_of((i % per) * GROUP, GROUP), GROUP)
        dn = [dot(dproj, w[...], 1, 0).astype(BF) for w in w_refs]
        for other in range(pair):

            @pl.when((owner % pair != core) == bool(other))
            def _():
                for j in range(shards):
                    dn_refs[other][k, inside, columns_of(at[j], shard)] = dn[j]

        return 0

    lax.fori_loop(0, blocks, step, 0, unroll=2)


def columns_kernel(heads, shards, dproj_ref, normed_ref, *refs):
    w_refs, refs = refs[:shards], refs[shards:]
    gcw_ref, gcb_ref, ghp_ref, ggain_ref, refs = *refs[:4], refs[4:]
    g_refs, (gnorm_ref, slots_ref, common_ref) = refs[:shards], refs[shards:]
    width = ggain_ref.shape[1]
    lanes = min(width, LANES)
    packed = ghp_ref[0:1]
    for n in range(1, 3):
        packed = packed + pltpu.roll(ghp_ref[n : n + 1], n * heads, 1)
    packed = packed[:, :lanes]
    if lanes < width:
        packed = jnp.concatenate([packed, jnp.zeros((1, width - lanes), F32)], axis=1)
    slots_ref[...] = jnp.zeros_like(slots_ref)
    slots_ref[lax.axis_index("seq")] = jnp.concatenate(
        [
            gcw_ref[:, :width],
            gcb_ref[:, :width],
            ggain_ref[...],
            packed,
            jnp.zeros((1, width), F32),
        ],
        axis=0,
    )
    common_ref[...] = jnp.concatenate(
        [gcw_ref[:, width:], gcb_ref[:, width:], jnp.zeros((3, 2 * STATE), F32)], axis=0
    )
    shard = w_refs[0].shape[1]
    for k in range(shards):
        at = columns_of(peer_to(lax.axis_index("fsdp"), k, shards), shard)
        g = dot(dproj_ref[...], normed_ref[:, at], 0, 0)
        g_refs[k][...] = g.astype(BF)
        source = peer_index(k, shards)
        gnorm_ref[0:1, at] = jnp.sum(g * w_refs[source][...].astype(F32), axis=0, keepdims=True)


def chosen(index, start, size):
    row = lax.broadcasted_iota(jnp.int32, (size, index.shape[1]), 0) + start
    return (row == index).astype(F32).astype(BF)


def table_row(table_ref):
    return table_ref[pl.ds(lax.axis_index("seq"), 1), :]


def pick_kernel(table_ref, w_ref, *out_refs):
    index, start = table_row(table_ref), 0
    for out_ref in out_refs:
        items = index[:, start : start + out_ref.shape[0]]
        out_ref[...] = dot(chosen(items, 0, w_ref.shape[0]), w_ref[...], 0, 0).astype(BF)
        start += out_ref.shape[0]


def place_kernel(table_ref, w_ref, *refs):
    arrived, out_ref = refs[:-1], refs[-1]
    index, start, out = table_row(table_ref), 0, None
    for piece in (w_ref, *arrived):
        part = dot(chosen(index, start, piece.shape[0]), piece[...], 0, 0)
        out = part if out is None else out + part
        start += piece.shape[0]
    out_ref[...] = out.astype(BF)


def back_kernel(table_ref, g_ref, common_ref, pool_ref, *out_refs):
    split = pool_ref.shape[0] - common_ref.shape[0]
    pool_ref[:split] = g_ref[:split]
    pool_ref[split:] = common_ref[...]
    index, start = table_row(table_ref), 0
    for out_ref in out_refs:
        items = index[:, start : start + out_ref.shape[0]]
        out_ref[...] = dot(chosen(items, 0, pool_ref.shape[0]), pool_ref[...], 0, 0).astype(BF)
        start += out_ref.shape[0]


def home_kernel(table_ref, *refs):
    pieces, out_ref = refs[:-1], refs[-1]
    index, start, out = table_row(table_ref), 0, None
    for piece in pieces:
        items = index[:, start : start + piece.shape[0]]
        part = dot(chosen(items, 0, out_ref.shape[0]), piece[...], 1, 0)
        out = part if out is None else out + part
        start += piece.shape[0]
    out_ref[...] = out


def hold_kernel(tokens, keep_ref, got_ref, own_ref, *out_refs):
    rows = keep_ref.shape[1]
    for k in range(keep_ref.shape[0]):
        total = keep_ref[k, :tokens].astype(F32) + got_ref[k, :tokens].astype(F32)
        if k == 0:
            own_ref[:tokens] = total
        else:
            out_refs[k - 1][:tokens] = total.astype(BF)
        if rows > tokens:
            extra = rows - tokens
            for n, ref in enumerate((keep_ref, got_ref)):
                at = slice(tokens + n * extra, tokens + (n + 1) * extra)
                if k == 0:
                    own_ref[at] = ref[k, tokens:].astype(F32)
                else:
                    out_refs[k - 1][at] = ref[k, tokens:]


def peer_index(k, count):
    return k if count & (count - 1) == 0 else (count - k) % count


def call(kernel, outs, scratch, *args):
    whole = pl.BlockSpec(memory_space=pltpu.VMEM)
    return pl.pallas_call(
        kernel,
        out_shape=[jax.ShapeDtypeStruct(shape, kind) for shape, kind in outs],
        in_specs=[whole] * len(args),
        out_specs=[whole] * len(outs),
        scratch_shapes=[pltpu.VMEM(shape, kind) for shape, kind in scratch],
    )(*args)


def per_device(
    fsdp,
    seq,
    block_input,
    norm_gain,
    w_in,
    conv_w,
    conv_b,
    dt_bias,
    a_log,
    skip_gain,
    gate_gain,
    w_out,
    out_cotangent,
):
    links = Links(fsdp, seq)
    residual = block_input[0]
    grad_out = out_cotangent[0]
    tokens, depth = residual.shape
    length = tokens * seq
    heads_all = dt_bias.shape[0]
    inner = gate_gain.shape[0]
    heads = heads_all // seq
    width = inner // seq
    chans = width + 2 * STATE
    routes = Routes(seq, w_in.shape[1] * seq, inner, STATE, heads_all)
    me = links.s
    shared = routes.shared

    mean = jnp.mean(residual * residual, axis=-1, keepdims=True)
    scale = lax.rsqrt(mean + EPS)
    normed_half = (residual * scale * norm_gain).astype(BF)

    w_cols = w_in.T
    rows_here = w_in.shape[0]
    picked = call(
        pick_kernel,
        [((size, rows_here), BF) for size in routes.sizes],
        [],
        jnp.asarray(routes.send),
        w_cols,
    )
    arrived = []
    for r, group in enumerate(routes.rounds):
        arrived.append(lax.ppermute(picked[r], "seq", [(p[0], p[1]) for p in group]))
    (mine,) = call(
        place_kernel,
        [((routes.rows, rows_here), BF)],
        [],
        jnp.asarray(routes.take),
        w_cols,
        *arrived,
    )
    common = mine[2 * width :]
    if links.pair == 2:
        common = common + lax.ppermute(
            common, "seq", [(i, i - 1) for i in range(1, seq, 2)]
        )
    head_row = jnp.arange(ceil_to(heads, 16), dtype=jnp.int32)
    head_row = jnp.where(head_row < heads, 2 * STATE + me * heads + head_row, -1)
    head_pick = one_hot(head_row, shared)
    w_mine = jnp.concatenate(
        [mine[: 2 * width], common[: 2 * STATE], dot(head_pick, common, 1, 0).astype(BF)], axis=0
    )
    normed = links.gather_seq(normed_half)
    w_all = links.gather_fsdp(w_mine)

    wo_half = w_out.reshape(-1, width, w_out.shape[1]).transpose(0, 2, 1)
    wo_rows = jnp.zeros((fsdp,) + wo_half.shape, BF)
    for k, piece in enumerate(links.gather_fsdp(wo_half)):
        wo_rows = lax.dynamic_update_index_in_dim(wo_rows, piece, peer_from(links.f, k, fsdp), 0)
    wo_rows = wo_rows.reshape((links.chips, links.pair) + wo_half.shape[1:])
    order = [links.chip_at(k) for k in range(links.chips)]

    def parity(core):
        picks = [lax.dynamic_slice(wo_rows, (c, core, 0, 0), (1, 1) + wo_half.shape[1:]) for c in order]
        return jnp.concatenate(picks, axis=0)[:, 0]

    wo = links.exchange_seq(parity(links.core), parity(1 - links.core))
    cot_half = grad_out.astype(BF)
    cot_half, _ = lax.optimization_barrier((cot_half, tuple(normed)))
    cot = links.gather_seq(cot_half)

    def local(vector, size, start):
        return lax.dynamic_slice_in_dim(vector, start, size, vector.ndim - 1)

    cw = jnp.concatenate([local(conv_w[:, :inner], width, me * width), conv_w[:, inner:]], axis=1)
    cb = jnp.concatenate([local(conv_b[:inner], width, me * width), conv_b[inner:]])[None]
    per_head = jnp.stack([local(p, heads, me * heads) for p in (dt_bias, a_log, skip_gain)])
    hp = jnp.pad(per_head, ((0, 5), (0, LANES - heads)))
    gain = local(gate_gain, width, me * width)[None]
    narrow = ceil_to(heads, 16)
    cols = 2 * width + 2 * STATE + narrow
    blocks = length // GROUP

    chips, pair = links.chips, links.pair
    normed_all, proj, y, core, opened = call(
        functools.partial(forward_kernel, heads, chips, pair, fsdp),
        [
            ((length, depth), BF),
            ((length, cols), BF),
            ((length, width), BF),
            ((length, width), F32),
            ((blocks, STATE, width), F32),
        ],
        [((STATE, width), F32)],
        *normed,
        *w_all,
        cw,
        cb,
        hp,
    )
    cot_all, wo_all, dgated, stats = call(
        functools.partial(stats_kernel, chips, pair),
        [((length, depth), BF), ((depth, width), BF), ((length, width), F32), ((2, length), F32)],
        [],
        *cot,
        *wo,
        y,
        proj,
        gain,
    )
    stats = links.sum_axis(stats, "seq")
    halves = [((chips, tokens, depth), BF)] * pair
    part = depth // seq
    extra = part * width // depth
    together = pair == 2 and extra % 16 == 0 and width % LANES == 0
    out_halves = [((chips, tokens + extra, depth), BF)] * pair if together else halves
    quarters = [] if together else [((chips, part, width), BF)] * pair
    gate_outs = call(
        functools.partial(gate_kernel, float(inner), chips, pair),
        out_halves
        + quarters
        + [((length, width), BF), ((length, width), BF), ((1, width), F32)],
        [((depth, width), F32)],
        cot_all,
        wo_all,
        y,
        proj,
        gain,
        dgated,
        stats,
    )
    out_halves, gwo_halves = gate_outs[:pair], gate_outs[pair:-3]
    dy, dz, ggain = gate_outs[-3:]
    back_outs = call(
        functools.partial(backward_kernel, heads, chips, pair, fsdp),
        halves
        + [((length, cols), BF), ((CONV_W, chans), F32), ((1, chans), F32), ((8, LANES), F32)],
        [((STATE, width), F32), ((HALO, chans), F32)],
        proj,
        core,
        opened,
        dy,
        dz,
        cw,
        cb,
        hp,
        *w_all,
    )
    dn_halves = back_outs[:pair]
    dproj, gcw, gcb, ghp = back_outs[pair:]
    shard = depth // fsdp
    *g_cols, g_norm, slots, g_shared = call(
        functools.partial(columns_kernel, heads, fsdp),
        [((cols, shard), BF)] * fsdp
        + [((1, depth), F32), ((seq, 8, width), F32), ((8, 2 * STATE), F32)],
        [],
        dproj,
        normed_all,
        *w_all,
        gcw,
        gcb,
        ghp,
        ggain,
    )

    out_sum, arrived = links.scatter_seq(out_halves[0], out_halves[-1], tokens)
    block_out = residual + out_sum
    if together:
        gwo = []
        for piece in arrived:
            both = piece[tokens:].astype(BF).reshape(2, extra, part // extra, width)
            both = both.transpose(0, 2, 1, 3).reshape(2, part, width)
            gwo.append(jnp.where(links.core == 0, both, both[::-1]))
    else:
        gwo = links.exchange_seq(gwo_halves[0], gwo_halves[-1])
    gwo_rows = jnp.zeros((chips,) + gwo[0].shape, BF)
    for k, piece in enumerate(gwo):
        gwo_rows = lax.dynamic_update_index_in_dim(gwo_rows, piece, links.chip_at(-k), 0)
    gwo_rows = gwo_rows.reshape((fsdp, seq // fsdp, depth // seq, width))
    to = [
        lax.dynamic_index_in_dim(gwo_rows, peer_to(links.f, k, fsdp), 0, keepdims=False)
        for k in range(fsdp)
    ]
    owned_w_out = links.scatter_fsdp(to).transpose(0, 2, 1).reshape(w_out.shape)

    g_mine = links.scatter_fsdp(g_cols)
    dnormed, dn_arrived = links.scatter_seq(dn_halves[0], dn_halves[-1], tokens)
    dscaled = dnormed * norm_gain
    du_norm = scale * dscaled - residual * (
        scale * scale * scale * jnp.mean(residual * dscaled, axis=-1, keepdims=True)
    )
    grad_in = grad_out + du_norm

    g_half = g_mine.astype(BF)
    g_heads = dot(head_pick, g_half[2 * width + 2 * STATE :], 0, 0)[2 * STATE :]
    g_common = jnp.concatenate([g_half[2 * width : 2 * width + 2 * STATE], g_heads.astype(BF)])
    if links.pair == 2:
        other = lax.ppermute(g_common, "seq", [(i, i + 1) for i in range(0, seq, 2)])
        g_common = (g_common.astype(F32) + other.astype(F32)).astype(BF)
    g_pool, *sent = call(
        back_kernel,
        [((routes.rows, rows_here), BF)] + [((size, rows_here), BF) for size in routes.sizes],
        [],
        jnp.asarray(routes.back),
        g_half,
        g_common,
    )
    homed = []
    for r, group in enumerate(routes.rounds):
        homed.append(lax.ppermute(sent[r], "seq", [(p[1], p[0]) for p in group]))
    (owned_w_in,) = call(
        home_kernel, [(w_cols.shape, F32)], [], jnp.asarray(routes.home), g_pool, *homed
    )
    owned_w_in = owned_w_in.T

    pieces, _ = lax.optimization_barrier(([slots, g_shared, g_norm], dn_arrived[0]))
    packed = jnp.concatenate([p.reshape(-1, LANES) for p in pieces], axis=0)
    packed = links.sum_axis(packed, "seq")
    packed = links.sum_axis(packed, "fsdp")
    first = slots.size // LANES
    slots = packed[:first].reshape(slots.shape)
    second = first + g_shared.size // LANES
    g_shared = packed[first:second].reshape(g_shared.shape)
    g_norm = packed[second:].reshape(-1) / norm_gain
    g_conv_w = jnp.concatenate(
        [slots[:, :CONV_W].transpose(1, 0, 2).reshape(CONV_W, inner), g_shared[:CONV_W]], axis=1
    )
    g_conv_b = jnp.concatenate([slots[:, CONV_W].reshape(inner), g_shared[CONV_W]])
    g_gain = slots[:, CONV_W + 1].reshape(inner)
    g_head = [slots[:, CONV_W + 2, n * heads : (n + 1) * heads].reshape(-1) for n in range(3)]
    return (
        block_out[None],
        grad_in[None],
        g_norm,
        owned_w_in,
        g_conv_w,
        g_conv_b,
        *g_head,
        g_gain,
        owned_w_out,
    )


def solution(mesh):
    weights = P("fsdp", "seq")
    acts = P("fsdp", "seq", None)
    fsdp, seq = mesh.shape["fsdp"], mesh.shape["seq"]

    def body(*args):
        return per_device(fsdp, seq, *args)

    return jax.shard_map(
        body,
        mesh=mesh,
        in_specs=(acts, P(), weights, P(), P(), P(), P(), P(), P(), weights, acts),
        out_specs=(acts, acts, P(), weights, P(), P(), P(), P(), P(), P(), weights),
        check_vma=False,
    )
```

profile of v0, /device:TPU:0, one launch (start us, length us, event | category | flops | bytes accessed | tf_op | source)
XLA Modules:
  0.0 310.6 jit_solution(10719890377223236527)
XLA Ops:
  1.7 3.0 collective-permute-start.14
  6.3 3.5 %shard_map.230 = (bf16[288,256]{1,0:T(8,128)(2,1)}, bf16[288,256]{1,0:T(8,128)(2,1)}, bf16[288,256]{1,0:T(8,128)(2,1)}, bf16[256,256]{1,0:T(8,128)(2,1)}, bf16[2...) custom-call(s32[8,1856]{1,0:T(8,128)} %constant.119.clone.table_ref, bf16[548,256]{1,0:T(8,128)(2,1)} %bitcast.133), custom_call_target="tpu_custom_call" | custom-call | tf_op jit(solution)/shard_map/pallas_call | solution.py:674
  10.6 3.9 %collective-permute-start.24 = (bf16[256,256]{1,0:T(8,128)(2,1)}, bf16[256,256]{1,0:T(8,128)(2,1)S(1)}, u32[]{:S(2)}, u32[]{:S(2)}) collective-permute-start(bf16[256,256]{1,0:T(8,128)(2,1)} %get-tuple-element.69), channel_id=1, source_target_pairs={{4,1},{5,3},{6,5},{2,4},{3,0},{0,2},{7,6},{12,9},{13,11},{14,13},{... | collective-permute-start | bytes 393224 | tf_op jit(solution)/shard_map/ppermute | solution.py:727
  17.8 6.6 %collective-permute-start.25 = (bf16[256,256]{1,0:T(8,128)(2,1)S(1)}, bf16[256,256]{1,0:T(8,128)(2,1)S(1)}, u32[]{:S(2)}, u32[]{:S(2)}) collective-permute-start(bf16[256,256]{1,0:T(8,128)(2,1)S(1)} %copy-done.51), channel_id=1, source_target_pairs={{0,1},{1,3},{2,5},{4,2},{3,6},{6,4},{8,9},{9,11},{10,13},{12,10},{... | collective-permute-start | bytes 393224 | tf_op jit(solution)/shard_map/ppermute | solution.py:727
  25.7 3.0 collective-permute-start
  30.3 2.8 collective-permute-start.2
  33.1 11.5 %collective-permute-done.26.refs_5_ = bf16[256,256]{1,0:T(8,128)(2,1)S(1)} collective-permute-done((bf16[256,256]{1,0:T(8,128)(2,1)S(1)}, bf16[256,256]{1,0:T(8,128)(2,1)S(1)}, u32[]{:S(2)}, u32[]{:S(2)}) %collective-permute-start.26) | collective-permute-done | bytes 131104 | tf_op jit(solution)/shard_map/ppermute | solution.py:727
  47.3 3.7 %shard_map.231 = bf16[800,256]{1,0:T(8,128)(2,1)} custom-call(s32[8,800]{1,0:T(8,128)} %constant.120.clone.table_ref, bf16[548,256]{1,0:T(8,128)(2,1)} %bitcast.134, bf16[288,256]{1,0:T(8,128)(2,1)} %copy-done.30, bf16[288,256]{1,0:T(8,128)(2,1)} %copy-done.31, bf16[288,256]{1,0:T(8,128)(2,1)} %copy-done.32, bf16[256,256]{1,0:T(8,128)(2,1)} %copy-done.36, ...), custom_call_target="tpu_custom_call" | custom-call | tf_op jit(solution)/shard_map/pallas_call | solution.py:674
  58.2 1.6 collective-permute-start.30
  59.8 4.2 %collective-permute-start.18 = (bf16[2,128,256]{2,1,0:T(8,128)(2,1)}, bf16[2,128,256]{2,1,0:T(8,128)(2,1)}, u32[]{:S(2)}, u32[]{:S(2)}) collective-permute-start(bf16[2,128,256]{2,1,0:T(8,128)(2,1)} %get-tuple-element.129), channel_id=1, source_target_pairs={{0,2},{1,3},{2,4},{3,5},{4,6},{5,7},{6,0},{7,1},{8,10},{9,11},{10,... | collective-permute-start | bytes 393224 | tf_op jit(solution)/shard_map/ppermute | solution.py:142
  65.8 2.4 collective-permute-done.18.refs_9_
  68.2 2.8 collective-permute-start.7
  70.9 13.9 %collective-permute-done.19.refs_10_ = bf16[2,128,256]{2,1,0:T(8,128)(2,1)} collective-permute-done((bf16[2,128,256]{2,1,0:T(8,128)(2,1)}, bf16[2,128,256]{2,1,0:T(8,128)(2,1)}, u32[]{:S(2)}, u32[]{:S(2)}) %collective-permute-start.19) | collective-permute-done | bytes 131104 | tf_op jit(solution)/shard_map/ppermute | solution.py:142
  85.7 9.2 %collective-permute-done.8.refs_2_ = bf16[128,1024]{1,0:T(8,128)(2,1)S(1)} collective-permute-done((bf16[128,1024]{1,0:T(8,128)(2,1)S(1)}, bf16[128,1024]{1,0:T(8,128)(2,1)S(1)}, u32[]{:S(2)}, u32[]{:S(2)}) %collective-permute-start.8) | collective-permute-done | bytes 262176 | tf_op jit(solution)/shard_map/ppermute | solution.py:142
  95.0 3.4 %collective-permute-done.9.refs_3_ = bf16[128,1024]{1,0:T(8,128)(2,1)S(1)} collective-permute-done((bf16[128,1024]{1,0:T(8,128)(2,1)S(1)}, bf16[128,1024]{1,0:T(8,128)(2,1)S(1)}, u32[]{:S(2)}, u32[]{:S(2)}) %collective-permute-start.9) | collective-permute-done | bytes 262176 | tf_op jit(solution)/shard_map/ppermute | solution.py:142
  99.1 2.2 collective-permute-start.20
  103.9 14.7 %shard_map.232 = (bf16[1024,1024]{1,0:T(8,128)(2,1)}, bf16[1024,784]{1,0:T(8,128)(2,1)}, bf16[1024,256]{1,0:T(8,128)(2,1)}, f32[1024,256]{1,0:T(8,128)}, f32[8,128,256]{2,1,0:T(8,128)}) custom-call(bf16[128,1024]{1,0:T(8,128)(2,1)} %copy-done.12, bf16[128,1024]{1,0:T(8,128)(2,1)} %copy-done.21, bf16[128,1024]{1,0:T(8,128)(2,1)} %copy-done.22, ...), custom_call_target="tpu_custom_call" | custom-call | tf_op jit(solution)/shard_map/pallas_call | solution.py:674
  118.6 6.6 %shard_map.233 = (bf16[1024,1024]{1,0:T(8,128)(2,1)}, bf16[1024,256]{1,0:T(8,128)(2,1)}, f32[1024,256]{1,0:T(8,128)}, f32[2,1024]{1,0:T(2,128)}) custom-call(bf16[128,1024]{1,0:T(8,128)(2,1)} %copy-done.17, bf16[128,1024]{1,0:T(8,128)(2,1)} %copy-done.27, bf16[128,1024]{1,0:T(8,128)(2,1)} %copy-done.28, bf16[128,1024]{1,0:T(8,128)(2,1)} %copy-done.29, ...), custom_call_target="tpu_custom_call" | custom-call | tf_op jit(solution)/shard_map/pallas_call | solution.py:674
  127.4 3.6 %collective-permute-done.33 = f32[2,1024]{1,0:T(2,128)S(1)} collective-permute-done((f32[2,1024]{1,0:T(2,128)S(1)}, f32[2,1024]{1,0:T(2,128)S(1)}, u32[]{:S(2)}, u32[]{:S(2)}) %collective-permute-start.33) | collective-permute-done | bytes 8224 | tf_op jit(solution)/shard_map/ppermute | solution.py:212
  131.9 3.7 %collective-permute-done.34 = f32[2,1024]{1,0:T(2,128)S(1)} collective-permute-done((f32[2,1024]{1,0:T(2,128)S(1)}, f32[2,1024]{1,0:T(2,128)S(1)}, u32[]{:S(2)}, u32[]{:S(2)}) %collective-permute-start.34) | collective-permute-done | bytes 8224 | tf_op jit(solution)/shard_map/ppermute | solution.py:212
  136.2 7.9 %shard_map.234 = (bf16[4,160,1024]{2,1,0:T(8,128)(2,1)}, bf16[4,160,1024]{2,1,0:T(8,128)(2,1)}, bf16[1024,256]{1,0:T(8,128)(2,1)}, bf16[1024,256]{1,0:T(8,128)(2,1)}, f32[1,256]{1,0:T(1,128)}) custom-call(bf16[1024,1024]{1,0:T(8,128)(2,1)} %get-tuple-element.75.cot_ref, bf16[1024,256]{1,0:T(8,128)(2,1)} %get-tuple-element.76.wo_ref, ...), custom_call_target="tpu_custom_call" | custom-call | tf_op jit(solution)/shard_map/pallas_call | solution.py:674
  144.1 22.4 %shard_map.236 = (bf16[4,128,1024]{2,1,0:T(8,128)(2,1)}, bf16[4,128,1024]{2,1,0:T(8,128)(2,1)}, bf16[1024,784]{1,0:T(8,128)(2,1)}, f32[4,512]{1,0:T(4,128)}, f32[1,512]{1,0:T(1,128)}, /*index=5*/f32[8,128]{1,0:T(8,128)}) custom-call(bf16[1024,784]{1,0:T(8,128)(2,1)} %get-tuple-element.74.refs_13_.proj_ref, f32[1024,256]{1,0:T(8,128)} %get-tuple-element.85.core_ref, ...), custom_call_target="tpu_custom_call" | custom-call | tf_op jit(solution)/shard_map/pallas_call | solution.py:674
  166.4 5.7 %shard_map.238 = (bf16[784,256]{1,0:T(8,128)(2,1)}, bf16[784,256]{1,0:T(8,128)(2,1)}, bf16[784,256]{1,0:T(8,128)(2,1)}, bf16[784,256]{1,0:T(8,128)(2,1)}, f32[1,...) custom-call(bf16[1024,784]{1,0:T(8,128)(2,1)} %get-tuple-element.95.dproj_ref, ...), custom_call_target="tpu_custom_call" | custom-call | tf_op jit(solution)/shard_map/pallas_call | solution.py:674
  173.1 2.5 collective-permute-start.50
  175.6 8.9 %collective-permute-done.48 = bf16[784,256]{1,0:T(8,128)(2,1)S(1)} collective-permute-done((bf16[784,256]{1,0:T(8,128)(2,1)}, bf16[784,256]{1,0:T(8,128)(2,1)S(1)}, u32[]{:S(2)}, u32[]{:S(2)}) %collective-permute-start.48) | collective-permute-done | bytes 401440 | tf_op jit(solution)/shard_map/ppermute | solution.py:152
  184.5 5.8 %collective-permute-done.49 = bf16[784,256]{1,0:T(8,128)(2,1)S(1)} collective-permute-done((bf16[784,256]{1,0:T(8,128)(2,1)}, bf16[784,256]{1,0:T(8,128)(2,1)S(1)}, u32[]{:S(2)}, u32[]{:S(2)}) %collective-permute-start.49) | collective-permute-done | bytes 401440 | tf_op jit(solution)/shard_map/ppermute | solution.py:152
  194.8 4.3 %shard_map.239 = (bf16[800,256]{1,0:T(8,128)(2,1)}, bf16[288,256]{1,0:T(8,128)(2,1)}, bf16[288,256]{1,0:T(8,128)(2,1)}, bf16[288,256]{1,0:T(8,128)(2,1)}, bf16[2...) custom-call(s32[8,1856]{1,0:T(8,128)} %constant.121.clone.table_ref, ...), custom_call_target="tpu_custom_call" | custom-call | tf_op jit(solution)/shard_map/pallas_call | solution.py:674
  199.1 2.1 collective-permute-start.55
  203.6 2.6 shard_map.237
  210.4 3.6 %collective-permute-start.57 = (bf16[256,256]{1,0:T(8,128)(2,1)}, bf16[256,256]{1,0:T(8,128)(2,1)S(1)}, u32[]{:S(2)}, u32[]{:S(2)}) collective-permute-start(bf16[256,256]{1,0:T(8,128)(2,1)} %get-tuple-element.117), channel_id=1, source_target_pairs={{7,3},{0,4},{6,2},{2,5},{4,1},{15,11},{8,12},{14,10},{10,13},{12,9... | collective-permute-start | bytes 393224 | tf_op jit(solution)/shard_map/ppermute | solution.py:904
  214.0 4.6 %collective-permute-start.44 = (f32[152,128]{1,0:T(8,128)S(1)}, f32[152,128]{1,0:T(8,128)S(1)}, u32[]{:S(2)}, u32[]{:S(2)}) collective-permute-start(f32[152,128]{1,0:T(8,128)S(1)} %fusion.31), channel_id=1, source_target_pairs={{0,2},{1,3},{2,0},{3,1},{4,6},{5,7},{6,4},{7,5},{8,10},{9,11},{10,... | collective-permute-start | bytes 233480 | tf_op jit(solution)/shard_map/ppermute | solution.py:212
  219.3 4.9 %collective-permute-start.40 = (bf16[128,1024]{1,0:T(8,128)(2,1)}, bf16[128,1024]{1,0:T(8,128)(2,1)S(1)}, u32[]{:S(2)}, u32[]{:S(2)}) collective-permute-start(bf16[128,1024]{1,0:T(8,128)(2,1)} %get-tuple-element.92), channel_id=1, source_target_pairs={{0,2},{1,3},{2,4},{3,5},{4,6},{5,7},{6,0},{7,1},{8,10},{9,11},{10,... | collective-permute-start | bytes 786440 | tf_op jit(solution)/shard_map/ppermute | solution.py:142
  224.9 2.6 collective-permute-start.42
  229.3 3.4 %shard_map.240 = f32[548,256]{1,0:T(8,128)} custom-call(s32[8,2656]{1,0:T(8,128)} %constant.122.clone.table_ref, bf16[800,256]{1,0:T(8,128)(2,1)} %get-tuple-element.111.refs_0_, bf16[288,256]{1,0:T(8,128)(2,1)} %copy-done.33, bf16[288,256]{1,0:T(8,128)(2,1)} %copy-done.34, bf16[288,256]{1,0:T(8,128)(2,1)} %copy-done.35, ...), custom_call_target="tpu_custom_call" | custom-call | tf_op jit(solution)/shard_map/pallas_call | solution.py:674
  232.7 19.0 %collective-permute-done.45 = f32[152,128]{1,0:T(8,128)} collective-permute-done((f32[152,128]{1,0:T(8,128)S(1)}, f32[152,128]{1,0:T(8,128)}, u32[]{:S(2)}, u32[]{:S(2)}) %collective-permute-start.45) | collective-permute-done | bytes 77856 | tf_op jit(solution)/shard_map/ppermute | solution.py:212
  257.1 3.0 shard_map.235
  261.3 2.5 collective-permute-start.37
  266.7 3.8 %collective-permute-done.47 = f32[152,128]{1,0:T(8,128)S(1)} collective-permute-done((f32[152,128]{1,0:T(8,128)S(1)}, f32[152,128]{1,0:T(8,128)S(1)}, u32[]{:S(2)}, u32[]{:S(2)}) %collective-permute-start.47) | collective-permute-done | bytes 77856 | tf_op jit(solution)/shard_map/ppermute | solution.py:212
  276.8 1.7 reshape.113
  278.5 1.6 copy.44
  280.1 10.8 %collective-permute-done.37 = bf16[192,1024]{1,0:T(8,128)(2,1)} collective-permute-done((bf16[192,1024]{1,0:T(8,128)(2,1)}, bf16[192,1024]{1,0:T(8,128)(2,1)}, u32[]{:S(2)}, u32[]{:S(2)}) %collective-permute-start.37) | collective-permute-done | bytes 393248 | tf_op jit(solution)/shard_map/ppermute | solution.py:142
  290.9 1.6 slice.165
  292.5 1.6 reshape.115
  294.1 1.6 copy.46
  295.7 1.6 slice.166
  297.3 1.6 reshape.117
  303.8 1.8 collective-permute-start.61
  305.6 2.4 fusion
  (285 shorter events, 66.6 us)
Async XLA Ops:
  1.7 15.4 %collective-permute-start.14 = (bf16[2,128,256]{2,1,0:T(8,128)(2,1)S(1)}, bf16[2,128,256]{2,1,0:T(8,128)(2,1)S(1)}, u32[]{:S(2)}, u32[]{:S(2)}) collective-permute-start(bf16[2,128,256]{2,1,0:T(8,128)(2,1)S(1)} %bitcast.136), channel_id=1, source_target_pairs={{0,8},{8,0},{16,24},{24,16},{1,9},{9,1},{17,25},{25,17},{2,10},{10... | collective-permute-start | bytes 393224 | tf_op jit(solution)/shard_map/ppermute | solution.py:152
  4.7 19.6 %collective-permute-start.15 = (bf16[2,128,256]{2,1,0:T(8,128)(2,1)S(1)}, bf16[2,128,256]{2,1,0:T(8,128)(2,1)S(1)}, u32[]{:S(2)}, u32[]{:S(2)}) collective-permute-start(bf16[2,128,256]{2,1,0:T(8,128)(2,1)S(1)} %bitcast.137), channel_id=1, source_target_pairs={{0,16},{8,24},{16,0},{24,8},{1,17},{9,25},{17,1},{25,9},{2,18},{10... | collective-permute-start | bytes 393224 | tf_op jit(solution)/shard_map/ppermute | solution.py:152
  6.2 19.5 %collective-permute-start.16 = (bf16[2,128,256]{2,1,0:T(8,128)(2,1)S(1)}, bf16[2,128,256]{2,1,0:T(8,128)(2,1)S(1)}, u32[]{:S(2)}, u32[]{:S(2)}) collective-permute-start(bf16[2,128,256]{2,1,0:T(8,128)(2,1)S(1)} %bitcast.138), channel_id=1, source_target_pairs={{0,24},{8,16},{16,8},{24,0},{1,25},{9,17},{17,9},{25,1},{2,26},{10... | collective-permute-start | bytes 393224 | tf_op jit(solution)/shard_map/ppermute | solution.py:152
  9.7 35.5 %collective-permute-start.21 = (bf16[288,256]{1,0:T(8,128)(2,1)}, bf16[288,256]{1,0:T(8,128)(2,1)S(1)}, u32[]{:S(2)}, u32[]{:S(2)}) collective-permute-start(bf16[288,256]{1,0:T(8,128)(2,1)} %get-tuple-element.66), channel_id=1, source_target_pairs={{7,1},{15,9},{23,17},{31,25}} | collective-permute-start | bytes 442376 | tf_op jit(solution)/shard_map/ppermute | solution.py:727
  10.6 18.2 %collective-permute-start.24 = (bf16[256,256]{1,0:T(8,128)(2,1)}, bf16[256,256]{1,0:T(8,128)(2,1)S(1)}, u32[]{:S(2)}, u32[]{:S(2)}) collective-permute-start(bf16[256,256]{1,0:T(8,128)(2,1)} %get-tuple-element.69), channel_id=1, source_target_pairs={{4,1},{5,3},{6,5},{2,4},{3,0},{0,2},{7,6},{12,9},{13,11},{14,13},{... | collective-permute-start | bytes 393224 | tf_op jit(solution)/shard_map/ppermute | solution.py:727
  17.8 12.5 %collective-permute-start.25 = (bf16[256,256]{1,0:T(8,128)(2,1)S(1)}, bf16[256,256]{1,0:T(8,128)(2,1)S(1)}, u32[]{:S(2)}, u32[]{:S(2)}) collective-permute-start(bf16[256,256]{1,0:T(8,128)(2,1)S(1)} %copy-done.51), channel_id=1, source_target_pairs={{0,1},{1,3},{2,5},{4,2},{3,6},{6,4},{8,9},{9,11},{10,13},{12,10},{... | collective-permute-start | bytes 393224 | tf_op jit(solution)/shard_map/ppermute | solution.py:727
  24.4 20.2 %collective-permute-start.26 = (bf16[256,256]{1,0:T(8,128)(2,1)S(1)}, bf16[256,256]{1,0:T(8,128)(2,1)S(1)}, u32[]{:S(2)}, u32[]{:S(2)}) collective-permute-start(bf16[256,256]{1,0:T(8,128)(2,1)S(1)} %copy-done.50), channel_id=1, source_target_pairs={{3,7},{4,0},{2,6},{5,2},{1,4},{11,15},{12,8},{10,14},{13,10},{9,12... | collective-permute-start | bytes 393224 | tf_op jit(solution)/shard_map/ppermute | solution.py:727
  25.7 27.7 %collective-permute-start = (bf16[128,1024]{1,0:T(8,128)(2,1)S(1)}, bf16[128,1024]{1,0:T(8,128)(2,1)S(1)}, u32[]{:S(2)}, u32[]{:S(2)}) collective-permute-start(bf16[128,1024]{1,0:T(8,128)(2,1)S(1)} %fusion.3.refs_0_), channel_id=1, source_target_pairs={{0,2},{1,3},{2,4},{3,5},{4,6},{5,7},{6,0},{7,1},{8,10},{9,11},{10,... | collective-permute-start | bytes 786440 | tf_op jit(solution)/shard_map/ppermute | solution.py:142
  28.7 25.9 %collective-permute-start.1 = (bf16[128,1024]{1,0:T(8,128)(2,1)S(1)}, bf16[128,1024]{1,0:T(8,128)(2,1)S(1)}, u32[]{:S(2)}, u32[]{:S(2)}) collective-permute-start(bf16[128,1024]{1,0:T(8,128)(2,1)S(1)} %fusion.3.refs_0_), channel_id=1, source_target_pairs={{0,4},{1,5},{2,6},{3,7},{4,0},{5,1},{6,2},{7,3},{8,12},{9,13},{10,... | collective-permute-start | bytes 786440 | tf_op jit(solution)/shard_map/ppermute | solution.py:142
  30.3 24.5 %collective-permute-start.2 = (bf16[128,1024]{1,0:T(8,128)(2,1)S(1)}, bf16[128,1024]{1,0:T(8,128)(2,1)S(1)}, u32[]{:S(2)}, u32[]{:S(2)}) collective-permute-start(bf16[128,1024]{1,0:T(8,128)(2,1)S(1)} %fusion.3.refs_0_), channel_id=1, source_target_pairs={{0,6},{1,7},{2,0},{3,1},{4,2},{5,3},{6,4},{7,5},{8,14},{9,15},{10,... | collective-permute-start | bytes 786440 | tf_op jit(solution)/shard_map/ppermute | solution.py:142
  46.0 12.2 %collective-permute-start.3 = (bf16[128,1024]{1,0:T(8,128)(2,1)S(1)}, bf16[128,1024]{1,0:T(8,128)(2,1)S(1)}, u32[]{:S(2)}, u32[]{:S(2)}) collective-permute-start(bf16[128,1024]{1,0:T(8,128)(2,1)S(1)} %fusion.3.refs_0_), channel_id=1, source_target_pairs={{0,1},{1,0},{2,3},{3,2},{4,5},{5,4},{6,7},{7,6},{8,9},{9,8},{10,11... | collective-permute-start | bytes 786440 | tf_op jit(solution)/shard_map/ppermute | solution.py:138
  54.7 9.2 %collective-permute-start.5 = (bf16[128,1024]{1,0:T(8,128)(2,1)S(1)}, bf16[128,1024]{1,0:T(8,128)(2,1)S(1)}, u32[]{:S(2)}, u32[]{:S(2)}) collective-permute-start(bf16[128,1024]{1,0:T(8,128)(2,1)S(1)} %collective-permute-done.1.refs_2_), channel_id=1, source_target_pairs={{0,1},{1,0},{2,3},{3,2},{4,5},{5,4},{6,7},{7,6},{8,9},{9,8},{10,11... | collective-permute-start | bytes 786440 | tf_op jit(solution)/shard_map/ppermute | solution.py:138
  55.3 9.9 %collective-permute-start.6 = (bf16[128,1024]{1,0:T(8,128)(2,1)S(1)}, bf16[128,1024]{1,0:T(8,128)(2,1)}, u32[]{:S(2)}, u32[]{:S(2)}) collective-permute-start(bf16[128,1024]{1,0:T(8,128)(2,1)S(1)} %collective-permute-done.2.refs_3_), channel_id=1, source_target_pairs={{0,1},{1,0},{2,3},{3,2},{4,5},{5,4},{6,7},{7,6},{8,9},{9,8},{10,11... | collective-permute-start | bytes 786440 | tf_op jit(solution)/shard_map/ppermute | solution.py:138
  55.8 29.1 %collective-permute-start.29 = (bf16[784,256]{1,0:T(8,128)(2,1)S(1)}, bf16[784,256]{1,0:T(8,128)(2,1)S(1)}, u32[]{:S(2)}, u32[]{:S(2)}) collective-permute-start(bf16[784,256]{1,0:T(8,128)(2,1)S(1)} %pad_maximum_fusion.refs_8_.refs_0_), channel_id=1, source_target_pairs={{0,8},{8,0},{16,24},{24,16},{1,9},{9,1},{17,25},{25,17},{2,10},{10... | collective-permute-start | bytes 1204232 | tf_op jit(solution)/shard_map/ppermute | solution.py:152
  58.2 26.9 %collective-permute-start.30 = (bf16[784,256]{1,0:T(8,128)(2,1)S(1)}, bf16[784,256]{1,0:T(8,128)(2,1)S(1)}, u32[]{:S(2)}, u32[]{:S(2)}) collective-permute-start(bf16[784,256]{1,0:T(8,128)(2,1)S(1)} %pad_maximum_fusion.refs_8_.refs_0_), channel_id=1, source_target_pairs={{0,16},{8,24},{16,0},{24,8},{1,17},{9,25},{17,1},{25,9},{2,18},{10... | collective-permute-start | bytes 1204232 | tf_op jit(solution)/shard_map/ppermute | solution.py:152
  59.8 8.4 %collective-permute-start.18 = (bf16[2,128,256]{2,1,0:T(8,128)(2,1)}, bf16[2,128,256]{2,1,0:T(8,128)(2,1)}, u32[]{:S(2)}, u32[]{:S(2)}) collective-permute-start(bf16[2,128,256]{2,1,0:T(8,128)(2,1)} %get-tuple-element.129), channel_id=1, source_target_pairs={{0,2},{1,3},{2,4},{3,5},{4,6},{5,7},{6,0},{7,1},{8,10},{9,11},{10,... | collective-permute-start | bytes 393224 | tf_op jit(solution)/shard_map/ppermute | solution.py:142
  64.7 20.2 %collective-permute-start.19 = (bf16[2,128,256]{2,1,0:T(8,128)(2,1)}, bf16[2,128,256]{2,1,0:T(8,128)(2,1)}, u32[]{:S(2)}, u32[]{:S(2)}) collective-permute-start(bf16[2,128,256]{2,1,0:T(8,128)(2,1)} %get-tuple-element.130), channel_id=1, source_target_pairs={{0,4},{1,5},{2,6},{3,7},{4,0},{5,1},{6,2},{7,3},{8,12},{9,13},{10,... | collective-permute-start | bytes 393224 | tf_op jit(solution)/shard_map/ppermute | solution.py:142
  65.2 33.9 %collective-permute-start.31 = (bf16[784,256]{1,0:T(8,128)(2,1)S(1)}, bf16[784,256]{1,0:T(8,128)(2,1)S(1)}, u32[]{:S(2)}, u32[]{:S(2)}) collective-permute-start(bf16[784,256]{1,0:T(8,128)(2,1)S(1)} %pad_maximum_fusion.refs_8_.refs_0_), channel_id=1, source_target_pairs={{0,24},{8,16},{16,8},{24,0},{1,25},{9,17},{17,9},{25,1},{2,26},{10... | collective-permute-start | bytes 1204232 | tf_op jit(solution)/shard_map/ppermute | solution.py:152
  68.2 17.0 %collective-permute-start.7 = (bf16[128,1024]{1,0:T(8,128)(2,1)S(1)}, bf16[128,1024]{1,0:T(8,128)(2,1)S(1)}, u32[]{:S(2)}, u32[]{:S(2)}) collective-permute-start(bf16[128,1024]{1,0:T(8,128)(2,1)S(1)} %bitcast_convert_fusion.refs_0_), channel_id=1, source_target_pairs={{0,2},{1,3},{2,4},{3,5},{4,6},{5,7},{6,0},{7,1},{8,10},{9,11},{10,... | collective-permute-start | bytes 786440 | tf_op jit(solution)/shard_map/ppermute | solution.py:142
  84.9 10.1 %collective-permute-start.8 = (bf16[128,1024]{1,0:T(8,128)(2,1)S(1)}, bf16[128,1024]{1,0:T(8,128)(2,1)S(1)}, u32[]{:S(2)}, u32[]{:S(2)}) collective-permute-start(bf16[128,1024]{1,0:T(8,128)(2,1)S(1)} %bitcast_convert_fusion.refs_0_), channel_id=1, source_target_pairs={{0,4},{1,5},{2,6},{3,7},{4,0},{5,1},{6,2},{7,3},{8,12},{9,13},{10,... | collective-permute-start | bytes 786440 | tf_op jit(solution)/shard_map/ppermute | solution.py:142
  84.9 13.5 %collective-permute-start.9 = (bf16[128,1024]{1,0:T(8,128)(2,1)S(1)}, bf16[128,1024]{1,0:T(8,128)(2,1)S(1)}, u32[]{:S(2)}, u32[]{:S(2)}) collective-permute-start(bf16[128,1024]{1,0:T(8,128)(2,1)S(1)} %bitcast_convert_fusion.refs_0_), channel_id=1, source_target_pairs={{0,6},{1,7},{2,0},{3,1},{4,2},{5,3},{6,4},{7,5},{8,14},{9,15},{10,... | collective-permute-start | bytes 786440 | tf_op jit(solution)/shard_map/ppermute | solution.py:142
  85.1 33.4 %collective-permute-start.10 = (bf16[128,1024]{1,0:T(8,128)(2,1)S(1)}, bf16[128,1024]{1,0:T(8,128)(2,1)}, u32[]{:S(2)}, u32[]{:S(2)}) collective-permute-start(bf16[128,1024]{1,0:T(8,128)(2,1)S(1)} %bitcast_convert_fusion.refs_0_), channel_id=1, source_target_pairs={{0,1},{1,0},{2,3},{3,2},{4,5},{5,4},{6,7},{7,6},{8,9},{9,8},{10,11... | collective-permute-start | bytes 786440 | tf_op jit(solution)/shard_map/ppermute | solution.py:138
  85.2 33.3 %collective-permute-start.11 = (bf16[128,1024]{1,0:T(8,128)(2,1)S(1)}, bf16[128,1024]{1,0:T(8,128)(2,1)}, u32[]{:S(2)}, u32[]{:S(2)}) collective-permute-start(bf16[128,1024]{1,0:T(8,128)(2,1)S(1)} %collective-permute-done.7.refs_1_), channel_id=1, source_target_pairs={{0,1},{1,0},{2,3},{3,2},{4,5},{5,4},{6,7},{7,6},{8,9},{9,8},{10,11... | collective-permute-start | bytes 786440 | tf_op jit(solution)/shard_map/ppermute | solution.py:138
  95.0 23.6 %collective-permute-start.12 = (bf16[128,1024]{1,0:T(8,128)(2,1)S(1)}, bf16[128,1024]{1,0:T(8,128)(2,1)}, u32[]{:S(2)}, u32[]{:S(2)}) collective-permute-start(bf16[128,1024]{1,0:T(8,128)(2,1)S(1)} %collective-permute-done.8.refs_2_), channel_id=1, source_target_pairs={{0,1},{1,0},{2,3},{3,2},{4,5},{5,4},{6,7},{7,6},{8,9},{9,8},{10,11... | collective-permute-start | bytes 786440 | tf_op jit(solution)/shard_map/ppermute | solution.py:138
  98.4 20.2 %collective-permute-start.13 = (bf16[128,1024]{1,0:T(8,128)(2,1)S(1)}, bf16[128,1024]{1,0:T(8,128)(2,1)}, u32[]{:S(2)}, u32[]{:S(2)}) collective-permute-start(bf16[128,1024]{1,0:T(8,128)(2,1)S(1)} %collective-permute-done.9.refs_3_), channel_id=1, source_target_pairs={{0,1},{1,0},{2,3},{3,2},{4,5},{5,4},{6,7},{7,6},{8,9},{9,8},{10,11... | collective-permute-start | bytes 786440 | tf_op jit(solution)/shard_map/ppermute | solution.py:138
  99.1 19.4 %collective-permute-start.20 = (bf16[2,128,256]{2,1,0:T(8,128)(2,1)}, bf16[2,128,256]{2,1,0:T(8,128)(2,1)}, u32[]{:S(2)}, u32[]{:S(2)}) collective-permute-start(bf16[2,128,256]{2,1,0:T(8,128)(2,1)} %get-tuple-element.127), channel_id=1, source_target_pairs={{0,6},{1,7},{2,0},{3,1},{4,2},{5,3},{6,4},{7,5},{8,14},{9,15},{10,... | collective-permute-start | bytes 393224 | tf_op jit(solution)/shard_map/ppermute | solution.py:142
  172.1 12.4 %collective-permute-start.48 = (bf16[784,256]{1,0:T(8,128)(2,1)}, bf16[784,256]{1,0:T(8,128)(2,1)S(1)}, u32[]{:S(2)}, u32[]{:S(2)}) collective-permute-start(bf16[784,256]{1,0:T(8,128)(2,1)} %get-tuple-element.108), channel_id=1, source_target_pairs={{0,8},{8,0},{16,24},{24,16},{1,9},{9,1},{17,25},{25,17},{2,10},{10... | collective-permute-start | bytes 1204232 | tf_op jit(solution)/shard_map/ppermute | solution.py:152
  172.6 17.6 %collective-permute-start.49 = (bf16[784,256]{1,0:T(8,128)(2,1)}, bf16[784,256]{1,0:T(8,128)(2,1)S(1)}, u32[]{:S(2)}, u32[]{:S(2)}) collective-permute-start(bf16[784,256]{1,0:T(8,128)(2,1)} %get-tuple-element.109), channel_id=1, source_target_pairs={{0,16},{8,24},{16,0},{24,8},{1,17},{9,25},{17,1},{25,9},{2,18},{10... | collective-permute-start | bytes 1204232 | tf_op jit(solution)/shard_map/ppermute | solution.py:152
  173.1 17.1 %collective-permute-start.50 = (bf16[784,256]{1,0:T(8,128)(2,1)}, bf16[784,256]{1,0:T(8,128)(2,1)S(1)}, u32[]{:S(2)}, u32[]{:S(2)}) collective-permute-start(bf16[784,256]{1,0:T(8,128)(2,1)} %get-tuple-element.110), channel_id=1, source_target_pairs={{0,24},{8,16},{16,8},{24,0},{1,25},{9,17},{17,9},{25,1},{2,26},{10... | collective-permute-start | bytes 1204232 | tf_op jit(solution)/shard_map/ppermute | solution.py:152
  175.6 27.0 %collective-permute-start.39 = (bf16[4,128,1024]{2,1,0:T(8,128)(2,1)}, bf16[4,128,1024]{2,1,0:T(8,128)(2,1)S(1)}, u32[]{:S(2)}, u32[]{:S(2)}) collective-permute-start(bf16[4,128,1024]{2,1,0:T(8,128)(2,1)} %get-tuple-element.90), channel_id=1, source_target_pairs={{0,1},{1,0},{2,3},{3,2},{4,5},{5,4},{6,7},{7,6},{8,9},{9,8},{10,11... | collective-permute-start | bytes 3145736 | tf_op jit(solution)/shard_map/ppermute | solution.py:138
  193.4 62.7 %collective-permute-start.35 = (bf16[4,160,1024]{2,1,0:T(8,128)(2,1)}, bf16[4,160,1024]{2,1,0:T(8,128)(2,1)S(1)}, u32[]{:S(2)}, u32[]{:S(2)}) collective-permute-start(bf16[4,160,1024]{2,1,0:T(8,128)(2,1)} %get-tuple-element.80), channel_id=1, source_target_pairs={{0,1},{1,0},{2,3},{3,2},{4,5},{5,4},{6,7},{7,6},{8,9},{9,8},{10,11... | collective-permute-start | bytes 3932168 | tf_op jit(solution)/shard_map/ppermute | solution.py:138
  199.1 10.0 %collective-permute-start.55 = (bf16[256,256]{1,0:T(8,128)(2,1)}, bf16[256,256]{1,0:T(8,128)(2,1)}, u32[]{:S(2)}, u32[]{:S(2)}) collective-permute-start(bf16[256,256]{1,0:T(8,128)(2,1)} %get-tuple-element.115), channel_id=1, source_target_pairs={{1,4},{3,5},{5,6},{4,2},{0,3},{2,0},{6,7},{9,12},{11,13},{13,14},{... | collective-permute-start | bytes 393224 | tf_op jit(solution)/shard_map/ppermute | solution.py:904
  201.2 7.1 %collective-permute-start.58 = (bf16[224,256]{1,0:T(8,128)(2,1)}, bf16[224,256]{1,0:T(8,128)(2,1)}, u32[]{:S(2)}, u32[]{:S(2)}) collective-permute-start(bf16[224,256]{1,0:T(8,128)(2,1)} %get-tuple-element.118), channel_id=1, source_target_pairs={{2,1},{4,5},{10,9},{12,13},{18,17},{20,21},{26,25},{28,29}} | collective-permute-start | bytes 344072 | tf_op jit(solution)/shard_map/ppermute | solution.py:904
  207.7 16.6 %collective-permute-start.52 = (bf16[288,256]{1,0:T(8,128)(2,1)}, bf16[288,256]{1,0:T(8,128)(2,1)S(1)}, u32[]{:S(2)}, u32[]{:S(2)}) collective-permute-start(bf16[288,256]{1,0:T(8,128)(2,1)} %get-tuple-element.112), channel_id=1, source_target_pairs={{1,7},{9,15},{17,23},{25,31}} | collective-permute-start | bytes 442376 | tf_op jit(solution)/shard_map/ppermute | solution.py:904
  208.4 16.6 %collective-permute-start.53 = (bf16[288,256]{1,0:T(8,128)(2,1)}, bf16[288,256]{1,0:T(8,128)(2,1)S(1)}, u32[]{:S(2)}, u32[]{:S(2)}) collective-permute-start(bf16[288,256]{1,0:T(8,128)(2,1)} %get-tuple-element.113), channel_id=1, source_target_pairs={{3,7},{11,15},{19,23},{27,31}} | collective-permute-start | bytes 442376 | tf_op jit(solution)/shard_map/ppermute | solution.py:904
  210.4 8.3 %collective-permute-start.57 = (bf16[256,256]{1,0:T(8,128)(2,1)}, bf16[256,256]{1,0:T(8,128)(2,1)S(1)}, u32[]{:S(2)}, u32[]{:S(2)}) collective-permute-start(bf16[256,256]{1,0:T(8,128)(2,1)} %get-tuple-element.117), channel_id=1, source_target_pairs={{7,3},{0,4},{6,2},{2,5},{4,1},{15,11},{8,12},{14,10},{10,13},{12,9... | collective-permute-start | bytes 393224 | tf_op jit(solution)/shard_map/ppermute | solution.py:904
  214.0 13.5 %collective-permute-start.44 = (f32[152,128]{1,0:T(8,128)S(1)}, f32[152,128]{1,0:T(8,128)S(1)}, u32[]{:S(2)}, u32[]{:S(2)}) collective-permute-start(f32[152,128]{1,0:T(8,128)S(1)} %fusion.31), channel_id=1, source_target_pairs={{0,2},{1,3},{2,0},{3,1},{4,6},{5,7},{6,4},{7,5},{8,10},{9,11},{10,... | collective-permute-start | bytes 233480 | tf_op jit(solution)/shard_map/ppermute | solution.py:212
  219.3 35.3 %collective-permute-start.40 = (bf16[128,1024]{1,0:T(8,128)(2,1)}, bf16[128,1024]{1,0:T(8,128)(2,1)S(1)}, u32[]{:S(2)}, u32[]{:S(2)}) collective-permute-start(bf16[128,1024]{1,0:T(8,128)(2,1)} %get-tuple-element.92), channel_id=1, source_target_pairs={{0,2},{1,3},{2,4},{3,5},{4,6},{5,7},{6,0},{7,1},{8,10},{9,11},{10,... | collective-permute-start | bytes 786440 | tf_op jit(solution)/shard_map/ppermute | solution.py:142
  224.9 29.7 %collective-permute-start.41 = (bf16[128,1024]{1,0:T(8,128)(2,1)}, bf16[128,1024]{1,0:T(8,128)(2,1)S(1)}, u32[]{:S(2)}, u32[]{:S(2)}) collective-permute-start(bf16[128,1024]{1,0:T(8,128)(2,1)} %get-tuple-element.93), channel_id=1, source_target_pairs={{0,4},{1,5},{2,6},{3,7},{4,0},{5,1},{6,2},{7,3},{8,12},{9,13},{10,... | collective-permute-start | bytes 786440 | tf_op jit(solution)/shard_map/ppermute | solution.py:142
  224.9 29.7 %collective-permute-start.42 = (bf16[128,1024]{1,0:T(8,128)(2,1)}, bf16[128,1024]{1,0:T(8,128)(2,1)}, u32[]{:S(2)}, u32[]{:S(2)}) collective-permute-start(bf16[128,1024]{1,0:T(8,128)(2,1)} %get-tuple-element.94), channel_id=1, source_target_pairs={{0,6},{1,7},{2,0},{3,1},{4,2},{5,3},{6,4},{7,5},{8,14},{9,15},{10,... | collective-permute-start | bytes 786440 | tf_op jit(solution)/shard_map/ppermute | solution.py:142
  229.0 22.7 %collective-permute-start.45 = (f32[152,128]{1,0:T(8,128)S(1)}, f32[152,128]{1,0:T(8,128)}, u32[]{:S(2)}, u32[]{:S(2)}) collective-permute-start(f32[152,128]{1,0:T(8,128)S(1)} %add.248), channel_id=1, source_target_pairs={{0,4},{1,5},{2,6},{3,7},{4,0},{5,1},{6,2},{7,3},{8,12},{9,13},{10,... | collective-permute-start | bytes 233480 | tf_op jit(solution)/shard_map/ppermute | solution.py:212
  253.1 12.0 %collective-permute-start.46 = (f32[152,128]{1,0:T(8,128)}, f32[152,128]{1,0:T(8,128)S(1)}, u32[]{:S(2)}, u32[]{:S(2)}) collective-permute-start(f32[152,128]{1,0:T(8,128)} %add.249), channel_id=1, source_target_pairs={{0,8},{8,0},{16,24},{24,16},{1,9},{9,1},{17,25},{25,17},{2,10},{10... | collective-permute-start | bytes 233480 | tf_op jit(solution)/shard_map/ppermute | solution.py:212
  261.2 14.1 %collective-permute-start.36 = (bf16[192,1024]{1,0:T(8,128)(2,1)}, bf16[192,1024]{1,0:T(8,128)(2,1)S(1)}, u32[]{:S(2)}, u32[]{:S(2)}) collective-permute-start(bf16[192,1024]{1,0:T(8,128)(2,1)} %get-tuple-element.82), channel_id=1, source_target_pairs={{0,2},{1,3},{2,4},{3,5},{4,6},{5,7},{6,0},{7,1},{8,10},{9,11},{10,... | collective-permute-start | bytes 1179656 | tf_op jit(solution)/shard_map/ppermute | solution.py:142
  261.3 29.6 %collective-permute-start.37 = (bf16[192,1024]{1,0:T(8,128)(2,1)}, bf16[192,1024]{1,0:T(8,128)(2,1)}, u32[]{:S(2)}, u32[]{:S(2)}) collective-permute-start(bf16[192,1024]{1,0:T(8,128)(2,1)} %get-tuple-element.83), channel_id=1, source_target_pairs={{0,4},{1,5},{2,6},{3,7},{4,0},{5,1},{6,2},{7,3},{8,12},{9,13},{10,... | collective-permute-start | bytes 1179656 | tf_op jit(solution)/shard_map/ppermute | solution.py:142
  263.8 31.9 %collective-permute-start.38 = (bf16[192,1024]{1,0:T(8,128)(2,1)}, bf16[192,1024]{1,0:T(8,128)(2,1)}, u32[]{:S(2)}, u32[]{:S(2)}) collective-permute-start(bf16[192,1024]{1,0:T(8,128)(2,1)} %get-tuple-element.84), channel_id=1, source_target_pairs={{0,6},{1,7},{2,0},{3,1},{4,2},{5,3},{6,4},{7,5},{8,14},{9,15},{10,... | collective-permute-start | bytes 1179656 | tf_op jit(solution)/shard_map/ppermute | solution.py:142
  302.0 6.0 %collective-permute-start.59 = (bf16[2,128,256]{2,1,0:T(8,128)(2,1)S(1)}, bf16[2,128,256]{2,1,0:T(8,128)(2,1)S(1)}, u32[]{:S(2)}, u32[]{:S(2)}) collective-permute-start(bf16[2,128,256]{2,1,0:T(8,128)(2,1)S(1)} %get-tuple-element.122), channel_id=1, source_target_pairs={{0,8},{8,0},{16,24},{24,16},{1,9},{9,1},{17,25},{25,17},{2,10},{10... | collective-permute-start | bytes 393224 | tf_op jit(solution)/shard_map/ppermute | solution.py:152
  302.6 5.5 %collective-permute-start.60 = (bf16[2,128,256]{2,1,0:T(8,128)(2,1)S(1)}, bf16[2,128,256]{2,1,0:T(8,128)(2,1)S(1)}, u32[]{:S(2)}, u32[]{:S(2)}) collective-permute-start(bf16[2,128,256]{2,1,0:T(8,128)(2,1)S(1)} %get-tuple-element.124), channel_id=1, source_target_pairs={{0,16},{8,24},{16,0},{24,8},{1,17},{9,25},{17,1},{25,9},{2,18},{10... | collective-permute-start | bytes 393224 | tf_op jit(solution)/shard_map/ppermute | solution.py:152
  303.8 5.9 %collective-permute-start.61 = (bf16[2,128,256]{2,1,0:T(8,128)(2,1)S(1)}, bf16[2,128,256]{2,1,0:T(8,128)(2,1)S(1)}, u32[]{:S(2)}, u32[]{:S(2)}) collective-permute-start(bf16[2,128,256]{2,1,0:T(8,128)(2,1)S(1)} %get-tuple-element.123), channel_id=1, source_target_pairs={{0,24},{8,16},{16,8},{24,0},{1,25},{9,17},{17,9},{25,1},{2,26},{10... | collective-permute-start | bytes 393224 | tf_op jit(solution)/shard_map/ppermute | solution.py:152
  (72 other events, 1170.3 us)
where the time goes:
time: 314 us; the launch traced here: 311 us
  waiting for transfers between devices  100 us (32%)
  starting transfers between devices  83.5 us (27%)
  Pallas kernels  77.7 us (25%)
  local copies, waits for them, and re-layouts  28 us (9%)
  other arithmetic  18.6 us (6%)
    pallas_call x11, Pallas kernels, call(): pl.pallas_call(kernel, out_shape=[jax.ShapeDtypeStruct(shape, kind) for s...  77.7 us
    ppermute x15, waiting for transfers between devices, hop(): lax.ppermute(x, 'seq', [(i, (i + step) % self.S) for i in range(self.S)])  40.3 us
    ppermute x8, waiting for transfers between devices, sum_axis(): x = x + lax.ppermute(x, axis, [(i, i ^ k) for i in range(size)])  31.3 us
    ppermute x15, starting transfers between devices, hop(): lax.ppermute(x, 'seq', [(i, (i + step) % self.S) for i in range(self.S)])  28.5 us
    ppermute x12, waiting for transfers between devices, across(): return lax.ppermute(x, 'fsdp', pairs)  16.3 us
    ppermute x12, starting transfers between devices, across(): return lax.ppermute(x, 'fsdp', pairs)  15.3 us
    ppermute x7, starting transfers between devices, per_device(): lax.ppermute(picked[r], 'seq', [(p[0], p[1]) for p in group])  14.6 us
    ppermute x7, waiting for transfers between devices, per_device(): lax.ppermute(picked[r], 'seq', [(p[0], p[1]) for p in group])  11.5 us
  transfers between devices with their start and end apart: 62, of which 18 were waited for; matrix products, arithmetic and copies ran while one was open for 10% of the time, Pallas kernels for 11%

commit v1 on v0

--- a/solution.py
+++ b/solution.py
@@ -18,17 +18,29 @@
 HALO = 8
 BF = jnp.bfloat16
 F32 = jnp.float32
-HIGH = lax.Precision.HIGHEST
 
 
 def ceil_to(n, k):
     return (n + k - 1) // k * k
 
 
-def dot(a, b, ca, cb, precision=None):
-    return lax.dot_general(
-        a, b, (((ca,), (cb,)), ((), ())), precision=precision, preferred_element_type=F32
-    )
+def dot(a, b, ca, cb):
+    return lax.dot_general(a, b, (((ca,), (cb,)), ((), ())), preferred_element_type=F32)
+
+
+def thirds(x):
+    parts = []
+    for _ in range(3):
+        part = x.astype(BF)
+        parts.append(part)
+        x = x - part.astype(F32)
+    return parts
+
+
+def pick_sums(picks, x, cp, cx, first=True):
+    if first:
+        return sum(dot(picks, part, cp, cx) for part in thirds(x))
+    return sum(dot(part, picks, cx, cp) for part in thirds(x))
 
 
 class Routes:
@@ -54,6 +66,7 @@
         remote = [p for p in pieces if p[0] != p[1]]
         common = [p for p in remote if p[4] >= 2 * width]
         self.rounds = self.color(common) + self.color([p for p in remote if p[4] < 2 * width])
+        self.kinds = [group[0][4] >= 2 * width for group in self.rounds]
         self.sizes = [ceil_to(max(p[3] for p in group), 16) for group in self.rounds]
         self.starts = [sum(self.sizes[:r]) for r in range(len(self.sizes))]
         total = sum(self.sizes)
@@ -203,15 +216,19 @@
             total = total + self.across(parts[k], k).astype(F32)
         return total
 
-    def sum_axis(self, x, axis):
-        size = self.S if axis == "seq" else self.F
-        if size & (size - 1):
-            return lax.psum(x, axis)
-        k = 1
-        while k < size:
-            x = x + lax.ppermute(x, axis, [(i, i ^ k) for i in range(size)])
-            k *= 2
-        return x
+    def sum_seq(self, x):
+        if self.pair == 2:
+            x = x + self.swap(x)
+        total = x
+        for k in range(1, self.chips):
+            total = total + self.hop(x, k)
+        return total
+
+    def sum_fsdp(self, x):
+        total = x
+        for k in range(1, self.F):
+            total = total + self.across(x, k)
+        return total
 
 
 def spread(values, heads):
@@ -311,7 +328,7 @@
         cs = act[:, width + STATE :].astype(BF)
         dt = softplus(widen(proj[:, width + chans :].astype(F32)) + hp_ref[0:1])
         rate = -jnp.exp(hp_ref[1:2]) * dt
-        run = dot(tri(True).astype(F32), rate, 1, 0, HIGH)
+        run = pick_sums(tri(True).astype(F32).astype(BF), rate, 1, 0)
         run_t = run.T
         last = run[GROUP - 1 : GROUP]
         xdt = (xs * spread(dt, heads)).astype(BF)
@@ -342,7 +359,7 @@
     wo_refs, refs = refs[:chips], refs[chips:]
     y_ref, proj_ref, gain_ref, cot_ref, wo_ref, dg_ref, stats_ref = refs
     width = y_ref.shape[1]
-    ones = jnp.ones((8, width), F32)
+    ones = jnp.ones((16, width), BF)
     assemble(pieces, cot_ref, chips, pair)
     part = wo_refs[0].shape[1]
     for k in range(chips):
@@ -356,8 +373,8 @@
         dg_ref[rows, :] = dg
         z = proj_ref[rows, :width].astype(F32)
         u = y_ref[rows, :].astype(F32) * (z * jax.nn.sigmoid(z))
-        stats_ref[0:1, rows] = dot(ones, u * u, 1, 1, HIGH)[0:1]
-        stats_ref[1:2, rows] = dot(ones, u * gain_ref[...] * dg, 1, 1, HIGH)[0:1]
+        stats_ref[0:1, rows] = pick_sums(ones, u * u, 1, 1)[0:1]
+        stats_ref[1:2, rows] = pick_sums(ones, u * gain_ref[...] * dg, 1, 1)[0:1]
         return 0
 
     lax.fori_loop(0, cot_ref.shape[0] // GROUP, step, 0, unroll=4)
@@ -457,7 +474,7 @@
     fold = (
         lax.broadcasted_iota(jnp.int32, (width, LANES), 0) // HEAD_DIM
         == lax.broadcasted_iota(jnp.int32, (width, LANES), 1)
-    ).astype(F32)
+    ).astype(F32).astype(BF)
 
     def step(n, _):
         i = blocks - 1 - n
@@ -475,7 +492,7 @@
         dt = softplus(shifted)
         neg = -jnp.exp(hp_ref[1:2])
         rate = neg * dt
-        run = dot(tri(True).astype(F32), rate, 1, 0, HIGH)
+        run = pick_sums(tri(True).astype(F32).astype(BF), rate, 1, 0)
         run_t = run.T
         last = run[GROUP - 1 : GROUP]
         dt_x = spread(dt, heads)
@@ -517,15 +534,15 @@
             ],
             axis=0,
         )
-        folded = dot(
+        folded = pick_sums(
+            fold,
             jnp.concatenate([xs * dxdt, dy * core_ref[rows, :] - xdt_f * dxdt, tops], axis=0),
-            fold,
+            0,
             1,
-            0,
-            HIGH,
+            first=False,
         )
         dend = folded[2 * GROUP : 2 * GROUP + 1]
-        drate = dot(tri(False).astype(F32), folded[GROUP : 2 * GROUP], 1, 0, HIGH) + dend
+        drate = pick_sums(tri(False).astype(F32).astype(BF), folded[GROUP : 2 * GROUP], 1, 0) + dend
         ddt = folded[:GROUP] + neg * drate
         ddtr = ddt * jax.nn.sigmoid(shifted)
         ghp_ref[0:1] += jnp.sum(ddtr, axis=0, keepdims=True)
@@ -576,7 +593,7 @@
     if lanes < width:
         packed = jnp.concatenate([packed, jnp.zeros((1, width - lanes), F32)], axis=1)
     slots_ref[...] = jnp.zeros_like(slots_ref)
-    slots_ref[lax.axis_index("seq")] = jnp.concatenate(
+    slot = jnp.concatenate(
         [
             gcw_ref[:, :width],
             gcb_ref[:, :width],
@@ -586,9 +603,13 @@
         ],
         axis=0,
     )
-    common_ref[...] = jnp.concatenate(
-        [gcw_ref[:, width:], gcb_ref[:, width:], jnp.zeros((3, 2 * STATE), F32)], axis=0
-    )
+    for j in range(width // lanes):
+        slots_ref[lax.axis_index("seq"), j] = slot[:, j * lanes : (j + 1) * lanes]
+    for j in range(2 * STATE // LANES):
+        at = slice(width + j * LANES, width + (j + 1) * LANES)
+        common_ref[j] = jnp.concatenate(
+            [gcw_ref[:, at], gcb_ref[:, at], jnp.zeros((3, LANES), F32)], axis=0
+        )
     shard = w_refs[0].shape[1]
     for k in range(shards):
         at = columns_of(peer_to(lax.axis_index("fsdp"), k, shards), shard)
@@ -615,24 +636,31 @@
         start += out_ref.shape[0]
 
 
-def place_kernel(table_ref, w_ref, *refs):
+def place_kernel(split, kinds, table_ref, w_ref, *refs):
     arrived, out_ref = refs[:-1], refs[-1]
-    index, start, out = table_row(table_ref), 0, None
-    for piece in (w_ref, *arrived):
-        part = dot(chosen(index, start, piece.shape[0]), piece[...], 0, 0)
-        out = part if out is None else out + part
-        start += piece.shape[0]
-    out_ref[...] = out.astype(BF)
-
-
-def back_kernel(table_ref, g_ref, common_ref, pool_ref, *out_refs):
+    index = table_row(table_ref)
+    for rows, kind in ((slice(0, split), False), (slice(split, out_ref.shape[0]), True)):
+        start = w_ref.shape[0]
+        out = dot(chosen(index[:, rows], 0, start), w_ref[...], 0, 0)
+        for shared, piece in zip(kinds, arrived):
+            if shared == kind:
+                out = out + dot(chosen(index[:, rows], start, piece.shape[0]), piece[...], 0, 0)
+            start += piece.shape[0]
+        out_ref[rows, :] = out.astype(BF)
+
+
+def back_kernel(kinds, table_ref, g_ref, common_ref, pool_ref, *out_refs):
     split = pool_ref.shape[0] - common_ref.shape[0]
     pool_ref[:split] = g_ref[:split]
     pool_ref[split:] = common_ref[...]
     index, start = table_row(table_ref), 0
-    for out_ref in out_refs:
+    for shared, out_ref in zip(kinds, out_refs):
         items = index[:, start : start + out_ref.shape[0]]
-        out_ref[...] = dot(chosen(items, 0, pool_ref.shape[0]), pool_ref[...], 0, 0).astype(BF)
+        if shared:
+            out = dot(chosen(items, split, common_ref.shape[0]), common_ref[...], 0, 0)
+        else:
+            out = dot(chosen(items, 0, split), g_ref[:split], 0, 0)
+        out_ref[...] = out.astype(BF)
         start += out_ref.shape[0]
 
 
@@ -726,7 +754,7 @@
     for r, group in enumerate(routes.rounds):
         arrived.append(lax.ppermute(picked[r], "seq", [(p[0], p[1]) for p in group]))
     (mine,) = call(
-        place_kernel,
+        functools.partial(place_kernel, 2 * width, routes.kinds),
         [((routes.rows, rows_here), BF)],
         [],
         jnp.asarray(routes.take),
@@ -760,7 +788,6 @@
 
     wo = links.exchange_seq(parity(links.core), parity(1 - links.core))
     cot_half = grad_out.astype(BF)
-    cot_half, _ = lax.optimization_barrier((cot_half, tuple(normed)))
     cot = links.gather_seq(cot_half)
 
     def local(vector, size, start):
@@ -802,7 +829,7 @@
         proj,
         gain,
     )
-    stats = links.sum_axis(stats, "seq")
+    stats = links.sum_seq(stats)
     halves = [((chips, tokens, depth), BF)] * pair
     part = depth // seq
     extra = part * width // depth
@@ -843,10 +870,15 @@
     dn_halves = back_outs[:pair]
     dproj, gcw, gcb, ghp = back_outs[pair:]
     shard = depth // fsdp
+    lanes = min(width, LANES)
     *g_cols, g_norm, slots, g_shared = call(
         functools.partial(columns_kernel, heads, fsdp),
         [((cols, shard), BF)] * fsdp
-        + [((1, depth), F32), ((seq, 8, width), F32), ((8, 2 * STATE), F32)],
+        + [
+            ((1, depth), F32),
+            ((seq, width // lanes, 8, lanes), F32),
+            ((2 * STATE // LANES, 8, LANES), F32),
+        ],
         [],
         dproj,
         normed_all,
@@ -878,7 +910,7 @@
     owned_w_out = links.scatter_fsdp(to).transpose(0, 2, 1).reshape(w_out.shape)
 
     g_mine = links.scatter_fsdp(g_cols)
-    dnormed, dn_arrived = links.scatter_seq(dn_halves[0], dn_halves[-1], tokens)
+    dnormed, _ = links.scatter_seq(dn_halves[0], dn_halves[-1], tokens)
     dscaled = dnormed * norm_gain
     du_norm = scale * dscaled - residual * (
         scale * scale * scale * jnp.mean(residual * dscaled, axis=-1, keepdims=True)
@@ -892,7 +924,7 @@
         other = lax.ppermute(g_common, "seq", [(i, i + 1) for i in range(0, seq, 2)])
         g_common = (g_common.astype(F32) + other.astype(F32)).astype(BF)
     g_pool, *sent = call(
-        back_kernel,
+        functools.partial(back_kernel, routes.kinds),
         [((routes.rows, rows_here), BF)] + [((size, rows_here), BF) for size in routes.sizes],
         [],
         jnp.asarray(routes.back),
@@ -907,15 +939,16 @@
     )
     owned_w_in = owned_w_in.T
 
-    pieces, _ = lax.optimization_barrier(([slots, g_shared, g_norm], dn_arrived[0]))
+    pieces, _ = lax.optimization_barrier(([slots, g_shared, g_norm], tuple(g_cols)))
     packed = jnp.concatenate([p.reshape(-1, LANES) for p in pieces], axis=0)
-    packed = links.sum_axis(packed, "seq")
-    packed = links.sum_axis(packed, "fsdp")
+    packed = links.sum_fsdp(links.sum_seq(packed))
     first = slots.size // LANES
     slots = packed[:first].reshape(slots.shape)
     second = first + g_shared.size // LANES
     g_shared = packed[first:second].reshape(g_shared.shape)
     g_norm = packed[second:].reshape(-1) / norm_gain
+    slots = slots.transpose(0, 2, 1, 3).reshape(seq, 8, width)
+    g_shared = g_shared.transpose(1, 0, 2).reshape(8, 2 * STATE)
     g_conv_w = jnp.concatenate(
         [slots[:, :CONV_W].transpose(1, 0, 2).reshape(CONV_W, inner), g_shared[:CONV_W]], axis=1
     )

time: 314 us -> 309 us (0.984)
  the two profiles are of different devices: /device:TPU:0 before, /device:TPU:24 now
where the time goes in v1:
time: 309 us; the launch traced here: 308 us
  waiting for transfers between devices  120 us (39%)
  starting transfers between devices  84.2 us (27%)
  Pallas kernels  71.9 us (23%)
  local copies, waits for them, and re-layouts  16.4 us (5%)
  other arithmetic  13.9 us (4%)
    pallas_call x11, Pallas kernels, call(): pl.pallas_call(kernel, out_shape=[jax.ShapeDtypeStruct(shape, kind) for s...  71.9 us
    ppermute x21, waiting for transfers between devices, hop(): lax.ppermute(x, 'seq', [(i, (i + step) % self.S) for i in range(self.S)])  71.4 us
    ppermute x21, starting transfers between devices, hop(): lax.ppermute(x, 'seq', [(i, (i + step) % self.S) for i in range(self.S)])  37.7 us
    ppermute x15, waiting for transfers between devices, across(): return lax.ppermute(x, 'fsdp', pairs)  35.2 us
    ppermute x15, starting transfers between devices, across(): return lax.ppermute(x, 'fsdp', pairs)  18.4 us
    ppermute x7, starting transfers between devices, per_device(): homed.append(lax.ppermute(sent[r], 'seq', [(p[1], p[0]) for p in group]))  12.8 us
    ppermute x7, starting transfers between devices, per_device(): lax.ppermute(picked[r], 'seq', [(p[0], p[1]) for p in group])  10.9 us
  transfers between devices with their start and end apart: 65, of which 26 were waited for; matrix products, arithmetic and copies ran while one was open for 6% of the time, Pallas kernels for 11%

profile of v1, /device:TPU:24, one launch (start us, length us, event | category | flops | bytes accessed | tf_op | source)
XLA Modules:
  0.0 308.4 jit_solution(10980041812012067989)
XLA Ops:
  1.8 1.6 collective-permute-start.7
  5.3 3.5 %shard_map.230 = (bf16[288,256]{1,0:T(8,128)(2,1)}, bf16[288,256]{1,0:T(8,128)(2,1)}, bf16[288,256]{1,0:T(8,128)(2,1)}, bf16[256,256]{1,0:T(8,128)(2,1)}, bf16[2...) custom-call(s32[8,1856]{1,0:T(8,128)} %constant.119.clone.table_ref, bf16[548,256]{1,0:T(8,128)(2,1)} %bitcast.164), custom_call_target="tpu_custom_call" | custom-call | tf_op jit(solution)/shard_map/pallas_call | solution.py:702
  12.9 1.9 collective-permute-start.24
  16.3 4.8 %collective-permute-start.25 = (bf16[256,256]{1,0:T(8,128)(2,1)S(1)}, bf16[256,256]{1,0:T(8,128)(2,1)S(1)}, u32[]{:S(2)}, u32[]{:S(2)}) collective-permute-start(bf16[256,256]{1,0:T(8,128)(2,1)S(1)} %copy-done.54), channel_id=1, source_target_pairs={{0,1},{1,3},{2,5},{4,2},{3,6},{6,4},{8,9},{9,11},{10,13},{12,10},{... | collective-permute-start | bytes 393224 | tf_op jit(solution)/shard_map/ppermute | solution.py:755
  23.9 2.2 collective-permute-start.14
  26.1 4.6 %collective-permute-done.26.refs_5_ = bf16[256,256]{1,0:T(8,128)(2,1)S(1)} collective-permute-done((bf16[256,256]{1,0:T(8,128)(2,1)S(1)}, bf16[256,256]{1,0:T(8,128)(2,1)S(1)}, u32[]{:S(2)}, u32[]{:S(2)}) %collective-permute-start.26) | collective-permute-done | bytes 131104 | tf_op jit(solution)/shard_map/ppermute | solution.py:755
  30.7 10.8 %collective-permute-start.15 = (bf16[128,1024]{1,0:T(8,128)(2,1)S(1)}, bf16[128,1024]{1,0:T(8,128)(2,1)S(1)}, u32[]{:S(2)}, u32[]{:S(2)}) collective-permute-start(bf16[128,1024]{1,0:T(8,128)(2,1)S(1)} %fusion.3.refs_0_), channel_id=1, source_target_pairs={{0,4},{1,5},{2,6},{3,7},{4,0},{5,1},{6,2},{7,3},{8,12},{9,13},{10,... | collective-permute-start | bytes 786440 | tf_op jit(solution)/shard_map/ppermute | solution.py:155
  41.5 1.7 collective-permute-start.16
  44.5 3.1 %shard_map.231 = bf16[800,256]{1,0:T(8,128)(2,1)} custom-call(s32[8,800]{1,0:T(8,128)} %constant.120.clone.table_ref, bf16[548,256]{1,0:T(8,128)(2,1)} %bitcast.165, bf16[288,256]{1,0:T(8,128)(2,1)} %copy-done.28, bf16[288,256]{1,0:T(8,128)(2,1)} %copy-done.29, bf16[288,256]{1,0:T(8,128)(2,1)} %copy-done.30, bf16[256,256]{1,0:T(8,128)(2,1)} %copy-done.35, ...), custom_call_target="tpu_custom_call" | custom-call | tf_op jit(solution)/shard_map/pallas_call | solution.py:702
  50.0 1.8 collective-permute-done.28
  52.3 2.2 collective-permute-start
  54.6 4.0 %collective-permute-done.15.refs_2_ = bf16[128,1024]{1,0:T(8,128)(2,1)S(1)} collective-permute-done((bf16[128,1024]{1,0:T(8,128)(2,1)S(1)}, bf16[128,1024]{1,0:T(8,128)(2,1)S(1)}, u32[]{:S(2)}, u32[]{:S(2)}) %collective-permute-start.15) | collective-permute-done | bytes 262176 | tf_op jit(solution)/shard_map/ppermute | solution.py:155
  60.0 3.1 %collective-permute-done.refs_1_ = bf16[128,1024]{1,0:T(8,128)(2,1)S(1)} collective-permute-done((bf16[128,1024]{1,0:T(8,128)(2,1)S(1)}, bf16[128,1024]{1,0:T(8,128)(2,1)S(1)}, u32[]{:S(2)}, u32[]{:S(2)}) %collective-permute-start) | collective-permute-done | bytes 262176 | tf_op jit(solution)/shard_map/ppermute | solution.py:155
  63.1 2.6 collective-permute-start.11
  65.7 15.1 %collective-permute-done.1.refs_2_ = bf16[128,1024]{1,0:T(8,128)(2,1)} collective-permute-done((bf16[128,1024]{1,0:T(8,128)(2,1)S(1)}, bf16[128,1024]{1,0:T(8,128)(2,1)}, u32[]{:S(2)}, u32[]{:S(2)}) %collective-permute-start.1) | collective-permute-done | bytes 262176 | tf_op jit(solution)/shard_map/ppermute | solution.py:155
  85.9 3.7 %collective-permute-done.29.refs_9_.refs_1_ = bf16[784,256]{1,0:T(8,128)(2,1)S(1)} collective-permute-done((bf16[784,256]{1,0:T(8,128)(2,1)S(1)}, bf16[784,256]{1,0:T(8,128)(2,1)S(1)}, u32[]{:S(2)}, u32[]{:S(2)}) %collective-permute-start.29) | collective-permute-done | bytes 401440 | tf_op jit(solution)/shard_map/ppermute | solution.py:165
  90.4 12.9 %collective-permute-done.30.refs_10_.refs_2_ = bf16[784,256]{1,0:T(8,128)(2,1)S(1)} collective-permute-done((bf16[784,256]{1,0:T(8,128)(2,1)S(1)}, bf16[784,256]{1,0:T(8,128)(2,1)S(1)}, u32[]{:S(2)}, u32[]{:S(2)}) %collective-permute-start.30) | collective-permute-done | bytes 401440 | tf_op jit(solution)/shard_map/ppermute | solution.py:165
  107.3 14.3 %shard_map.232 = (bf16[1024,1024]{1,0:T(8,128)(2,1)}, bf16[1024,784]{1,0:T(8,128)(2,1)}, bf16[1024,256]{1,0:T(8,128)(2,1)}, f32[1024,256]{1,0:T(8,128)}, f32[8,128,256]{2,1,0:T(8,128)}) custom-call(bf16[128,1024]{1,0:T(8,128)(2,1)} %copy-done.11, bf16[128,1024]{1,0:T(8,128)(2,1)} %copy-done.19, bf16[128,1024]{1,0:T(8,128)(2,1)} %copy-done.20, ...), custom_call_target="tpu_custom_call" | custom-call | tf_op jit(solution)/shard_map/pallas_call | solution.py:702
  121.7 6.0 %shard_map.233 = (bf16[1024,1024]{1,0:T(8,128)(2,1)}, bf16[1024,256]{1,0:T(8,128)(2,1)}, f32[1024,256]{1,0:T(8,128)}, f32[2,1024]{1,0:T(2,128)}) custom-call(bf16[128,1024]{1,0:T(8,128)(2,1)} %copy-done.14, bf16[128,1024]{1,0:T(8,128)(2,1)} %copy-done.25, bf16[128,1024]{1,0:T(8,128)(2,1)} %collective-permute-done.1.refs_2_, bf16[128,1024]{1,0:T(8,128)(2,1)} %copy-done.26, ...), custom_call_target="tpu_custom_call" | custom-call | tf_op jit(solution)/shard_map/pallas_call | solution.py:702
  129.7 3.8 %collective-permute-start.33 = (f32[2,1024]{1,0:T(2,128)S(1)}, f32[2,1024]{1,0:T(2,128)S(1)}, u32[]{:S(2)}, u32[]{:S(2)}) collective-permute-start(f32[2,1024]{1,0:T(2,128)S(1)} %add.245), channel_id=1, source_target_pairs={{0,2},{1,3},{2,4},{3,5},{4,6},{5,7},{6,0},{7,1},{8,10},{9,11},{10,... | collective-permute-start | bytes 24584 | tf_op jit(solution)/shard_map/ppermute | solution.py:155
  134.9 3.2 %collective-permute-done.34 = f32[2,1024]{1,0:T(2,128)S(1)} collective-permute-done((f32[2,1024]{1,0:T(2,128)S(1)}, f32[2,1024]{1,0:T(2,128)S(1)}, u32[]{:S(2)}, u32[]{:S(2)}) %collective-permute-start.34) | collective-permute-done | bytes 8224 | tf_op jit(solution)/shard_map/ppermute | solution.py:155
  139.6 7.9 %shard_map.234 = (bf16[4,160,1024]{2,1,0:T(8,128)(2,1)}, bf16[4,160,1024]{2,1,0:T(8,128)(2,1)}, bf16[1024,256]{1,0:T(8,128)(2,1)}, bf16[1024,256]{1,0:T(8,128)(2,1)}, f32[1,256]{1,0:T(1,128)}) custom-call(bf16[1024,1024]{1,0:T(8,128)(2,1)} %get-tuple-element.73.cot_ref, bf16[1024,256]{1,0:T(8,128)(2,1)} %get-tuple-element.74.wo_ref, ...), custom_call_target="tpu_custom_call" | custom-call | tf_op jit(solution)/shard_map/pallas_call | solution.py:702
  147.4 19.3 %shard_map.236 = (bf16[4,128,1024]{2,1,0:T(8,128)(2,1)}, bf16[4,128,1024]{2,1,0:T(8,128)(2,1)}, bf16[1024,784]{1,0:T(8,128)(2,1)}, f32[4,512]{1,0:T(4,128)}, f32[1,512]{1,0:T(1,128)}, /*index=5*/f32[8,128]{1,0:T(8,128)}) custom-call(bf16[1024,784]{1,0:T(8,128)(2,1)} %get-tuple-element.72.refs_13_.proj_ref, f32[1024,256]{1,0:T(8,128)} %get-tuple-element.83.core_ref, ...), custom_call_target="tpu_custom_call" | custom-call | tf_op jit(solution)/shard_map/pallas_call | solution.py:702
  166.7 5.6 %shard_map.238 = (bf16[784,256]{1,0:T(8,128)(2,1)}, bf16[784,256]{1,0:T(8,128)(2,1)}, bf16[784,256]{1,0:T(8,128)(2,1)}, bf16[784,256]{1,0:T(8,128)(2,1)}, f32[1,...) custom-call(bf16[1024,784]{1,0:T(8,128)(2,1)} %get-tuple-element.93.dproj_ref, ...), custom_call_target="tpu_custom_call" | custom-call | tf_op jit(solution)/shard_map/pallas_call | solution.py:702
  176.7 1.9 collective-permute-start.47
  178.7 2.2 collective-permute-done.45
  180.9 3.7 %collective-permute-done.46 = f32[152,128]{1,0:T(8,128)S(1)} collective-permute-done((f32[152,128]{1,0:T(8,128)S(1)}, f32[152,128]{1,0:T(8,128)S(1)}, u32[]{:S(2)}, u32[]{:S(2)}) %collective-permute-start.46) | collective-permute-done | bytes 77856 | tf_op jit(solution)/shard_map/ppermute | solution.py:155
  184.6 1.6 collective-permute-start.48
  186.2 1.5 collective-permute-start.49
  189.7 1.5 collective-permute-start.52
  192.3 1.5 collective-permute-done.50
  195.2 6.3 %collective-permute-done.51 = bf16[784,256]{1,0:T(8,128)(2,1)S(1)} collective-permute-done((bf16[784,256]{1,0:T(8,128)(2,1)}, bf16[784,256]{1,0:T(8,128)(2,1)S(1)}, u32[]{:S(2)}, u32[]{:S(2)}) %collective-permute-start.51) | collective-permute-done | bytes 401440 | tf_op jit(solution)/shard_map/ppermute | solution.py:165
  201.5 7.2 %collective-permute-done.52 = bf16[784,256]{1,0:T(8,128)(2,1)S(1)} collective-permute-done((bf16[784,256]{1,0:T(8,128)(2,1)}, bf16[784,256]{1,0:T(8,128)(2,1)S(1)}, u32[]{:S(2)}, u32[]{:S(2)}) %collective-permute-start.52) | collective-permute-done | bytes 401440 | tf_op jit(solution)/shard_map/ppermute | solution.py:165
  212.3 3.1 %shard_map.239 = (bf16[800,256]{1,0:T(8,128)(2,1)}, bf16[288,256]{1,0:T(8,128)(2,1)}, bf16[288,256]{1,0:T(8,128)(2,1)}, bf16[288,256]{1,0:T(8,128)(2,1)}, bf16[2...) custom-call(s32[8,1856]{1,0:T(8,128)} %constant.121.clone.table_ref, ...), custom_call_target="tpu_custom_call" | custom-call | tf_op jit(solution)/shard_map/pallas_call | solution.py:702
  215.4 2.3 collective-permute-start.58
  221.9 4.8 %collective-permute-start.59 = (bf16[256,256]{1,0:T(8,128)(2,1)}, bf16[256,256]{1,0:T(8,128)(2,1)S(1)}, u32[]{:S(2)}, u32[]{:S(2)}) collective-permute-start(bf16[256,256]{1,0:T(8,128)(2,1)} %get-tuple-element.114), channel_id=1, source_target_pairs={{1,0},{3,1},{5,2},{2,4},{6,3},{4,6},{9,8},{11,9},{13,10},{10,12},{... | collective-permute-start | bytes 393224 | tf_op jit(solution)/shard_map/ppermute | solution.py:936
  226.7 3.1 collective-permute-start.60
  230.4 2.7 shard_map.237
  234.2 4.2 %collective-permute-start.42 = (bf16[128,1024]{1,0:T(8,128)(2,1)}, bf16[128,1024]{1,0:T(8,128)(2,1)S(1)}, u32[]{:S(2)}, u32[]{:S(2)}) collective-permute-start(bf16[128,1024]{1,0:T(8,128)(2,1)} %get-tuple-element.91), channel_id=1, source_target_pairs={{0,4},{1,5},{2,6},{3,7},{4,0},{5,1},{6,2},{7,3},{8,12},{9,13},{10,... | collective-permute-start | bytes 786440 | tf_op jit(solution)/shard_map/ppermute | solution.py:155
  243.1 3.4 %shard_map.240 = f32[548,256]{1,0:T(8,128)} custom-call(s32[8,2656]{1,0:T(8,128)} %constant.122.clone.table_ref, bf16[800,256]{1,0:T(8,128)(2,1)} %get-tuple-element.109.refs_0_, bf16[288,256]{1,0:T(8,128)(2,1)} %copy-done.31, bf16[288,256]{1,0:T(8,128)(2,1)} %copy-done.32, bf16[288,256]{1,0:T(8,128)(2,1)} %copy-done.33, bf16[256,256]{1,0:T(8,128)(2,1)} %copy-done.38, ...), custom_call_target="tpu_custom_call" | custom-call | tf_op jit(solution)/shard_map/pallas_call | solution.py:702
  247.6 3.1 shard_map.235
  251.7 3.7 %collective-permute-start.37 = (bf16[192,1024]{1,0:T(8,128)(2,1)}, bf16[192,1024]{1,0:T(8,128)(2,1)S(1)}, u32[]{:S(2)}, u32[]{:S(2)}) collective-permute-start(bf16[192,1024]{1,0:T(8,128)(2,1)} %get-tuple-element.80), channel_id=1, source_target_pairs={{0,2},{1,3},{2,4},{3,5},{4,6},{5,7},{6,0},{7,1},{8,10},{9,11},{10,... | collective-permute-start | bytes 1179656 | tf_op jit(solution)/shard_map/ppermute | solution.py:155
  256.1 5.9 %collective-permute-done.42 = bf16[128,1024]{1,0:T(8,128)(2,1)S(1)} collective-permute-done((bf16[128,1024]{1,0:T(8,128)(2,1)}, bf16[128,1024]{1,0:T(8,128)(2,1)S(1)}, u32[]{:S(2)}, u32[]{:S(2)}) %collective-permute-start.42) | collective-permute-done | bytes 262176 | tf_op jit(solution)/shard_map/ppermute | solution.py:155
  262.3 8.1 %collective-permute-done.37 = bf16[192,1024]{1,0:T(8,128)(2,1)S(1)} collective-permute-done((bf16[192,1024]{1,0:T(8,128)(2,1)}, bf16[192,1024]{1,0:T(8,128)(2,1)S(1)}, u32[]{:S(2)}, u32[]{:S(2)}) %collective-permute-start.37) | collective-permute-done | bytes 393248 | tf_op jit(solution)/shard_map/ppermute | solution.py:155
  271.4 24.4 %collective-permute-done.38 = bf16[192,1024]{1,0:T(8,128)(2,1)} collective-permute-done((bf16[192,1024]{1,0:T(8,128)(2,1)}, bf16[192,1024]{1,0:T(8,128)(2,1)}, u32[]{:S(2)}, u32[]{:S(2)}) %collective-permute-start.38) | collective-permute-done | bytes 393248 | tf_op jit(solution)/shard_map/ppermute | solution.py:155
  300.0 1.6 collective-permute-start.64
  301.6 2.3 fusion
  305.3 2.2 collective-permute-done.64
  (299 shorter events, 64.7 us)
Async XLA Ops:
  1.8 11.1 %collective-permute-start.7 = (bf16[2,128,256]{2,1,0:T(8,128)(2,1)S(1)}, bf16[2,128,256]{2,1,0:T(8,128)(2,1)S(1)}, u32[]{:S(2)}, u32[]{:S(2)}) collective-permute-start(bf16[2,128,256]{2,1,0:T(8,128)(2,1)S(1)} %bitcast.167), channel_id=1, source_target_pairs={{0,8},{8,0},{16,24},{24,16},{1,9},{9,1},{17,25},{25,17},{2,10},{10... | collective-permute-start | bytes 393224 | tf_op jit(solution)/shard_map/ppermute | solution.py:165
  3.3 11.6 %collective-permute-start.8 = (bf16[2,128,256]{2,1,0:T(8,128)(2,1)S(1)}, bf16[2,128,256]{2,1,0:T(8,128)(2,1)S(1)}, u32[]{:S(2)}, u32[]{:S(2)}) collective-permute-start(bf16[2,128,256]{2,1,0:T(8,128)(2,1)S(1)} %bitcast.168), channel_id=1, source_target_pairs={{0,16},{8,24},{16,0},{24,8},{1,17},{9,25},{17,1},{25,9},{2,18},{10... | collective-permute-start | bytes 393224 | tf_op jit(solution)/shard_map/ppermute | solution.py:165
  4.8 11.5 %collective-permute-start.9 = (bf16[2,128,256]{2,1,0:T(8,128)(2,1)S(1)}, bf16[2,128,256]{2,1,0:T(8,128)(2,1)S(1)}, u32[]{:S(2)}, u32[]{:S(2)}) collective-permute-start(bf16[2,128,256]{2,1,0:T(8,128)(2,1)S(1)} %bitcast.169), channel_id=1, source_target_pairs={{0,24},{8,16},{16,8},{24,0},{1,25},{9,17},{17,9},{25,1},{2,26},{10... | collective-permute-start | bytes 393224 | tf_op jit(solution)/shard_map/ppermute | solution.py:165
  8.8 32.7 %collective-permute-start.21 = (bf16[288,256]{1,0:T(8,128)(2,1)}, bf16[288,256]{1,0:T(8,128)(2,1)S(1)}, u32[]{:S(2)}, u32[]{:S(2)}) collective-permute-start(bf16[288,256]{1,0:T(8,128)(2,1)} %get-tuple-element.64), channel_id=1, source_target_pairs={{7,1},{15,9},{23,17},{31,25}} | collective-permute-start | bytes 442376 | tf_op jit(solution)/shard_map/ppermute | solution.py:755
  9.6 33.6 %collective-permute-start.22 = (bf16[288,256]{1,0:T(8,128)(2,1)}, bf16[288,256]{1,0:T(8,128)(2,1)S(1)}, u32[]{:S(2)}, u32[]{:S(2)}) collective-permute-start(bf16[288,256]{1,0:T(8,128)(2,1)} %get-tuple-element.65), channel_id=1, source_target_pairs={{7,3},{15,11},{23,19},{31,27}} | collective-permute-start | bytes 442376 | tf_op jit(solution)/shard_map/ppermute | solution.py:755
  12.9 8.3 %collective-permute-start.24 = (bf16[256,256]{1,0:T(8,128)(2,1)S(1)}, bf16[256,256]{1,0:T(8,128)(2,1)S(1)}, u32[]{:S(2)}, u32[]{:S(2)}) collective-permute-start(bf16[256,256]{1,0:T(8,128)(2,1)S(1)} %copy-done.55), channel_id=1, source_target_pairs={{4,1},{5,3},{6,5},{2,4},{3,0},{0,2},{7,6},{12,9},{13,11},{14,13},{... | collective-permute-start | bytes 393224 | tf_op jit(solution)/shard_map/ppermute | solution.py:755
  15.6 27.6 %collective-permute-start.23 = (bf16[288,256]{1,0:T(8,128)(2,1)}, bf16[288,256]{1,0:T(8,128)(2,1)S(1)}, u32[]{:S(2)}, u32[]{:S(2)}) collective-permute-start(bf16[288,256]{1,0:T(8,128)(2,1)} %get-tuple-element.66), channel_id=1, source_target_pairs={{7,5},{15,13},{23,21},{31,29}} | collective-permute-start | bytes 442376 | tf_op jit(solution)/shard_map/ppermute | solution.py:755
  16.3 7.6 %collective-permute-start.25 = (bf16[256,256]{1,0:T(8,128)(2,1)S(1)}, bf16[256,256]{1,0:T(8,128)(2,1)S(1)}, u32[]{:S(2)}, u32[]{:S(2)}) collective-permute-start(bf16[256,256]{1,0:T(8,128)(2,1)S(1)} %copy-done.54), channel_id=1, source_target_pairs={{0,1},{1,3},{2,5},{4,2},{3,6},{6,4},{8,9},{9,11},{10,13},{12,10},{... | collective-permute-start | bytes 393224 | tf_op jit(solution)/shard_map/ppermute | solution.py:755
  21.2 9.5 %collective-permute-start.26 = (bf16[256,256]{1,0:T(8,128)(2,1)S(1)}, bf16[256,256]{1,0:T(8,128)(2,1)S(1)}, u32[]{:S(2)}, u32[]{:S(2)}) collective-permute-start(bf16[256,256]{1,0:T(8,128)(2,1)S(1)} %copy-done.53), channel_id=1, source_target_pairs={{3,7},{4,0},{2,6},{5,2},{1,4},{11,15},{12,8},{10,14},{13,10},{9,12... | collective-permute-start | bytes 393224 | tf_op jit(solution)/shard_map/ppermute | solution.py:755
  23.9 28.4 %collective-permute-start.14 = (bf16[128,1024]{1,0:T(8,128)(2,1)S(1)}, bf16[128,1024]{1,0:T(8,128)(2,1)S(1)}, u32[]{:S(2)}, u32[]{:S(2)}) collective-permute-start(bf16[128,1024]{1,0:T(8,128)(2,1)S(1)} %fusion.3.refs_0_), channel_id=1, source_target_pairs={{0,2},{1,3},{2,4},{3,5},{4,6},{5,7},{6,0},{7,1},{8,10},{9,11},{10,... | collective-permute-start | bytes 786440 | tf_op jit(solution)/shard_map/ppermute | solution.py:155
  30.7 27.8 %collective-permute-start.15 = (bf16[128,1024]{1,0:T(8,128)(2,1)S(1)}, bf16[128,1024]{1,0:T(8,128)(2,1)S(1)}, u32[]{:S(2)}, u32[]{:S(2)}) collective-permute-start(bf16[128,1024]{1,0:T(8,128)(2,1)S(1)} %fusion.3.refs_0_), channel_id=1, source_target_pairs={{0,4},{1,5},{2,6},{3,7},{4,0},{5,1},{6,2},{7,3},{8,12},{9,13},{10,... | collective-permute-start | bytes 786440 | tf_op jit(solution)/shard_map/ppermute | solution.py:155
  41.5 17.1 %collective-permute-start.16 = (bf16[128,1024]{1,0:T(8,128)(2,1)S(1)}, bf16[128,1024]{1,0:T(8,128)(2,1)S(1)}, u32[]{:S(2)}, u32[]{:S(2)}) collective-permute-start(bf16[128,1024]{1,0:T(8,128)(2,1)S(1)} %fusion.3.refs_0_), channel_id=1, source_target_pairs={{0,6},{1,7},{2,0},{3,1},{4,2},{5,3},{6,4},{7,5},{8,14},{9,15},{10,... | collective-permute-start | bytes 786440 | tf_op jit(solution)/shard_map/ppermute | solution.py:155
  43.2 15.5 %collective-permute-start.17 = (bf16[128,1024]{1,0:T(8,128)(2,1)S(1)}, bf16[128,1024]{1,0:T(8,128)(2,1)S(1)}, u32[]{:S(2)}, u32[]{:S(2)}) collective-permute-start(bf16[128,1024]{1,0:T(8,128)(2,1)S(1)} %fusion.3.refs_0_), channel_id=1, source_target_pairs={{0,1},{1,0},{2,3},{3,2},{4,5},{5,4},{6,7},{7,6},{8,9},{9,8},{10,11... | collective-permute-start | bytes 786440 | tf_op jit(solution)/shard_map/ppermute | solution.py:151
  52.3 10.8 %collective-permute-start = (bf16[128,1024]{1,0:T(8,128)(2,1)S(1)}, bf16[128,1024]{1,0:T(8,128)(2,1)S(1)}, u32[]{:S(2)}, u32[]{:S(2)}) collective-permute-start(bf16[128,1024]{1,0:T(8,128)(2,1)S(1)} %bitcast_convert_fusion.refs_0_), channel_id=1, source_target_pairs={{0,2},{1,3},{2,4},{3,5},{4,6},{5,7},{6,0},{7,1},{8,10},{9,11},{10,... | collective-permute-start | bytes 786440 | tf_op jit(solution)/shard_map/ppermute | solution.py:155
  54.5 26.2 %collective-permute-start.1 = (bf16[128,1024]{1,0:T(8,128)(2,1)S(1)}, bf16[128,1024]{1,0:T(8,128)(2,1)}, u32[]{:S(2)}, u32[]{:S(2)}) collective-permute-start(bf16[128,1024]{1,0:T(8,128)(2,1)S(1)} %bitcast_convert_fusion.refs_0_), channel_id=1, source_target_pairs={{0,4},{1,5},{2,6},{3,7},{4,0},{5,1},{6,2},{7,3},{8,12},{9,13},{10,... | collective-permute-start | bytes 786440 | tf_op jit(solution)/shard_map/ppermute | solution.py:155
  58.5 23.7 %collective-permute-start.2 = (bf16[128,1024]{1,0:T(8,128)(2,1)S(1)}, bf16[128,1024]{1,0:T(8,128)(2,1)S(1)}, u32[]{:S(2)}, u32[]{:S(2)}) collective-permute-start(bf16[128,1024]{1,0:T(8,128)(2,1)S(1)} %bitcast_convert_fusion.refs_0_), channel_id=1, source_target_pairs={{0,6},{1,7},{2,0},{3,1},{4,2},{5,3},{6,4},{7,5},{8,14},{9,15},{10,... | collective-permute-start | bytes 786440 | tf_op jit(solution)/shard_map/ppermute | solution.py:155
  58.6 23.7 %collective-permute-start.3 = (bf16[128,1024]{1,0:T(8,128)(2,1)S(1)}, bf16[128,1024]{1,0:T(8,128)(2,1)S(1)}, u32[]{:S(2)}, u32[]{:S(2)}) collective-permute-start(bf16[128,1024]{1,0:T(8,128)(2,1)S(1)} %bitcast_convert_fusion.refs_0_), channel_id=1, source_target_pairs={{0,1},{1,0},{2,3},{3,2},{4,5},{5,4},{6,7},{7,6},{8,9},{9,8},{10,11... | collective-permute-start | bytes 786440 | tf_op jit(solution)/shard_map/ppermute | solution.py:151
  58.7 25.9 %collective-permute-start.18 = (bf16[128,1024]{1,0:T(8,128)(2,1)S(1)}, bf16[128,1024]{1,0:T(8,128)(2,1)S(1)}, u32[]{:S(2)}, u32[]{:S(2)}) collective-permute-start(bf16[128,1024]{1,0:T(8,128)(2,1)S(1)} %collective-permute-done.14.refs_1_), channel_id=1, source_target_pairs={{0,1},{1,0},{2,3},{3,2},{4,5},{5,4},{6,7},{7,6},{8,9},{9,8},{10,11... | collective-permute-start | bytes 786440 | tf_op jit(solution)/shard_map/ppermute | solution.py:151
  63.1 20.0 %collective-permute-start.11 = (bf16[2,128,256]{2,1,0:T(8,128)(2,1)S(1)}, bf16[2,128,256]{2,1,0:T(8,128)(2,1)S(1)}, u32[]{:S(2)}, u32[]{:S(2)}) collective-permute-start(bf16[2,128,256]{2,1,0:T(8,128)(2,1)S(1)} %get-tuple-element.124), channel_id=1, source_target_pairs={{0,2},{1,3},{2,4},{3,5},{4,6},{5,7},{6,0},{7,1},{8,10},{9,11},{10,... | collective-permute-start | bytes 393224 | tf_op jit(solution)/shard_map/ppermute | solution.py:155
  80.7 8.9 %collective-permute-start.29 = (bf16[784,256]{1,0:T(8,128)(2,1)S(1)}, bf16[784,256]{1,0:T(8,128)(2,1)S(1)}, u32[]{:S(2)}, u32[]{:S(2)}) collective-permute-start(bf16[784,256]{1,0:T(8,128)(2,1)S(1)} %pad_maximum_fusion.refs_8_.refs_0_), channel_id=1, source_target_pairs={{0,8},{8,0},{16,24},{24,16},{1,9},{9,1},{17,25},{25,17},{2,10},{10... | collective-permute-start | bytes 1204232 | tf_op jit(solution)/shard_map/ppermute | solution.py:165
  83.0 20.2 %collective-permute-start.30 = (bf16[784,256]{1,0:T(8,128)(2,1)S(1)}, bf16[784,256]{1,0:T(8,128)(2,1)S(1)}, u32[]{:S(2)}, u32[]{:S(2)}) collective-permute-start(bf16[784,256]{1,0:T(8,128)(2,1)S(1)} %pad_maximum_fusion.refs_8_.refs_0_), channel_id=1, source_target_pairs={{0,16},{8,24},{16,0},{24,8},{1,17},{9,25},{17,1},{25,9},{2,18},{10... | collective-permute-start | bytes 1204232 | tf_op jit(solution)/shard_map/ppermute | solution.py:165
  84.6 20.1 %collective-permute-start.31 = (bf16[784,256]{1,0:T(8,128)(2,1)S(1)}, bf16[784,256]{1,0:T(8,128)(2,1)S(1)}, u32[]{:S(2)}, u32[]{:S(2)}) collective-permute-start(bf16[784,256]{1,0:T(8,128)(2,1)S(1)} %pad_maximum_fusion.refs_8_.refs_0_), channel_id=1, source_target_pairs={{0,24},{8,16},{16,8},{24,0},{1,25},{9,17},{17,9},{25,1},{2,26},{10... | collective-permute-start | bytes 1204232 | tf_op jit(solution)/shard_map/ppermute | solution.py:165
  85.4 36.3 %collective-permute-start.4 = (bf16[128,1024]{1,0:T(8,128)(2,1)}, bf16[128,1024]{1,0:T(8,128)(2,1)}, u32[]{:S(2)}, u32[]{:S(2)}) collective-permute-start(bf16[128,1024]{1,0:T(8,128)(2,1)} %copy-done.25), channel_id=1, source_target_pairs={{0,1},{1,0},{2,3},{3,2},{4,5},{5,4},{6,7},{7,6},{8,9},{9,8},{10,11... | collective-permute-start | bytes 786440 | tf_op jit(solution)/shard_map/ppermute | solution.py:151
  85.6 36.1 %collective-permute-start.5 = (bf16[128,1024]{1,0:T(8,128)(2,1)}, bf16[128,1024]{1,0:T(8,128)(2,1)}, u32[]{:S(2)}, u32[]{:S(2)}) collective-permute-start(bf16[128,1024]{1,0:T(8,128)(2,1)} %collective-permute-done.1.refs_2_), channel_id=1, source_target_pairs={{0,1},{1,0},{2,3},{3,2},{4,5},{5,4},{6,7},{7,6},{8,9},{9,8},{10,11... | collective-permute-start | bytes 786440 | tf_op jit(solution)/shard_map/ppermute | solution.py:151
  89.7 32.0 %collective-permute-start.6 = (bf16[128,1024]{1,0:T(8,128)(2,1)}, bf16[128,1024]{1,0:T(8,128)(2,1)}, u32[]{:S(2)}, u32[]{:S(2)}) collective-permute-start(bf16[128,1024]{1,0:T(8,128)(2,1)} %copy-done.26), channel_id=1, source_target_pairs={{0,1},{1,0},{2,3},{3,2},{4,5},{5,4},{6,7},{7,6},{8,9},{9,8},{10,11... | collective-permute-start | bytes 786440 | tf_op jit(solution)/shard_map/ppermute | solution.py:151
  103.3 18.4 %collective-permute-start.12 = (bf16[2,128,256]{2,1,0:T(8,128)(2,1)}, bf16[2,128,256]{2,1,0:T(8,128)(2,1)}, u32[]{:S(2)}, u32[]{:S(2)}) collective-permute-start(bf16[2,128,256]{2,1,0:T(8,128)(2,1)} %get-tuple-element.125), channel_id=1, source_target_pairs={{0,4},{1,5},{2,6},{3,7},{4,0},{5,1},{6,2},{7,3},{8,12},{9,13},{10,... | collective-permute-start | bytes 393224 | tf_op jit(solution)/shard_map/ppermute | solution.py:155
  104.7 17.0 %collective-permute-start.13 = (bf16[2,128,256]{2,1,0:T(8,128)(2,1)}, bf16[2,128,256]{2,1,0:T(8,128)(2,1)}, u32[]{:S(2)}, u32[]{:S(2)}) collective-permute-start(bf16[2,128,256]{2,1,0:T(8,128)(2,1)} %get-tuple-element.122), channel_id=1, source_target_pairs={{0,6},{1,7},{2,0},{3,1},{4,2},{5,3},{6,4},{7,5},{8,14},{9,15},{10,... | collective-permute-start | bytes 393224 | tf_op jit(solution)/shard_map/ppermute | solution.py:155
  176.1 8.5 %collective-permute-start.46 = (f32[152,128]{1,0:T(8,128)S(1)}, f32[152,128]{1,0:T(8,128)S(1)}, u32[]{:S(2)}, u32[]{:S(2)}) collective-permute-start(f32[152,128]{1,0:T(8,128)S(1)} %fusion.31), channel_id=1, source_target_pairs={{0,4},{1,5},{2,6},{3,7},{4,0},{5,1},{6,2},{7,3},{8,12},{9,13},{10,... | collective-permute-start | bytes 233480 | tf_op jit(solution)/shard_map/ppermute | solution.py:155
  176.7 7.9 %collective-permute-start.47 = (f32[152,128]{1,0:T(8,128)S(1)}, f32[152,128]{1,0:T(8,128)S(1)}, u32[]{:S(2)}, u32[]{:S(2)}) collective-permute-start(f32[152,128]{1,0:T(8,128)S(1)} %fusion.31), channel_id=1, source_target_pairs={{0,6},{1,7},{2,0},{3,1},{4,2},{5,3},{6,4},{7,5},{8,14},{9,15},{10,... | collective-permute-start | bytes 233480 | tf_op jit(solution)/shard_map/ppermute | solution.py:155
  184.6 6.6 %collective-permute-start.48 = (f32[152,128]{1,0:T(8,128)S(1)}, f32[152,128]{1,0:T(8,128)S(1)}, u32[]{:S(2)}, u32[]{:S(2)}) collective-permute-start(f32[152,128]{1,0:T(8,128)S(1)} %add_add_fusion.1), channel_id=1, source_target_pairs={{0,8},{8,0},{16,24},{24,16},{1,9},{9,1},{17,25},{25,17},{2,10},{10... | collective-permute-start | bytes 233480 | tf_op jit(solution)/shard_map/ppermute | solution.py:165
  188.2 13.3 %collective-permute-start.51 = (bf16[784,256]{1,0:T(8,128)(2,1)}, bf16[784,256]{1,0:T(8,128)(2,1)S(1)}, u32[]{:S(2)}, u32[]{:S(2)}) collective-permute-start(bf16[784,256]{1,0:T(8,128)(2,1)} %get-tuple-element.103), channel_id=1, source_target_pairs={{0,8},{8,0},{16,24},{24,16},{1,9},{9,1},{17,25},{25,17},{2,10},{10... | collective-permute-start | bytes 1204232 | tf_op jit(solution)/shard_map/ppermute | solution.py:165
  189.7 19.0 %collective-permute-start.52 = (bf16[784,256]{1,0:T(8,128)(2,1)}, bf16[784,256]{1,0:T(8,128)(2,1)S(1)}, u32[]{:S(2)}, u32[]{:S(2)}) collective-permute-start(bf16[784,256]{1,0:T(8,128)(2,1)} %get-tuple-element.104), channel_id=1, source_target_pairs={{0,16},{8,24},{16,0},{24,8},{1,17},{9,25},{17,1},{25,9},{2,18},{10... | collective-permute-start | bytes 1204232 | tf_op jit(solution)/shard_map/ppermute | solution.py:165
  191.2 17.5 %collective-permute-start.53 = (bf16[784,256]{1,0:T(8,128)(2,1)}, bf16[784,256]{1,0:T(8,128)(2,1)S(1)}, u32[]{:S(2)}, u32[]{:S(2)}) collective-permute-start(bf16[784,256]{1,0:T(8,128)(2,1)} %get-tuple-element.105), channel_id=1, source_target_pairs={{0,24},{8,16},{16,8},{24,0},{1,25},{9,17},{17,9},{25,1},{2,26},{10... | collective-permute-start | bytes 1204232 | tf_op jit(solution)/shard_map/ppermute | solution.py:165
  192.3 54.2 %collective-permute-start.36 = (bf16[4,160,1024]{2,1,0:T(8,128)(2,1)}, bf16[4,160,1024]{2,1,0:T(8,128)(2,1)S(1)}, u32[]{:S(2)}, u32[]{:S(2)}) collective-permute-start(bf16[4,160,1024]{2,1,0:T(8,128)(2,1)} %get-tuple-element.78), channel_id=1, source_target_pairs={{0,1},{1,0},{2,3},{3,2},{4,5},{5,4},{6,7},{7,6},{8,9},{9,8},{10,11... | collective-permute-start | bytes 3932168 | tf_op jit(solution)/shard_map/ppermute | solution.py:151
  193.8 32.9 %collective-permute-start.40 = (bf16[4,128,1024]{2,1,0:T(8,128)(2,1)}, bf16[4,128,1024]{2,1,0:T(8,128)(2,1)}, u32[]{:S(2)}, u32[]{:S(2)}) collective-permute-start(bf16[4,128,1024]{2,1,0:T(8,128)(2,1)} %get-tuple-element.88), channel_id=1, source_target_pairs={{0,1},{1,0},{2,3},{3,2},{4,5},{5,4},{6,7},{7,6},{8,9},{9,8},{10,11... | collective-permute-start | bytes 3145736 | tf_op jit(solution)/shard_map/ppermute | solution.py:151
  215.4 6.5 %collective-permute-start.58 = (bf16[256,256]{1,0:T(8,128)(2,1)}, bf16[256,256]{1,0:T(8,128)(2,1)S(1)}, u32[]{:S(2)}, u32[]{:S(2)}) collective-permute-start(bf16[256,256]{1,0:T(8,128)(2,1)} %get-tuple-element.113), channel_id=1, source_target_pairs={{1,4},{3,5},{5,6},{4,2},{0,3},{2,0},{6,7},{9,12},{11,13},{13,14},{... | collective-permute-start | bytes 393224 | tf_op jit(solution)/shard_map/ppermute | solution.py:936
  219.0 15.1 %collective-permute-start.55 = (bf16[288,256]{1,0:T(8,128)(2,1)}, bf16[288,256]{1,0:T(8,128)(2,1)S(1)}, u32[]{:S(2)}, u32[]{:S(2)}) collective-permute-start(bf16[288,256]{1,0:T(8,128)(2,1)} %get-tuple-element.110), channel_id=1, source_target_pairs={{1,7},{9,15},{17,23},{25,31}} | collective-permute-start | bytes 442376 | tf_op jit(solution)/shard_map/ppermute | solution.py:936
  219.7 18.6 %collective-permute-start.56 = (bf16[288,256]{1,0:T(8,128)(2,1)}, bf16[288,256]{1,0:T(8,128)(2,1)S(1)}, u32[]{:S(2)}, u32[]{:S(2)}) collective-permute-start(bf16[288,256]{1,0:T(8,128)(2,1)} %get-tuple-element.111), channel_id=1, source_target_pairs={{3,7},{11,15},{19,23},{27,31}} | collective-permute-start | bytes 442376 | tf_op jit(solution)/shard_map/ppermute | solution.py:936
  221.9 11.2 %collective-permute-start.59 = (bf16[256,256]{1,0:T(8,128)(2,1)}, bf16[256,256]{1,0:T(8,128)(2,1)S(1)}, u32[]{:S(2)}, u32[]{:S(2)}) collective-permute-start(bf16[256,256]{1,0:T(8,128)(2,1)} %get-tuple-element.114), channel_id=1, source_target_pairs={{1,0},{3,1},{5,2},{2,4},{6,3},{4,6},{9,8},{11,9},{13,10},{10,12},{... | collective-permute-start | bytes 393224 | tf_op jit(solution)/shard_map/ppermute | solution.py:936
  226.7 7.0 %collective-permute-start.60 = (bf16[256,256]{1,0:T(8,128)(2,1)}, bf16[256,256]{1,0:T(8,128)(2,1)S(1)}, u32[]{:S(2)}, u32[]{:S(2)}) collective-permute-start(bf16[256,256]{1,0:T(8,128)(2,1)} %get-tuple-element.115), channel_id=1, source_target_pairs={{7,3},{0,4},{6,2},{2,5},{4,1},{15,11},{8,12},{14,10},{10,13},{12,9... | collective-permute-start | bytes 393224 | tf_op jit(solution)/shard_map/ppermute | solution.py:936
  233.1 9.4 %collective-permute-start.57 = (bf16[288,256]{1,0:T(8,128)(2,1)}, bf16[288,256]{1,0:T(8,128)(2,1)S(1)}, u32[]{:S(2)}, u32[]{:S(2)}) collective-permute-start(bf16[288,256]{1,0:T(8,128)(2,1)} %get-tuple-element.112), channel_id=1, source_target_pairs={{5,7},{13,15},{21,23},{29,31}} | collective-permute-start | bytes 442376 | tf_op jit(solution)/shard_map/ppermute | solution.py:936
  233.8 21.7 %collective-permute-start.41 = (bf16[128,1024]{1,0:T(8,128)(2,1)}, bf16[128,1024]{1,0:T(8,128)(2,1)S(1)}, u32[]{:S(2)}, u32[]{:S(2)}) collective-permute-start(bf16[128,1024]{1,0:T(8,128)(2,1)} %get-tuple-element.90), channel_id=1, source_target_pairs={{0,2},{1,3},{2,4},{3,5},{4,6},{5,7},{6,0},{7,1},{8,10},{9,11},{10,... | collective-permute-start | bytes 786440 | tf_op jit(solution)/shard_map/ppermute | solution.py:155
  234.2 27.8 %collective-permute-start.42 = (bf16[128,1024]{1,0:T(8,128)(2,1)}, bf16[128,1024]{1,0:T(8,128)(2,1)S(1)}, u32[]{:S(2)}, u32[]{:S(2)}) collective-permute-start(bf16[128,1024]{1,0:T(8,128)(2,1)} %get-tuple-element.91), channel_id=1, source_target_pairs={{0,4},{1,5},{2,6},{3,7},{4,0},{5,1},{6,2},{7,3},{8,12},{9,13},{10,... | collective-permute-start | bytes 786440 | tf_op jit(solution)/shard_map/ppermute | solution.py:155
  238.3 23.6 %collective-permute-start.43 = (bf16[128,1024]{1,0:T(8,128)(2,1)}, bf16[128,1024]{1,0:T(8,128)(2,1)S(1)}, u32[]{:S(2)}, u32[]{:S(2)}) collective-permute-start(bf16[128,1024]{1,0:T(8,128)(2,1)} %get-tuple-element.92), channel_id=1, source_target_pairs={{0,6},{1,7},{2,0},{3,1},{4,2},{5,3},{6,4},{7,5},{8,14},{9,15},{10,... | collective-permute-start | bytes 786440 | tf_op jit(solution)/shard_map/ppermute | solution.py:155
  251.7 18.7 %collective-permute-start.37 = (bf16[192,1024]{1,0:T(8,128)(2,1)}, bf16[192,1024]{1,0:T(8,128)(2,1)S(1)}, u32[]{:S(2)}, u32[]{:S(2)}) collective-permute-start(bf16[192,1024]{1,0:T(8,128)(2,1)} %get-tuple-element.80), channel_id=1, source_target_pairs={{0,2},{1,3},{2,4},{3,5},{4,6},{5,7},{6,0},{7,1},{8,10},{9,11},{10,... | collective-permute-start | bytes 1179656 | tf_op jit(solution)/shard_map/ppermute | solution.py:155
  255.4 40.4 %collective-permute-start.38 = (bf16[192,1024]{1,0:T(8,128)(2,1)}, bf16[192,1024]{1,0:T(8,128)(2,1)}, u32[]{:S(2)}, u32[]{:S(2)}) collective-permute-start(bf16[192,1024]{1,0:T(8,128)(2,1)} %get-tuple-element.81), channel_id=1, source_target_pairs={{0,4},{1,5},{2,6},{3,7},{4,0},{5,1},{6,2},{7,3},{8,12},{9,13},{10,... | collective-permute-start | bytes 1179656 | tf_op jit(solution)/shard_map/ppermute | solution.py:155
  255.4 41.4 %collective-permute-start.39 = (bf16[192,1024]{1,0:T(8,128)(2,1)}, bf16[192,1024]{1,0:T(8,128)(2,1)}, u32[]{:S(2)}, u32[]{:S(2)}) collective-permute-start(bf16[192,1024]{1,0:T(8,128)(2,1)} %get-tuple-element.82), channel_id=1, source_target_pairs={{0,6},{1,7},{2,0},{3,1},{4,2},{5,3},{6,4},{7,5},{8,14},{9,15},{10,... | collective-permute-start | bytes 1179656 | tf_op jit(solution)/shard_map/ppermute | solution.py:155
  300.0 7.5 %collective-permute-start.64 = (bf16[2,128,256]{2,1,0:T(8,128)(2,1)S(1)}, bf16[2,128,256]{2,1,0:T(8,128)(2,1)S(1)}, u32[]{:S(2)}, u32[]{:S(2)}) collective-permute-start(bf16[2,128,256]{2,1,0:T(8,128)(2,1)S(1)} %get-tuple-element.118), channel_id=1, source_target_pairs={{0,24},{8,16},{16,8},{24,0},{1,25},{9,17},{17,9},{25,1},{2,26},{10... | collective-permute-start | bytes 393224 | tf_op jit(solution)/shard_map/ppermute | solution.py:165
  (79 other events, 1206.3 us)

commit v2 on v1

--- a/solution.py
+++ b/solution.py
@@ -44,7 +44,7 @@
 
 
 class Routes:
-    def __init__(self, seq, columns, inner, state, heads):
+    def __init__(self, seq, columns, inner, state, heads, merged=False):
         self.pair = 2 if seq % 2 == 0 else 1
         self.own = columns // seq
         self.width = inner // seq
@@ -65,8 +65,12 @@
         self.local = [p for p in pieces if p[0] == p[1]]
         remote = [p for p in pieces if p[0] != p[1]]
         common = [p for p in remote if p[4] >= 2 * width]
-        self.rounds = self.color(common) + self.color([p for p in remote if p[4] < 2 * width])
-        self.kinds = [group[0][4] >= 2 * width for group in self.rounds]
+        if merged:
+            self.rounds = self.color(remote)
+            self.kinds = [None] * len(self.rounds)
+        else:
+            self.rounds = self.color(common) + self.color([p for p in remote if p[4] < 2 * width])
+            self.kinds = [group[0][4] >= 2 * width for group in self.rounds]
         self.sizes = [ceil_to(max(p[3] for p in group), 16) for group in self.rounds]
         self.starts = [sum(self.sizes[:r]) for r in range(len(self.sizes))]
         total = sum(self.sizes)
@@ -637,16 +641,17 @@
 
 
 def place_kernel(split, kinds, table_ref, w_ref, *refs):
-    arrived, out_ref = refs[:-1], refs[-1]
+    arrived, out_refs = refs[:-2], refs[-2:]
     index = table_row(table_ref)
-    for rows, kind in ((slice(0, split), False), (slice(split, out_ref.shape[0]), True)):
+    for kind, out_ref in enumerate(out_refs):
+        rows = slice(kind * split, kind * split + out_ref.shape[0])
         start = w_ref.shape[0]
         out = dot(chosen(index[:, rows], 0, start), w_ref[...], 0, 0)
         for shared, piece in zip(kinds, arrived):
-            if shared == kind:
+            if shared is None or shared == bool(kind):
                 out = out + dot(chosen(index[:, rows], start, piece.shape[0]), piece[...], 0, 0)
             start += piece.shape[0]
-        out_ref[rows, :] = out.astype(BF)
+        out_ref[...] = out.astype(BF)
 
 
 def back_kernel(kinds, table_ref, g_ref, common_ref, pool_ref, *out_refs):
@@ -656,7 +661,9 @@
     index, start = table_row(table_ref), 0
     for shared, out_ref in zip(kinds, out_refs):
         items = index[:, start : start + out_ref.shape[0]]
-        if shared:
+        if shared is None:
+            out = dot(chosen(items, 0, pool_ref.shape[0]), pool_ref[...], 0, 0)
+        elif shared:
             out = dot(chosen(items, split, common_ref.shape[0]), common_ref[...], 0, 0)
         else:
             out = dot(chosen(items, 0, split), g_ref[:split], 0, 0)
@@ -733,7 +740,9 @@
     heads = heads_all // seq
     width = inner // seq
     chans = width + 2 * STATE
-    routes = Routes(seq, w_in.shape[1] * seq, inner, STATE, heads_all)
+    sizes = (seq, w_in.shape[1] * seq, inner, STATE, heads_all)
+    routes = Routes(*sizes)
+    homes = Routes(*sizes, merged=True)
     me = links.s
     shared = routes.shared
 
@@ -753,15 +762,14 @@
     arrived = []
     for r, group in enumerate(routes.rounds):
         arrived.append(lax.ppermute(picked[r], "seq", [(p[0], p[1]) for p in group]))
-    (mine,) = call(
+    mine, common = call(
         functools.partial(place_kernel, 2 * width, routes.kinds),
-        [((routes.rows, rows_here), BF)],
+        [((2 * width, rows_here), BF), ((shared, rows_here), BF)],
         [],
         jnp.asarray(routes.take),
         w_cols,
         *arrived,
     )
-    common = mine[2 * width :]
     if links.pair == 2:
         common = common + lax.ppermute(
             common, "seq", [(i, i - 1) for i in range(1, seq, 2)]
@@ -770,7 +778,7 @@
     head_row = jnp.where(head_row < heads, 2 * STATE + me * heads + head_row, -1)
     head_pick = one_hot(head_row, shared)
     w_mine = jnp.concatenate(
-        [mine[: 2 * width], common[: 2 * STATE], dot(head_pick, common, 1, 0).astype(BF)], axis=0
+        [mine, common[: 2 * STATE], dot(head_pick, common, 1, 0).astype(BF)], axis=0
     )
     normed = links.gather_seq(normed_half)
     w_all = links.gather_fsdp(w_mine)
@@ -924,18 +932,18 @@
         other = lax.ppermute(g_common, "seq", [(i, i + 1) for i in range(0, seq, 2)])
         g_common = (g_common.astype(F32) + other.astype(F32)).astype(BF)
     g_pool, *sent = call(
-        functools.partial(back_kernel, routes.kinds),
-        [((routes.rows, rows_here), BF)] + [((size, rows_here), BF) for size in routes.sizes],
+        functools.partial(back_kernel, homes.kinds),
+        [((homes.rows, rows_here), BF)] + [((size, rows_here), BF) for size in homes.sizes],
         [],
-        jnp.asarray(routes.back),
+        jnp.asarray(homes.back),
         g_half,
         g_common,
     )
     homed = []
-    for r, group in enumerate(routes.rounds):
+    for r, group in enumerate(homes.rounds):
         homed.append(lax.ppermute(sent[r], "seq", [(p[1], p[0]) for p in group]))
     (owned_w_in,) = call(
-        home_kernel, [(w_cols.shape, F32)], [], jnp.asarray(routes.home), g_pool, *homed
+        home_kernel, [(w_cols.shape, F32)], [], jnp.asarray(homes.home), g_pool, *homed
     )
     owned_w_in = owned_w_in.T
 

time: 309 us -> 303 us (0.981)
  the two profiles are of different devices: /device:TPU:24 before, /device:TPU:0 now
where the time goes in v2:
time: 303 us; the launch traced here: 298 us
  starting transfers between devices  111 us (37%)
  waiting for transfers between devices  84 us (28%)
  Pallas kernels  71.6 us (24%)
  other arithmetic  14.8 us (5%)
  local copies, waits for them, and re-layouts  14.7 us (5%)
    pallas_call x11, Pallas kernels, call(): pl.pallas_call(kernel, out_shape=[jax.ShapeDtypeStruct(shape, kind) for s...  71.6 us
    ppermute x21, starting transfers between devices, hop(): lax.ppermute(x, 'seq', [(i, (i + step) % self.S) for i in range(self.S)])  58.3 us
    ppermute x15, waiting for transfers between devices, across(): return lax.ppermute(x, 'fsdp', pairs)  34.7 us
    ppermute x21, waiting for transfers between devices, hop(): lax.ppermute(x, 'seq', [(i, (i + step) % self.S) for i in range(self.S)])  34.1 us
    ppermute x15, starting transfers between devices, across(): return lax.ppermute(x, 'fsdp', pairs)  19.5 us
    ppermute x7, starting transfers between devices, per_device(): lax.ppermute(picked[r], 'seq', [(p[0], p[1]) for p in group])  14.6 us
    ppermute x4, starting transfers between devices, per_device(): homed.append(lax.ppermute(sent[r], 'seq', [(p[1], p[0]) for p in group]))  12.6 us
    ppermute x7, waiting for transfers between devices, per_device(): lax.ppermute(picked[r], 'seq', [(p[0], p[1]) for p in group])  10.6 us
  transfers between devices with their start and end apart: 62, of which 20 were waited for; matrix products, arithmetic and copies ran while one was open for 6% of the time, Pallas kernels for 11%

profile of v2, /device:TPU:0, one launch (start us, length us, event | category | flops | bytes accessed | tf_op | source)
XLA Modules:
  0.0 297.9 jit_solution(11125642608143511003)
XLA Ops:
  1.8 3.0 %collective-permute-start.7 = (bf16[2,128,256]{2,1,0:T(8,128)(2,1)S(1)}, bf16[2,128,256]{2,1,0:T(8,128)(2,1)S(1)}, u32[]{:S(2)}, u32[]{:S(2)}) collective-permute-start(bf16[2,128,256]{2,1,0:T(8,128)(2,1)S(1)} %bitcast.167), channel_id=1, source_target_pairs={{0,8},{8,0},{16,24},{24,16},{1,9},{9,1},{17,25},{25,17},{2,10},{10... | collective-permute-start | bytes 393224 | tf_op jit(solution)/shard_map/ppermute | solution.py:169
  4.8 1.5 collective-permute-start.8
  6.3 3.4 %shard_map.230 = (bf16[288,256]{1,0:T(8,128)(2,1)}, bf16[288,256]{1,0:T(8,128)(2,1)}, bf16[288,256]{1,0:T(8,128)(2,1)}, bf16[256,256]{1,0:T(8,128)(2,1)}, bf16[2...) custom-call(s32[8,1856]{1,0:T(8,128)} %constant.119.clone.table_ref, bf16[548,256]{1,0:T(8,128)(2,1)} %bitcast.164), custom_call_target="tpu_custom_call" | custom-call | tf_op jit(solution)/shard_map/pallas_call | solution.py:709
  13.9 3.9 %collective-permute-start.24 = (bf16[256,256]{1,0:T(8,128)(2,1)S(1)}, bf16[256,256]{1,0:T(8,128)(2,1)S(1)}, u32[]{:S(2)}, u32[]{:S(2)}) collective-permute-start(bf16[256,256]{1,0:T(8,128)(2,1)S(1)} %copy-done.43), channel_id=1, source_target_pairs={{4,1},{5,3},{6,5},{2,4},{3,0},{0,2},{7,6},{12,9},{13,11},{14,13},{... | collective-permute-start | bytes 393224 | tf_op jit(solution)/shard_map/ppermute | solution.py:764
  19.3 6.6 %collective-permute-start.25 = (bf16[256,256]{1,0:T(8,128)(2,1)}, bf16[256,256]{1,0:T(8,128)(2,1)S(1)}, u32[]{:S(2)}, u32[]{:S(2)}) collective-permute-start(bf16[256,256]{1,0:T(8,128)(2,1)} %get-tuple-element.67), channel_id=1, source_target_pairs={{0,1},{1,3},{2,5},{4,2},{3,6},{6,4},{8,9},{9,11},{10,13},{12,10},{... | collective-permute-start | bytes 393224 | tf_op jit(solution)/shard_map/ppermute | solution.py:764
  27.3 6.1 %collective-permute-start.14 = (bf16[128,1024]{1,0:T(8,128)(2,1)S(1)}, bf16[128,1024]{1,0:T(8,128)(2,1)S(1)}, u32[]{:S(2)}, u32[]{:S(2)}) collective-permute-start(bf16[128,1024]{1,0:T(8,128)(2,1)S(1)} %fusion.3.refs_0_), channel_id=1, source_target_pairs={{0,2},{1,3},{2,4},{3,5},{4,6},{5,7},{6,0},{7,1},{8,10},{9,11},{10,... | collective-permute-start | bytes 786440 | tf_op jit(solution)/shard_map/ppermute | solution.py:159
  33.4 10.6 %collective-permute-done.26.refs_5_ = bf16[256,256]{1,0:T(8,128)(2,1)S(1)} collective-permute-done((bf16[256,256]{1,0:T(8,128)(2,1)}, bf16[256,256]{1,0:T(8,128)(2,1)S(1)}, u32[]{:S(2)}, u32[]{:S(2)}) %collective-permute-start.26) | collective-permute-done | bytes 131104 | tf_op jit(solution)/shard_map/ppermute | solution.py:764
  44.0 2.9 collective-permute-start.16
  48.2 3.1 %shard_map.231 = (bf16[512,256]{1,0:T(8,128)(2,1)}, bf16[288,256]{1,0:T(8,128)(2,1)}) custom-call(s32[8,800]{1,0:T(8,128)} %constant.120.clone.table_ref, bf16[548,256]{1,0:T(8,128)(2,1)} %bitcast.165, bf16[288,256]{1,0:T(8,128)(2,1)} %copy-done.28, bf16[288,256]{1,0:T(8,128)(2,1)} %copy-done.29, bf16[288,256]{1,0:T(8,128)(2,1)} %copy-done.30, ...), custom_call_target="tpu_custom_call" | custom-call | tf_op jit(solution)/shard_map/pallas_call | solution.py:709
  56.3 2.1 collective-permute-start.1
  58.5 5.6 %collective-permute-start.2 = (bf16[128,1024]{1,0:T(8,128)(2,1)S(1)}, bf16[128,1024]{1,0:T(8,128)(2,1)S(1)}, u32[]{:S(2)}, u32[]{:S(2)}) collective-permute-start(bf16[128,1024]{1,0:T(8,128)(2,1)S(1)} %bitcast_convert_fusion.refs_0_), channel_id=1, source_target_pairs={{0,6},{1,7},{2,0},{3,1},{4,2},{5,3},{6,4},{7,5},{8,14},{9,15},{10,... | collective-permute-start | bytes 786440 | tf_op jit(solution)/shard_map/ppermute | solution.py:159
  65.4 2.0 collective-permute-done.refs_1_
  67.4 10.7 %collective-permute-start.11 = (bf16[2,128,256]{2,1,0:T(8,128)(2,1)S(1)}, bf16[2,128,256]{2,1,0:T(8,128)(2,1)S(1)}, u32[]{:S(2)}, u32[]{:S(2)}) collective-permute-start(bf16[2,128,256]{2,1,0:T(8,128)(2,1)S(1)} %get-tuple-element.122), channel_id=1, source_target_pairs={{0,2},{1,3},{2,4},{3,5},{4,6},{5,7},{6,0},{7,1},{8,10},{9,11},{10,... | collective-permute-start | bytes 393224 | tf_op jit(solution)/shard_map/ppermute | solution.py:159
  78.9 1.5 collective-permute-start.29
  81.2 1.5 collective-permute-start.30
  84.8 6.3 %collective-permute-done.29.refs_9_.refs_1_ = bf16[784,256]{1,0:T(8,128)(2,1)S(1)} collective-permute-done((bf16[784,256]{1,0:T(8,128)(2,1)S(1)}, bf16[784,256]{1,0:T(8,128)(2,1)S(1)}, u32[]{:S(2)}, u32[]{:S(2)}) %collective-permute-start.29) | collective-permute-done | bytes 401440 | tf_op jit(solution)/shard_map/ppermute | solution.py:169
  91.8 9.6 %collective-permute-done.30.refs_10_.refs_2_ = bf16[784,256]{1,0:T(8,128)(2,1)S(1)} collective-permute-done((bf16[784,256]{1,0:T(8,128)(2,1)S(1)}, bf16[784,256]{1,0:T(8,128)(2,1)S(1)}, u32[]{:S(2)}, u32[]{:S(2)}) %collective-permute-start.30) | collective-permute-done | bytes 401440 | tf_op jit(solution)/shard_map/ppermute | solution.py:169
  101.4 4.7 %collective-permute-start.12 = (bf16[2,128,256]{2,1,0:T(8,128)(2,1)}, bf16[2,128,256]{2,1,0:T(8,128)(2,1)}, u32[]{:S(2)}, u32[]{:S(2)}) collective-permute-start(bf16[2,128,256]{2,1,0:T(8,128)(2,1)} %get-tuple-element.123), channel_id=1, source_target_pairs={{0,4},{1,5},{2,6},{3,7},{4,0},{5,1},{6,2},{7,3},{8,12},{9,13},{10,... | collective-permute-start | bytes 393224 | tf_op jit(solution)/shard_map/ppermute | solution.py:159
  106.2 3.4 %collective-permute-start.13 = (bf16[2,128,256]{2,1,0:T(8,128)(2,1)}, bf16[2,128,256]{2,1,0:T(8,128)(2,1)}, u32[]{:S(2)}, u32[]{:S(2)}) collective-permute-start(bf16[2,128,256]{2,1,0:T(8,128)(2,1)} %get-tuple-element.120), channel_id=1, source_target_pairs={{0,6},{1,7},{2,0},{3,1},{4,2},{5,3},{6,4},{7,5},{8,14},{9,15},{10,... | collective-permute-start | bytes 393224 | tf_op jit(solution)/shard_map/ppermute | solution.py:159
  112.1 14.3 %shard_map.232 = (bf16[1024,1024]{1,0:T(8,128)(2,1)}, bf16[1024,784]{1,0:T(8,128)(2,1)}, bf16[1024,256]{1,0:T(8,128)(2,1)}, f32[1024,256]{1,0:T(8,128)}, f32[8,128,256]{2,1,0:T(8,128)}) custom-call(bf16[128,1024]{1,0:T(8,128)(2,1)} %copy-done.10, bf16[128,1024]{1,0:T(8,128)(2,1)} %copy-done.18, bf16[128,1024]{1,0:T(8,128)(2,1)} %copy-done.19, ...), custom_call_target="tpu_custom_call" | custom-call | tf_op jit(solution)/shard_map/pallas_call | solution.py:709
  126.5 6.0 %shard_map.233 = (bf16[1024,1024]{1,0:T(8,128)(2,1)}, bf16[1024,256]{1,0:T(8,128)(2,1)}, f32[1024,256]{1,0:T(8,128)}, f32[2,1024]{1,0:T(2,128)}) custom-call(bf16[128,1024]{1,0:T(8,128)(2,1)} %copy-done.13, bf16[128,1024]{1,0:T(8,128)(2,1)} %copy-done.24, bf16[128,1024]{1,0:T(8,128)(2,1)} %copy-done.25, bf16[128,1024]{1,0:T(8,128)(2,1)} %copy-done.26, ...), custom_call_target="tpu_custom_call" | custom-call | tf_op jit(solution)/shard_map/pallas_call | solution.py:709
  136.4 2.9 collective-permute-start.35
  141.3 7.8 %shard_map.234 = (bf16[4,160,1024]{2,1,0:T(8,128)(2,1)}, bf16[4,160,1024]{2,1,0:T(8,128)(2,1)}, bf16[1024,256]{1,0:T(8,128)(2,1)}, bf16[1024,256]{1,0:T(8,128)(2,1)}, f32[1,256]{1,0:T(1,128)}) custom-call(bf16[1024,1024]{1,0:T(8,128)(2,1)} %get-tuple-element.74.cot_ref, bf16[1024,256]{1,0:T(8,128)(2,1)} %get-tuple-element.75.wo_ref, ...), custom_call_target="tpu_custom_call" | custom-call | tf_op jit(solution)/shard_map/pallas_call | solution.py:709
  149.0 19.3 %shard_map.236 = (bf16[4,128,1024]{2,1,0:T(8,128)(2,1)}, bf16[4,128,1024]{2,1,0:T(8,128)(2,1)}, bf16[1024,784]{1,0:T(8,128)(2,1)}, f32[4,512]{1,0:T(4,128)}, f32[1,512]{1,0:T(1,128)}, /*index=5*/f32[8,128]{1,0:T(8,128)}) custom-call(bf16[1024,784]{1,0:T(8,128)(2,1)} %get-tuple-element.73.refs_13_.proj_ref, f32[1024,256]{1,0:T(8,128)} %get-tuple-element.84.core_ref, ...), custom_call_target="tpu_custom_call" | custom-call | tf_op jit(solution)/shard_map/pallas_call | solution.py:709
  168.3 5.7 %shard_map.238 = (bf16[784,256]{1,0:T(8,128)(2,1)}, bf16[784,256]{1,0:T(8,128)(2,1)}, bf16[784,256]{1,0:T(8,128)(2,1)}, bf16[784,256]{1,0:T(8,128)(2,1)}, f32[1,...) custom-call(bf16[1024,784]{1,0:T(8,128)(2,1)} %get-tuple-element.94.dproj_ref, ...), custom_call_target="tpu_custom_call" | custom-call | tf_op jit(solution)/shard_map/pallas_call | solution.py:709
  177.1 1.9 collective-permute-start.45
  179.0 2.8 collective-permute-start.46
  181.8 2.7 collective-permute-done.45
  184.5 2.8 collective-permute-done.46
  188.4 1.5 collective-permute-start.49
  191.9 1.5 collective-permute-start.52
  196.9 6.8 %collective-permute-done.51 = bf16[784,256]{1,0:T(8,128)(2,1)S(1)} collective-permute-done((bf16[784,256]{1,0:T(8,128)(2,1)}, bf16[784,256]{1,0:T(8,128)(2,1)S(1)}, u32[]{:S(2)}, u32[]{:S(2)}) %collective-permute-start.51) | collective-permute-done | bytes 401440 | tf_op jit(solution)/shard_map/ppermute | solution.py:169
  203.7 7.0 %collective-permute-done.52 = bf16[784,256]{1,0:T(8,128)(2,1)S(1)} collective-permute-done((bf16[784,256]{1,0:T(8,128)(2,1)}, bf16[784,256]{1,0:T(8,128)(2,1)S(1)}, u32[]{:S(2)}, u32[]{:S(2)}) %collective-permute-start.52) | collective-permute-done | bytes 401440 | tf_op jit(solution)/shard_map/ppermute | solution.py:169
  215.5 3.3 %shard_map.239 = (bf16[800,256]{1,0:T(8,128)(2,1)}, bf16[288,256]{1,0:T(8,128)(2,1)}, bf16[288,256]{1,0:T(8,128)(2,1)}, bf16[288,256]{1,0:T(8,128)(2,1)}, bf16[224,256]{1,0:T(8,128)(2,1)}) custom-call(s32[8,1088]{1,0:T(8,128)} %constant.121.clone.table_ref, bf16[784,256]{1,0:T(8,128)(2,1)} %copy-done.6, bf16[288,256]{1,0:T(8,128)(2,1)} %add_convert_fusion.1.common_ref), custom_call_target="tpu_custom_call" | custom-call | tf_op jit(solution)/shard_map/pallas_call | solution.py:709
  218.8 3.9 %collective-permute-start.55 = (bf16[288,256]{1,0:T(8,128)(2,1)}, bf16[288,256]{1,0:T(8,128)(2,1)S(1)}, u32[]{:S(2)}, u32[]{:S(2)}) collective-permute-start(bf16[288,256]{1,0:T(8,128)(2,1)} %get-tuple-element.111), channel_id=1, source_target_pairs={{1,7},{3,5},{5,6},{0,3},{6,2},{4,1},{2,0},{9,15},{11,13},{13,14},{... | collective-permute-start | bytes 442376 | tf_op jit(solution)/shard_map/ppermute | solution.py:944
  224.7 7.3 %collective-permute-start.57 = (bf16[288,256]{1,0:T(8,128)(2,1)}, bf16[288,256]{1,0:T(8,128)(2,1)S(1)}, u32[]{:S(2)}, u32[]{:S(2)}) collective-permute-start(bf16[288,256]{1,0:T(8,128)(2,1)} %get-tuple-element.113), channel_id=1, source_target_pairs={{5,7},{1,0},{3,1},{7,3},{4,2},{0,4},{2,5},{13,15},{9,8},{11,9},{15... | collective-permute-start | bytes 442376 | tf_op jit(solution)/shard_map/ppermute | solution.py:944
  232.1 2.7 shard_map.237
  235.4 1.5 collective-permute-start.42
  236.9 2.8 collective-permute-start.43
  243.4 3.0 %shard_map.240 = f32[548,256]{1,0:T(8,128)} custom-call(s32[8,1888]{1,0:T(8,128)} %constant.122.clone.table_ref, bf16[800,256]{1,0:T(8,128)(2,1)} %get-tuple-element.110.refs_0_, bf16[288,256]{1,0:T(8,128)(2,1)} %copy-done.31, bf16[288,256]{1,0:T(8,128)(2,1)} %copy-done.32, bf16[288,256]{1,0:T(8,128)(2,1)} %copy-done.33, bf16[224,256]{1,0:T(8,128)(2,1)} %copy-done.39), custom_call_target="tpu_custom_call" | custom-call | tf_op jit(solution)/shard_map/pallas_call | solution.py:709
  247.6 3.0 %shard_map.235 = (f32[192,1024]{1,0:T(8,128)}, bf16[192,1024]{1,0:T(8,128)(2,1)}, bf16[192,1024]{1,0:T(8,128)(2,1)}, bf16[192,1024]{1,0:T(8,128)(2,1)}) custom-call(bf16[4,160,1024]{2,1,0:T(8,128)(2,1)} %get-tuple-element.78.keep_ref, bf16[4,160,1024]{2,1,0:T(8,128)(2,1)} %copy-done.9), custom_call_target="tpu_custom_call" | custom-call | tf_op jit(solution)/shard_map/pallas_call | solution.py:709
  251.7 5.9 %collective-permute-start.37 = (bf16[192,1024]{1,0:T(8,128)(2,1)}, bf16[192,1024]{1,0:T(8,128)(2,1)S(1)}, u32[]{:S(2)}, u32[]{:S(2)}) collective-permute-start(bf16[192,1024]{1,0:T(8,128)(2,1)} %get-tuple-element.81), channel_id=1, source_target_pairs={{0,2},{1,3},{2,4},{3,5},{4,6},{5,7},{6,0},{7,1},{8,10},{9,11},{10,... | collective-permute-start | bytes 1179656 | tf_op jit(solution)/shard_map/ppermute | solution.py:159
  257.6 2.4 collective-permute-start.39
  260.1 10.5 %collective-permute-done.42 = bf16[128,1024]{1,0:T(8,128)(2,1)S(1)} collective-permute-done((bf16[128,1024]{1,0:T(8,128)(2,1)}, bf16[128,1024]{1,0:T(8,128)(2,1)S(1)}, u32[]{:S(2)}, u32[]{:S(2)}) %collective-permute-start.42) | collective-permute-done | bytes 262176 | tf_op jit(solution)/shard_map/ppermute | solution.py:159
  272.1 14.4 %collective-permute-done.38 = bf16[192,1024]{1,0:T(8,128)(2,1)} collective-permute-done((bf16[192,1024]{1,0:T(8,128)(2,1)}, bf16[192,1024]{1,0:T(8,128)(2,1)}, u32[]{:S(2)}, u32[]{:S(2)}) %collective-permute-start.38) | collective-permute-done | bytes 393248 | tf_op jit(solution)/shard_map/ppermute | solution.py:159
  289.5 1.6 collective-permute-start.60
  292.3 2.3 fusion
  294.7 2.4 collective-permute-done.61
  (266 shorter events, 57.3 us)
Async XLA Ops:
  1.8 12.1 %collective-permute-start.7 = (bf16[2,128,256]{2,1,0:T(8,128)(2,1)S(1)}, bf16[2,128,256]{2,1,0:T(8,128)(2,1)S(1)}, u32[]{:S(2)}, u32[]{:S(2)}) collective-permute-start(bf16[2,128,256]{2,1,0:T(8,128)(2,1)S(1)} %bitcast.167), channel_id=1, source_target_pairs={{0,8},{8,0},{16,24},{24,16},{1,9},{9,1},{17,25},{25,17},{2,10},{10... | collective-permute-start | bytes 393224 | tf_op jit(solution)/shard_map/ppermute | solution.py:169
  4.8 13.1 %collective-permute-start.8 = (bf16[2,128,256]{2,1,0:T(8,128)(2,1)S(1)}, bf16[2,128,256]{2,1,0:T(8,128)(2,1)S(1)}, u32[]{:S(2)}, u32[]{:S(2)}) collective-permute-start(bf16[2,128,256]{2,1,0:T(8,128)(2,1)S(1)} %bitcast.168), channel_id=1, source_target_pairs={{0,16},{8,24},{16,0},{24,8},{1,17},{9,25},{17,1},{25,9},{2,18},{10... | collective-permute-start | bytes 393224 | tf_op jit(solution)/shard_map/ppermute | solution.py:169
  6.3 13.0 %collective-permute-start.9 = (bf16[2,128,256]{2,1,0:T(8,128)(2,1)S(1)}, bf16[2,128,256]{2,1,0:T(8,128)(2,1)S(1)}, u32[]{:S(2)}, u32[]{:S(2)}) collective-permute-start(bf16[2,128,256]{2,1,0:T(8,128)(2,1)S(1)} %bitcast.169), channel_id=1, source_target_pairs={{0,24},{8,16},{16,8},{24,0},{1,25},{9,17},{17,9},{25,1},{2,26},{10... | collective-permute-start | bytes 393224 | tf_op jit(solution)/shard_map/ppermute | solution.py:169
  9.8 34.2 %collective-permute-start.21 = (bf16[288,256]{1,0:T(8,128)(2,1)}, bf16[288,256]{1,0:T(8,128)(2,1)S(1)}, u32[]{:S(2)}, u32[]{:S(2)}) collective-permute-start(bf16[288,256]{1,0:T(8,128)(2,1)} %get-tuple-element.63), channel_id=1, source_target_pairs={{7,1},{15,9},{23,17},{31,25}} | collective-permute-start | bytes 442376 | tf_op jit(solution)/shard_map/ppermute | solution.py:764
  10.6 36.3 %collective-permute-start.22 = (bf16[288,256]{1,0:T(8,128)(2,1)}, bf16[288,256]{1,0:T(8,128)(2,1)S(1)}, u32[]{:S(2)}, u32[]{:S(2)}) collective-permute-start(bf16[288,256]{1,0:T(8,128)(2,1)} %get-tuple-element.64), channel_id=1, source_target_pairs={{7,3},{15,11},{23,19},{31,27}} | collective-permute-start | bytes 442376 | tf_op jit(solution)/shard_map/ppermute | solution.py:764
  13.9 12.0 %collective-permute-start.24 = (bf16[256,256]{1,0:T(8,128)(2,1)S(1)}, bf16[256,256]{1,0:T(8,128)(2,1)S(1)}, u32[]{:S(2)}, u32[]{:S(2)}) collective-permute-start(bf16[256,256]{1,0:T(8,128)(2,1)S(1)} %copy-done.43), channel_id=1, source_target_pairs={{4,1},{5,3},{6,5},{2,4},{3,0},{0,2},{7,6},{12,9},{13,11},{14,13},{... | collective-permute-start | bytes 393224 | tf_op jit(solution)/shard_map/ppermute | solution.py:764
  18.6 28.3 %collective-permute-start.23 = (bf16[288,256]{1,0:T(8,128)(2,1)}, bf16[288,256]{1,0:T(8,128)(2,1)S(1)}, u32[]{:S(2)}, u32[]{:S(2)}) collective-permute-start(bf16[288,256]{1,0:T(8,128)(2,1)} %get-tuple-element.65), channel_id=1, source_target_pairs={{7,5},{15,13},{23,21},{31,29}} | collective-permute-start | bytes 442376 | tf_op jit(solution)/shard_map/ppermute | solution.py:764
  19.3 8.0 %collective-permute-start.25 = (bf16[256,256]{1,0:T(8,128)(2,1)}, bf16[256,256]{1,0:T(8,128)(2,1)S(1)}, u32[]{:S(2)}, u32[]{:S(2)}) collective-permute-start(bf16[256,256]{1,0:T(8,128)(2,1)} %get-tuple-element.67), channel_id=1, source_target_pairs={{0,1},{1,3},{2,5},{4,2},{3,6},{6,4},{8,9},{9,11},{10,13},{12,10},{... | collective-permute-start | bytes 393224 | tf_op jit(solution)/shard_map/ppermute | solution.py:764
  25.9 18.1 %collective-permute-start.26 = (bf16[256,256]{1,0:T(8,128)(2,1)}, bf16[256,256]{1,0:T(8,128)(2,1)S(1)}, u32[]{:S(2)}, u32[]{:S(2)}) collective-permute-start(bf16[256,256]{1,0:T(8,128)(2,1)} %get-tuple-element.68), channel_id=1, source_target_pairs={{3,7},{4,0},{2,6},{5,2},{1,4},{11,15},{12,8},{10,14},{13,10},{9,12... | collective-permute-start | bytes 393224 | tf_op jit(solution)/shard_map/ppermute | solution.py:764
  27.3 29.0 %collective-permute-start.14 = (bf16[128,1024]{1,0:T(8,128)(2,1)S(1)}, bf16[128,1024]{1,0:T(8,128)(2,1)S(1)}, u32[]{:S(2)}, u32[]{:S(2)}) collective-permute-start(bf16[128,1024]{1,0:T(8,128)(2,1)S(1)} %fusion.3.refs_0_), channel_id=1, source_target_pairs={{0,2},{1,3},{2,4},{3,5},{4,6},{5,7},{6,0},{7,1},{8,10},{9,11},{10,... | collective-permute-start | bytes 786440 | tf_op jit(solution)/shard_map/ppermute | solution.py:159
  44.0 14.5 %collective-permute-start.15 = (bf16[128,1024]{1,0:T(8,128)(2,1)S(1)}, bf16[128,1024]{1,0:T(8,128)(2,1)S(1)}, u32[]{:S(2)}, u32[]{:S(2)}) collective-permute-start(bf16[128,1024]{1,0:T(8,128)(2,1)S(1)} %fusion.3.refs_0_), channel_id=1, source_target_pairs={{0,4},{1,5},{2,6},{3,7},{4,0},{5,1},{6,2},{7,3},{8,12},{9,13},{10,... | collective-permute-start | bytes 786440 | tf_op jit(solution)/shard_map/ppermute | solution.py:159
  44.0 20.0 %collective-permute-start.16 = (bf16[128,1024]{1,0:T(8,128)(2,1)S(1)}, bf16[128,1024]{1,0:T(8,128)(2,1)S(1)}, u32[]{:S(2)}, u32[]{:S(2)}) collective-permute-start(bf16[128,1024]{1,0:T(8,128)(2,1)S(1)} %fusion.3.refs_0_), channel_id=1, source_target_pairs={{0,6},{1,7},{2,0},{3,1},{4,2},{5,3},{6,4},{7,5},{8,14},{9,15},{10,... | collective-permute-start | bytes 786440 | tf_op jit(solution)/shard_map/ppermute | solution.py:159
  54.9 9.2 %collective-permute-start.17 = (bf16[128,1024]{1,0:T(8,128)(2,1)S(1)}, bf16[128,1024]{1,0:T(8,128)(2,1)S(1)}, u32[]{:S(2)}, u32[]{:S(2)}) collective-permute-start(bf16[128,1024]{1,0:T(8,128)(2,1)S(1)} %fusion.3.refs_0_), channel_id=1, source_target_pairs={{0,1},{1,0},{2,3},{3,2},{4,5},{5,4},{6,7},{7,6},{8,9},{9,8},{10,11... | collective-permute-start | bytes 786440 | tf_op jit(solution)/shard_map/ppermute | solution.py:155
  56.3 11.2 %collective-permute-start = (bf16[128,1024]{1,0:T(8,128)(2,1)S(1)}, bf16[128,1024]{1,0:T(8,128)(2,1)S(1)}, u32[]{:S(2)}, u32[]{:S(2)}) collective-permute-start(bf16[128,1024]{1,0:T(8,128)(2,1)S(1)} %bitcast_convert_fusion.refs_0_), channel_id=1, source_target_pairs={{0,2},{1,3},{2,4},{3,5},{4,6},{5,7},{6,0},{7,1},{8,10},{9,11},{10,... | collective-permute-start | bytes 786440 | tf_op jit(solution)/shard_map/ppermute | solution.py:159
  56.3 21.8 %collective-permute-start.1 = (bf16[128,1024]{1,0:T(8,128)(2,1)S(1)}, bf16[128,1024]{1,0:T(8,128)(2,1)S(1)}, u32[]{:S(2)}, u32[]{:S(2)}) collective-permute-start(bf16[128,1024]{1,0:T(8,128)(2,1)S(1)} %bitcast_convert_fusion.refs_0_), channel_id=1, source_target_pairs={{0,4},{1,5},{2,6},{3,7},{4,0},{5,1},{6,2},{7,3},{8,12},{9,13},{10,... | collective-permute-start | bytes 786440 | tf_op jit(solution)/shard_map/ppermute | solution.py:159
  58.5 21.9 %collective-permute-start.2 = (bf16[128,1024]{1,0:T(8,128)(2,1)S(1)}, bf16[128,1024]{1,0:T(8,128)(2,1)S(1)}, u32[]{:S(2)}, u32[]{:S(2)}) collective-permute-start(bf16[128,1024]{1,0:T(8,128)(2,1)S(1)} %bitcast_convert_fusion.refs_0_), channel_id=1, source_target_pairs={{0,6},{1,7},{2,0},{3,1},{4,2},{5,3},{6,4},{7,5},{8,14},{9,15},{10,... | collective-permute-start | bytes 786440 | tf_op jit(solution)/shard_map/ppermute | solution.py:159
  64.1 16.3 %collective-permute-start.3 = (bf16[128,1024]{1,0:T(8,128)(2,1)S(1)}, bf16[128,1024]{1,0:T(8,128)(2,1)S(1)}, u32[]{:S(2)}, u32[]{:S(2)}) collective-permute-start(bf16[128,1024]{1,0:T(8,128)(2,1)S(1)} %bitcast_convert_fusion.refs_0_), channel_id=1, source_target_pairs={{0,1},{1,0},{2,3},{3,2},{4,5},{5,4},{6,7},{7,6},{8,9},{9,8},{10,11... | collective-permute-start | bytes 786440 | tf_op jit(solution)/shard_map/ppermute | solution.py:155
  64.2 18.5 %collective-permute-start.18 = (bf16[128,1024]{1,0:T(8,128)(2,1)S(1)}, bf16[128,1024]{1,0:T(8,128)(2,1)}, u32[]{:S(2)}, u32[]{:S(2)}) collective-permute-start(bf16[128,1024]{1,0:T(8,128)(2,1)S(1)} %collective-permute-done.14.refs_1_), channel_id=1, source_target_pairs={{0,1},{1,0},{2,3},{3,2},{4,5},{5,4},{6,7},{7,6},{8,9},{9,8},{10,11... | collective-permute-start | bytes 786440 | tf_op jit(solution)/shard_map/ppermute | solution.py:155
  67.4 13.7 %collective-permute-start.11 = (bf16[2,128,256]{2,1,0:T(8,128)(2,1)S(1)}, bf16[2,128,256]{2,1,0:T(8,128)(2,1)S(1)}, u32[]{:S(2)}, u32[]{:S(2)}) collective-permute-start(bf16[2,128,256]{2,1,0:T(8,128)(2,1)S(1)} %get-tuple-element.122), channel_id=1, source_target_pairs={{0,2},{1,3},{2,4},{3,5},{4,6},{5,7},{6,0},{7,1},{8,10},{9,11},{10,... | collective-permute-start | bytes 393224 | tf_op jit(solution)/shard_map/ppermute | solution.py:159
  78.9 12.2 %collective-permute-start.29 = (bf16[784,256]{1,0:T(8,128)(2,1)S(1)}, bf16[784,256]{1,0:T(8,128)(2,1)S(1)}, u32[]{:S(2)}, u32[]{:S(2)}) collective-permute-start(bf16[784,256]{1,0:T(8,128)(2,1)S(1)} %pad_maximum_fusion.refs_8_.refs_0_), channel_id=1, source_target_pairs={{0,8},{8,0},{16,24},{24,16},{1,9},{9,1},{17,25},{25,17},{2,10},{10... | collective-permute-start | bytes 1204232 | tf_op jit(solution)/shard_map/ppermute | solution.py:169
  81.2 20.2 %collective-permute-start.30 = (bf16[784,256]{1,0:T(8,128)(2,1)S(1)}, bf16[784,256]{1,0:T(8,128)(2,1)S(1)}, u32[]{:S(2)}, u32[]{:S(2)}) collective-permute-start(bf16[784,256]{1,0:T(8,128)(2,1)S(1)} %pad_maximum_fusion.refs_8_.refs_0_), channel_id=1, source_target_pairs={{0,16},{8,24},{16,0},{24,8},{1,17},{9,25},{17,1},{25,9},{2,18},{10... | collective-permute-start | bytes 1204232 | tf_op jit(solution)/shard_map/ppermute | solution.py:169
  82.7 23.5 %collective-permute-start.31 = (bf16[784,256]{1,0:T(8,128)(2,1)S(1)}, bf16[784,256]{1,0:T(8,128)(2,1)S(1)}, u32[]{:S(2)}, u32[]{:S(2)}) collective-permute-start(bf16[784,256]{1,0:T(8,128)(2,1)S(1)} %pad_maximum_fusion.refs_8_.refs_0_), channel_id=1, source_target_pairs={{0,24},{8,16},{16,8},{24,0},{1,25},{9,17},{17,9},{25,1},{2,26},{10... | collective-permute-start | bytes 1204232 | tf_op jit(solution)/shard_map/ppermute | solution.py:169
  84.2 42.2 %collective-permute-start.4 = (bf16[128,1024]{1,0:T(8,128)(2,1)}, bf16[128,1024]{1,0:T(8,128)(2,1)}, u32[]{:S(2)}, u32[]{:S(2)}) collective-permute-start(bf16[128,1024]{1,0:T(8,128)(2,1)} %copy-done.24), channel_id=1, source_target_pairs={{0,1},{1,0},{2,3},{3,2},{4,5},{5,4},{6,7},{7,6},{8,9},{9,8},{10,11... | collective-permute-start | bytes 786440 | tf_op jit(solution)/shard_map/ppermute | solution.py:155
  84.3 42.1 %collective-permute-start.5 = (bf16[128,1024]{1,0:T(8,128)(2,1)}, bf16[128,1024]{1,0:T(8,128)(2,1)}, u32[]{:S(2)}, u32[]{:S(2)}) collective-permute-start(bf16[128,1024]{1,0:T(8,128)(2,1)} %copy-done.25), channel_id=1, source_target_pairs={{0,1},{1,0},{2,3},{3,2},{4,5},{5,4},{6,7},{7,6},{8,9},{9,8},{10,11... | collective-permute-start | bytes 786440 | tf_op jit(solution)/shard_map/ppermute | solution.py:155
  91.1 35.4 %collective-permute-start.6 = (bf16[128,1024]{1,0:T(8,128)(2,1)}, bf16[128,1024]{1,0:T(8,128)(2,1)}, u32[]{:S(2)}, u32[]{:S(2)}) collective-permute-start(bf16[128,1024]{1,0:T(8,128)(2,1)} %copy-done.26), channel_id=1, source_target_pairs={{0,1},{1,0},{2,3},{3,2},{4,5},{5,4},{6,7},{7,6},{8,9},{9,8},{10,11... | collective-permute-start | bytes 786440 | tf_op jit(solution)/shard_map/ppermute | solution.py:155
  101.4 25.0 %collective-permute-start.12 = (bf16[2,128,256]{2,1,0:T(8,128)(2,1)}, bf16[2,128,256]{2,1,0:T(8,128)(2,1)}, u32[]{:S(2)}, u32[]{:S(2)}) collective-permute-start(bf16[2,128,256]{2,1,0:T(8,128)(2,1)} %get-tuple-element.123), channel_id=1, source_target_pairs={{0,4},{1,5},{2,6},{3,7},{4,0},{5,1},{6,2},{7,3},{8,12},{9,13},{10,... | collective-permute-start | bytes 393224 | tf_op jit(solution)/shard_map/ppermute | solution.py:159
  106.2 20.2 %collective-permute-start.13 = (bf16[2,128,256]{2,1,0:T(8,128)(2,1)}, bf16[2,128,256]{2,1,0:T(8,128)(2,1)}, u32[]{:S(2)}, u32[]{:S(2)}) collective-permute-start(bf16[2,128,256]{2,1,0:T(8,128)(2,1)} %get-tuple-element.120), channel_id=1, source_target_pairs={{0,6},{1,7},{2,0},{3,1},{4,2},{5,3},{6,4},{7,5},{8,14},{9,15},{10,... | collective-permute-start | bytes 393224 | tf_op jit(solution)/shard_map/ppermute | solution.py:159
  177.1 7.4 %collective-permute-start.45 = (f32[152,128]{1,0:T(8,128)S(1)}, f32[152,128]{1,0:T(8,128)S(1)}, u32[]{:S(2)}, u32[]{:S(2)}) collective-permute-start(f32[152,128]{1,0:T(8,128)S(1)} %fusion.31), channel_id=1, source_target_pairs={{0,2},{1,3},{2,4},{3,5},{4,6},{5,7},{6,0},{7,1},{8,10},{9,11},{10,... | collective-permute-start | bytes 233480 | tf_op jit(solution)/shard_map/ppermute | solution.py:159
  179.0 8.3 %collective-permute-start.46 = (f32[152,128]{1,0:T(8,128)S(1)}, f32[152,128]{1,0:T(8,128)S(1)}, u32[]{:S(2)}, u32[]{:S(2)}) collective-permute-start(f32[152,128]{1,0:T(8,128)S(1)} %fusion.31), channel_id=1, source_target_pairs={{0,4},{1,5},{2,6},{3,7},{4,0},{5,1},{6,2},{7,3},{8,12},{9,13},{10,... | collective-permute-start | bytes 233480 | tf_op jit(solution)/shard_map/ppermute | solution.py:159
  181.8 5.9 %collective-permute-start.47 = (f32[152,128]{1,0:T(8,128)S(1)}, f32[152,128]{1,0:T(8,128)S(1)}, u32[]{:S(2)}, u32[]{:S(2)}) collective-permute-start(f32[152,128]{1,0:T(8,128)S(1)} %fusion.31), channel_id=1, source_target_pairs={{0,6},{1,7},{2,0},{3,1},{4,2},{5,3},{6,4},{7,5},{8,14},{9,15},{10,... | collective-permute-start | bytes 233480 | tf_op jit(solution)/shard_map/ppermute | solution.py:159
  188.4 6.3 %collective-permute-start.49 = (f32[152,128]{1,0:T(8,128)S(1)}, f32[152,128]{1,0:T(8,128)S(1)}, u32[]{:S(2)}, u32[]{:S(2)}) collective-permute-start(f32[152,128]{1,0:T(8,128)S(1)} %add_add_fusion.1), channel_id=1, source_target_pairs={{0,16},{8,24},{16,0},{24,8},{1,17},{9,25},{17,1},{25,9},{2,18},{10... | collective-permute-start | bytes 233480 | tf_op jit(solution)/shard_map/ppermute | solution.py:169
  189.9 6.1 %collective-permute-start.50 = (f32[152,128]{1,0:T(8,128)S(1)}, f32[152,128]{1,0:T(8,128)S(1)}, u32[]{:S(2)}, u32[]{:S(2)}) collective-permute-start(f32[152,128]{1,0:T(8,128)S(1)} %add_add_fusion.1), channel_id=1, source_target_pairs={{0,24},{8,16},{16,8},{24,0},{1,25},{9,17},{17,9},{25,1},{2,26},{10... | collective-permute-start | bytes 233480 | tf_op jit(solution)/shard_map/ppermute | solution.py:169
  191.2 12.5 %collective-permute-start.51 = (bf16[784,256]{1,0:T(8,128)(2,1)}, bf16[784,256]{1,0:T(8,128)(2,1)S(1)}, u32[]{:S(2)}, u32[]{:S(2)}) collective-permute-start(bf16[784,256]{1,0:T(8,128)(2,1)} %get-tuple-element.104), channel_id=1, source_target_pairs={{0,8},{8,0},{16,24},{24,16},{1,9},{9,1},{17,25},{25,17},{2,10},{10... | collective-permute-start | bytes 1204232 | tf_op jit(solution)/shard_map/ppermute | solution.py:169
  191.9 18.8 %collective-permute-start.52 = (bf16[784,256]{1,0:T(8,128)(2,1)}, bf16[784,256]{1,0:T(8,128)(2,1)S(1)}, u32[]{:S(2)}, u32[]{:S(2)}) collective-permute-start(bf16[784,256]{1,0:T(8,128)(2,1)} %get-tuple-element.105), channel_id=1, source_target_pairs={{0,16},{8,24},{16,0},{24,8},{1,17},{9,25},{17,1},{25,9},{2,18},{10... | collective-permute-start | bytes 1204232 | tf_op jit(solution)/shard_map/ppermute | solution.py:169
  193.4 18.5 %collective-permute-start.53 = (bf16[784,256]{1,0:T(8,128)(2,1)}, bf16[784,256]{1,0:T(8,128)(2,1)S(1)}, u32[]{:S(2)}, u32[]{:S(2)}) collective-permute-start(bf16[784,256]{1,0:T(8,128)(2,1)} %get-tuple-element.106), channel_id=1, source_target_pairs={{0,24},{8,16},{16,8},{24,0},{1,25},{9,17},{17,9},{25,1},{2,26},{10... | collective-permute-start | bytes 1204232 | tf_op jit(solution)/shard_map/ppermute | solution.py:169
  194.7 51.7 %collective-permute-start.36 = (bf16[4,160,1024]{2,1,0:T(8,128)(2,1)}, bf16[4,160,1024]{2,1,0:T(8,128)(2,1)S(1)}, u32[]{:S(2)}, u32[]{:S(2)}) collective-permute-start(bf16[4,160,1024]{2,1,0:T(8,128)(2,1)} %get-tuple-element.79), channel_id=1, source_target_pairs={{0,1},{1,0},{2,3},{3,2},{4,5},{5,4},{6,7},{7,6},{8,9},{9,8},{10,11... | collective-permute-start | bytes 3932168 | tf_op jit(solution)/shard_map/ppermute | solution.py:155
  196.1 28.7 %collective-permute-start.40 = (bf16[4,128,1024]{2,1,0:T(8,128)(2,1)}, bf16[4,128,1024]{2,1,0:T(8,128)(2,1)}, u32[]{:S(2)}, u32[]{:S(2)}) collective-permute-start(bf16[4,128,1024]{2,1,0:T(8,128)(2,1)} %get-tuple-element.89), channel_id=1, source_target_pairs={{0,1},{1,0},{2,3},{3,2},{4,5},{5,4},{6,7},{7,6},{8,9},{9,8},{10,11... | collective-permute-start | bytes 3145736 | tf_op jit(solution)/shard_map/ppermute | solution.py:155
  218.8 16.5 %collective-permute-start.55 = (bf16[288,256]{1,0:T(8,128)(2,1)}, bf16[288,256]{1,0:T(8,128)(2,1)S(1)}, u32[]{:S(2)}, u32[]{:S(2)}) collective-permute-start(bf16[288,256]{1,0:T(8,128)(2,1)} %get-tuple-element.111), channel_id=1, source_target_pairs={{1,7},{3,5},{5,6},{0,3},{6,2},{4,1},{2,0},{9,15},{11,13},{13,14},{... | collective-permute-start | bytes 442376 | tf_op jit(solution)/shard_map/ppermute | solution.py:944
  222.8 14.1 %collective-permute-start.56 = (bf16[288,256]{1,0:T(8,128)(2,1)}, bf16[288,256]{1,0:T(8,128)(2,1)S(1)}, u32[]{:S(2)}, u32[]{:S(2)}) collective-permute-start(bf16[288,256]{1,0:T(8,128)(2,1)} %get-tuple-element.112), channel_id=1, source_target_pairs={{3,7},{1,4},{5,2},{2,1},{6,3},{4,6},{11,15},{9,12},{13,10},{10,9},... | collective-permute-start | bytes 442376 | tf_op jit(solution)/shard_map/ppermute | solution.py:944
  223.5 11.3 %collective-permute-start.58 = (bf16[224,256]{1,0:T(8,128)(2,1)}, bf16[224,256]{1,0:T(8,128)(2,1)S(1)}, u32[]{:S(2)}, u32[]{:S(2)}) collective-permute-start(bf16[224,256]{1,0:T(8,128)(2,1)} %get-tuple-element.114), channel_id=1, source_target_pairs={{4,5},{2,4},{6,7},{12,13},{10,12},{14,15},{20,21},{18,20},{22,23},... | collective-permute-start | bytes 344072 | tf_op jit(solution)/shard_map/ppermute | solution.py:944
  224.7 18.0 %collective-permute-start.57 = (bf16[288,256]{1,0:T(8,128)(2,1)}, bf16[288,256]{1,0:T(8,128)(2,1)S(1)}, u32[]{:S(2)}, u32[]{:S(2)}) collective-permute-start(bf16[288,256]{1,0:T(8,128)(2,1)} %get-tuple-element.113), channel_id=1, source_target_pairs={{5,7},{1,0},{3,1},{7,3},{4,2},{0,4},{2,5},{13,15},{9,8},{11,9},{15... | collective-permute-start | bytes 442376 | tf_op jit(solution)/shard_map/ppermute | solution.py:944
  234.8 22.9 %collective-permute-start.41 = (bf16[128,1024]{1,0:T(8,128)(2,1)}, bf16[128,1024]{1,0:T(8,128)(2,1)S(1)}, u32[]{:S(2)}, u32[]{:S(2)}) collective-permute-start(bf16[128,1024]{1,0:T(8,128)(2,1)} %get-tuple-element.91), channel_id=1, source_target_pairs={{0,2},{1,3},{2,4},{3,5},{4,6},{5,7},{6,0},{7,1},{8,10},{9,11},{10,... | collective-permute-start | bytes 786440 | tf_op jit(solution)/shard_map/ppermute | solution.py:159
  235.4 35.2 %collective-permute-start.42 = (bf16[128,1024]{1,0:T(8,128)(2,1)}, bf16[128,1024]{1,0:T(8,128)(2,1)S(1)}, u32[]{:S(2)}, u32[]{:S(2)}) collective-permute-start(bf16[128,1024]{1,0:T(8,128)(2,1)} %get-tuple-element.92), channel_id=1, source_target_pairs={{0,4},{1,5},{2,6},{3,7},{4,0},{5,1},{6,2},{7,3},{8,12},{9,13},{10,... | collective-permute-start | bytes 786440 | tf_op jit(solution)/shard_map/ppermute | solution.py:159
  236.9 33.6 %collective-permute-start.43 = (bf16[128,1024]{1,0:T(8,128)(2,1)}, bf16[128,1024]{1,0:T(8,128)(2,1)S(1)}, u32[]{:S(2)}, u32[]{:S(2)}) collective-permute-start(bf16[128,1024]{1,0:T(8,128)(2,1)} %get-tuple-element.93), channel_id=1, source_target_pairs={{0,6},{1,7},{2,0},{3,1},{4,2},{5,3},{6,4},{7,5},{8,14},{9,15},{10,... | collective-permute-start | bytes 786440 | tf_op jit(solution)/shard_map/ppermute | solution.py:159
  251.7 19.2 %collective-permute-start.37 = (bf16[192,1024]{1,0:T(8,128)(2,1)}, bf16[192,1024]{1,0:T(8,128)(2,1)S(1)}, u32[]{:S(2)}, u32[]{:S(2)}) collective-permute-start(bf16[192,1024]{1,0:T(8,128)(2,1)} %get-tuple-element.81), channel_id=1, source_target_pairs={{0,2},{1,3},{2,4},{3,5},{4,6},{5,7},{6,0},{7,1},{8,10},{9,11},{10,... | collective-permute-start | bytes 1179656 | tf_op jit(solution)/shard_map/ppermute | solution.py:159
  257.6 28.9 %collective-permute-start.38 = (bf16[192,1024]{1,0:T(8,128)(2,1)}, bf16[192,1024]{1,0:T(8,128)(2,1)}, u32[]{:S(2)}, u32[]{:S(2)}) collective-permute-start(bf16[192,1024]{1,0:T(8,128)(2,1)} %get-tuple-element.82), channel_id=1, source_target_pairs={{0,4},{1,5},{2,6},{3,7},{4,0},{5,1},{6,2},{7,3},{8,12},{9,13},{10,... | collective-permute-start | bytes 1179656 | tf_op jit(solution)/shard_map/ppermute | solution.py:159
  257.6 29.9 %collective-permute-start.39 = (bf16[192,1024]{1,0:T(8,128)(2,1)}, bf16[192,1024]{1,0:T(8,128)(2,1)}, u32[]{:S(2)}, u32[]{:S(2)}) collective-permute-start(bf16[192,1024]{1,0:T(8,128)(2,1)} %get-tuple-element.83), channel_id=1, source_target_pairs={{0,6},{1,7},{2,0},{3,1},{4,2},{5,3},{6,4},{7,5},{8,14},{9,15},{10,... | collective-permute-start | bytes 1179656 | tf_op jit(solution)/shard_map/ppermute | solution.py:159
  288.7 5.9 %collective-permute-start.59 = (bf16[2,128,256]{2,1,0:T(8,128)(2,1)S(1)}, bf16[2,128,256]{2,1,0:T(8,128)(2,1)S(1)}, u32[]{:S(2)}, u32[]{:S(2)}) collective-permute-start(bf16[2,128,256]{2,1,0:T(8,128)(2,1)S(1)} %get-tuple-element.115), channel_id=1, source_target_pairs={{0,8},{8,0},{16,24},{24,16},{1,9},{9,1},{17,25},{25,17},{2,10},{10... | collective-permute-start | bytes 393224 | tf_op jit(solution)/shard_map/ppermute | solution.py:169
  (63 other events, 1060.0 us)
